TPU v7x, 256 devices: a whole 4x4x8 slice. The times are simulated.
256 devices in a mesh: tm: 32 (over y, z), row: 8 (over x, core).
Axes of the slice: x: 4, y: 4, z: 8, core: 2. Of those that a mesh axis runs over, the one named last changes fastest.
Arguments:
- movie: float32 [2, 128, 1024, 1024], P(None, 'tm', 'row'), may hold values from -80 to 80, as said below
- cycle_label: int32 [1024, 1024], P(None, 'row'), may hold values from 0 to 127, as said below
- valid_mask: int32 [1024, 1024], P(None, 'row'), may hold values from 0 to 1, as said below
Outputs:
- cycle_curve: float32 [4, 128], replicated
- image_structure: float32 [4, 1024, 1024], P(None, 'tm', 'row')
Inputs may be any that keep to these rules, and one draw needn't show every extreme that they name: `movie`: field components. `cycle_label`: cycle number of each frequency pixel; both 0 and 127 occur. `valid_mask`: some cycles have no counted pixel.
All inputs are finite; a program needn't handle non-finite values.
Results may differ from a plain program's by a relative error of at most 0.00023.
Values sent between devices are 32-bit elements; how exact they have to be, the bound alone decides.
No kernel may reach another device: no remote copies, remote signals or barrier semaphores. Data moves between devices by JAX's collectives and lax.ppermute only.
A program may use at most 128 MiB of HBM per device.

v0:
```python
import functools
import math

import jax
import jax.numpy as jnp
import ml_dtypes
import numpy as np
from jax import lax
from jax.experimental import pallas as pl
from jax.experimental.pallas import tpu as pltpu
from jax.sharding import Mesh
from jax.sharding import PartitionSpec as P

N = 1024
LAGS = 4
CYCLES = 128
FRAMES = 128
RADIX = 4
SUB = N // RADIX
OWN = 4
CHUNKS = ((0,), (1,), (2,), (3,))
ROW = ("row_0", "row_1")
TM = ("tm_0", "tm_1")

highest = lax.Precision.HIGHEST
f32 = jnp.float32
bf16 = jnp.bfloat16


def dft_tables():
    freq = 4 * np.arange(SUB)[None, :, None] + np.arange(RADIX)[:, None, None]
    phase = (freq * np.arange(SUB)[None, None, :]) % N
    angle = phase * (2.0 * math.pi / N)
    table = np.concatenate([np.cos(angle), np.sin(angle)], axis=2) / 32.0
    high = table.astype(ml_dtypes.bfloat16)
    low = (table - high.astype(np.float64)).astype(ml_dtypes.bfloat16)
    return high, low


def butterfly(parts_re, parts_im, p):
    (a, b, c, d), (e, f, g, h) = parts_re, parts_im
    if p == 0:
        return (a + c) + (b + d), (e + g) + (f + h)
    if p == 2:
        return (a + c) - (b + d), (e + g) - (f + h)
    if p == 1:
        return (a - c) + (f - h), (e - g) - (b - d)
    return (a - c) - (f - h), (e - g) + (b - d)


def split(z):
    high = z.astype(bf16)
    return high, (z - high.astype(f32)).astype(bf16)


def stacked(zr, zi):
    return jnp.concatenate(
        [jnp.concatenate([zr, zi], axis=1), jnp.concatenate([zi, -zr], axis=1)], axis=0
    )


def nt(a, b):
    return lax.dot_general(a, b, (((1,), (1,)), ((), ())), preferred_element_type=f32)


def first_kernel(residues, movie_ref, high_ref, low_ref, out_ref):
    parts = [[movie_ref[c, 0, :, q * SUB:(q + 1) * SUB] for q in range(RADIX)] for c in range(2)]
    for j, p in enumerate(residues):
        zr, zi = butterfly(parts[0], parts[1], p)
        zh, zl = split(stacked(zr, zi))
        th, tl = high_ref[j], low_ref[j]
        got = nt(th, zh) + nt(tl, zh) + nt(th, zl)
        rows = got.shape[1] // 2
        for c in range(2):
            piece = got[:, c * rows:(c + 1) * rows]
            out_ref[:, c, j] = piece.reshape(out_ref.shape[0], 32, rows)


def first_transform(movie, high, low, index, residues):
    count = len(residues)
    return pl.pallas_call(
        functools.partial(first_kernel, residues),
        grid=(OWN,),
        in_specs=[
            pl.BlockSpec((2, 1, 128, N), lambda f: (0, f, 0, 0)),
            pl.BlockSpec((count, SUB, 2 * SUB), lambda f: (index, 0, 0)),
            pl.BlockSpec((count, SUB, 2 * SUB), lambda f: (index, 0, 0)),
        ],
        out_specs=pl.BlockSpec((8, 2, count, 32, 128), lambda f: (0, 0, 0, 0, f)),
        out_shape=jax.ShapeDtypeStruct((8, 2, count, 32, OWN * 128), f32),
        compiler_params=pltpu.CompilerParams(vmem_limit_bytes=24 << 20),
        cost_estimate=pl.CostEstimate(
            flops=count * 6 * 256 * 512 * 1024, bytes_accessed=(4 + count) << 20, transcendentals=0
        ),
        name="first_transform",
    )(movie, high, low)


def second_kernel(count, piece_ref, high_ref, low_ref, early_ref, late_ref):
    for j in range(count):

        def part(c, q):
            halves = []
            for h in range(2):
                s = 2 * q + h
                halves.append(
                    jnp.concatenate(
                        [piece_ref[s, c, j, :, f * 128:(f + 1) * 128] for f in range(OWN)], axis=0
                    )
                )
            return jnp.concatenate(halves, axis=1)

        parts = [[part(c, q) for q in range(RADIX)] for c in range(2)]
        for p in range(RADIX):
            zr, zi = butterfly(parts[0], parts[1], p)
            zh, zl = split(stacked(zr, zi))
            th, tl = high_ref[p], low_ref[p]
            got = nt(zh, th) + nt(zh, tl) + nt(zl, th)
            for c in range(2):
                for f in range(OWN):
                    ref = early_ref if f < 2 else late_ref
                    ref[f % 2, c, j, :, p * SUB:(p + 1) * SUB] = got[
                        (c * OWN + f) * 32:(c * OWN + f + 1) * 32
                    ]


def second_transform(piece, high, low, count):
    half = jax.ShapeDtypeStruct((2, 2, count, 32, N), f32)
    return pl.pallas_call(
        functools.partial(second_kernel, count),
        out_shape=(half, half),
        compiler_params=pltpu.CompilerParams(vmem_limit_bytes=40 << 20),
        cost_estimate=pl.CostEstimate(
            flops=count * 6 * 256 * 512 * 1024, bytes_accessed=(2 + 2 * count) << 20, transcendentals=0
        ),
        name="second_transform",
    )(piece, high, low)


def lag_kernel(count, ends_ref, early_ref, late_ref, right_ref, left_ref, out_ref):
    has_right, has_left = ends_ref[0], ends_ref[1]
    for j in range(count):
        for b in range(8):
            lanes = slice(b * 128, (b + 1) * 128)
            frames = {}
            for f in range(2):
                frames[f] = [early_ref[f, c, j, :, lanes] for c in range(2)]
                frames[2 + f] = [late_ref[f, c, j, :, lanes] for c in range(2)]
                frames[4 + f] = [right_ref[f, c, j, :, lanes] for c in range(2)]
                frames[f - 2] = [left_ref[f, c, j, :, lanes] for c in range(2)]

            def pair(s, t):
                dr = frames[t][0] - frames[s][0]
                di = frames[t][1] - frames[s][1]
                return dr * dr + di * di

            def total(pairs):
                return functools.reduce(lambda x, y: x + y, [pair(s, t) for s, t in pairs])

            lag_rows = []
            for lag in range(1, LAGS + 1):
                own = [(s, s + lag) for s in range(OWN) if s + lag < OWN]
                right = [(s, s + lag) for s in range(OWN) if 4 <= s + lag < 6]
                left = [(s, s + lag) for s in (-2, -1) if s + lag in (2, 3)]
                terms = []
                if own:
                    terms.append(total(own))
                terms.append(has_right * total(right))
                if left:
                    terms.append(has_left * total(left))
                whole = functools.reduce(lambda x, y: x + y, terms)
                lag_rows.append(whole * (1.0 / float(FRAMES - lag)))
            block = jnp.concatenate(lag_rows, axis=0).T
            p, h = b // 2, b % 2
            out_ref[2 * h:2 * h + 2, :, j, p] = block.reshape(2, 8, 8, 128)


def partial_lags(ends, early, late, right, left, count):
    vmem = pl.BlockSpec(memory_space=pltpu.VMEM)
    return pl.pallas_call(
        functools.partial(lag_kernel, count),
        in_specs=[pl.BlockSpec(memory_space=pltpu.SMEM)] + [vmem] * 4,
        out_specs=vmem,
        out_shape=jax.ShapeDtypeStruct((4, 8, count, RADIX, 8, 128), f32),
        compiler_params=pltpu.CompilerParams(vmem_limit_bytes=24 << 20),
        cost_estimate=pl.CostEstimate(
            flops=count * 100 * 32 * 1024, bytes_accessed=count * 5 << 19, transcendentals=0
        ),
        name="partial_lags",
    )(ends, early, late, right, left)


def cycle_table(labels, mask_block, cycle_count):
    cycle_ids = jnp.arange(cycle_count, dtype=jnp.int32)
    chosen = (labels.reshape(-1)[:, None] == cycle_ids[None, :]) & (
        mask_block.reshape(-1)[:, None] == 1
    )
    return chosen.astype(f32)


def sum_everywhere(value):
    for axes in (ROW, TM):
        size = lax.axis_size(axes)
        copies = jnp.broadcast_to(value[None], (size,) + value.shape)
        value = jnp.sum(lax.all_to_all(copies, axes, 0, 0, tiled=True), axis=0)
    return value


def body(movie, cycle_label, valid_mask):
    high, low = dft_tables()
    high, low = jnp.asarray(high), jnp.asarray(low)
    time_count = lax.axis_size(TM)
    time_place = lax.axis_index(TM)
    slab_rows = N // time_count
    slab_labels = lax.dynamic_slice_in_dim(cycle_label, time_place * slab_rows, slab_rows, 0)
    slab_mask = lax.dynamic_slice_in_dim(valid_mask, time_place * slab_rows, slab_rows, 0)
    slab_table = cycle_table(slab_labels, slab_mask, CYCLES)
    counts = jnp.sum(slab_table, axis=0)
    ends = jnp.stack([time_place < time_count - 1, time_place > 0]).astype(f32)
    to_left = [(i + 1, i) for i in range(time_count - 1)]
    to_right = [(i, i + 1) for i in range(time_count - 1)]
    slabs = []
    for index, residues in enumerate(CHUNKS):
        count = len(residues)
        piece = first_transform(movie, high, low, index, residues)
        piece = lax.all_to_all(piece, ROW, 0, 0, tiled=True)
        early, late = second_transform(piece, high, low, count)
        right = lax.ppermute(early, TM, to_left)
        left = lax.ppermute(late, TM, to_right)
        part = partial_lags(ends, early, late, right, left, count)
        part = jnp.sum(lax.all_to_all(part, "tm_0", 0, 0, tiled=True), axis=0)
        part = jnp.sum(lax.all_to_all(part, "tm_1", 0, 0, tiled=True), axis=0)
        slabs.append(part)
    slab = jnp.concatenate(slabs, axis=0).reshape(RADIX, RADIX, 8, LAGS, 32)
    image_structure = jnp.transpose(slab, (3, 2, 1, 4, 0)).reshape(LAGS, slab_rows, 128)
    cycle_part = jnp.dot(
        image_structure.reshape(LAGS, -1), slab_table, precision=highest, preferred_element_type=f32
    )
    sums = sum_everywhere(jnp.concatenate([cycle_part, counts[None, :]], axis=0))
    cycle_curve = sums[:LAGS] / jnp.maximum(sums[LAGS], 1.0)[None, :]
    return (cycle_curve, image_structure)


def solution(mesh):
    torus = Mesh(mesh.devices.reshape(4, 8, 4, 2), ("tm_0", "tm_1", "row_0", "row_1"))
    placed = (P(None, TM, ROW, None), P(None, ROW), P(None, ROW))
    return jax.shard_map(
        body, mesh=torus, in_specs=placed, out_specs=(P(), P(None, TM, ROW)), check_vma=False
    )
```

profile of v0, /device:TPU:1, one launch (start us, length us, event | category | flops | bytes accessed | tf_op | source)
XLA Modules:
  0.0 250.1 jit_solution(12752937641336653892)
XLA Ops:
  0.7 1.3 copy-done.1
  1.9 1.2 copy-done.3
  3.2 2.2 copy-done.5
  5.3 2.1 first_transform.4
  7.5 1.0 copy-done.12
  8.4 7.5 %all-to-all-start = ((f32[8,2,1,32,512]{4,3,2,1,0:T(8,128)}), f32[8,2,1,32,512]{4,3,2,1,0:T(8,128)}, u32[]{:S(2)}, u32[]{:S(2)}) async-start(f32[8,2,1,32,512]{4,3,2,1,0:T(8,128)} %copy-done.12), calls=%async_computation | async-start | bytes 2097152 | tf_op jit(solution)/shard_map/all_to_all | solution.py:226
  16.0 2.2 copy-done.6
  18.2 2.1 first_transform.5
  20.3 1.0 copy-done.10
  21.3 9.9 %all-to-all-done.piece_ref = f32[8,2,1,32,512]{4,3,2,1,0:T(8,128)} async-done(((f32[8,2,1,32,512]{4,3,2,1,0:T(8,128)}), f32[8,2,1,32,512]{4,3,2,1,0:T(8,128)}, u32[]{:S(2)}, u32[]{:S(2)}) %all-to-all-start) | async-done | bytes 1048608 | tf_op jit(solution)/shard_map/all_to_all | solution.py:226
  31.2 5.0 %all-to-all-start.3 = ((f32[8,2,1,32,512]{4,3,2,1,0:T(8,128)}), f32[8,2,1,32,512]{4,3,2,1,0:T(8,128)}, u32[]{:S(2)}, u32[]{:S(2)}) async-start(f32[8,2,1,32,512]{4,3,2,1,0:T(8,128)} %copy-done.10), calls=%async_computation.3 | async-start | bytes 2097152 | tf_op jit(solution)/shard_map/all_to_all | solution.py:226
  36.2 2.2 copy-done.7
  38.4 2.1 first_transform.6
  40.5 1.0 copy-done.11
  41.5 9.9 %all-to-all-done.3.piece_ref = f32[8,2,1,32,512]{4,3,2,1,0:T(8,128)} async-done(((f32[8,2,1,32,512]{4,3,2,1,0:T(8,128)}), f32[8,2,1,32,512]{4,3,2,1,0:T(8,128)}, u32[]{:S(2)}, u32[]{:S(2)}) %all-to-all-start.3) | async-done | bytes 1048608 | tf_op jit(solution)/shard_map/all_to_all | solution.py:226
  51.4 5.0 %all-to-all-start.6 = ((f32[8,2,1,32,512]{4,3,2,1,0:T(8,128)}), f32[8,2,1,32,512]{4,3,2,1,0:T(8,128)}, u32[]{:S(2)}, u32[]{:S(2)}) async-start(f32[8,2,1,32,512]{4,3,2,1,0:T(8,128)} %copy-done.11), calls=%async_computation.6 | async-start | bytes 2097152 | tf_op jit(solution)/shard_map/all_to_all | solution.py:226
  56.4 2.2 copy-done.8
  58.6 2.1 first_transform.7
  60.7 1.0 copy-done.9
  61.7 9.9 %all-to-all-done.6.piece_ref = f32[8,2,1,32,512]{4,3,2,1,0:T(8,128)} async-done(((f32[8,2,1,32,512]{4,3,2,1,0:T(8,128)}), f32[8,2,1,32,512]{4,3,2,1,0:T(8,128)}, u32[]{:S(2)}, u32[]{:S(2)}) %all-to-all-start.6) | async-done | bytes 1048608 | tf_op jit(solution)/shard_map/all_to_all | solution.py:226
  71.6 5.0 %all-to-all-start.9 = ((f32[8,2,1,32,512]{4,3,2,1,0:T(8,128)}), f32[8,2,1,32,512]{4,3,2,1,0:T(8,128)}, u32[]{:S(2)}, u32[]{:S(2)}) async-start(f32[8,2,1,32,512]{4,3,2,1,0:T(8,128)} %copy-done.9), calls=%async_computation.9 | async-start | bytes 2097152 | tf_op jit(solution)/shard_map/all_to_all | solution.py:226
  76.6 3.3 %second_transform.4 = (f32[2,2,1,32,1024]{4,3,2,1,0:T(8,128)}, f32[2,2,1,32,1024]{4,3,2,1,0:T(8,128)}) custom-call(f32[8,2,1,32,512]{4,3,2,1,0:T(8,128)} %all-to-all-done.piece_ref, bf16[4,256,512]{2,1,0:T(8,128)(2,1)S(1)} %copy-done.2, bf16[4,256,512]{2,1,0:T(8,128)(2,1)S(1)} %copy-done.4), custom_call_target="tpu_custom_call" | custom-call | flops 805306368 | bytes 4194304 | tf_op jit(solution)/shard_map/second_transform/pallas_call | solution.py:129
  79.9 1.3 collective-permute-start
  81.2 4.8 %collective-permute-start.1 = (f32[2,2,1,32,1024]{4,3,2,1,0:T(8,128)}, f32[2,2,1,32,1024]{4,3,2,1,0:T(8,128)}, u32[]{:S(2)}, u32[]{:S(2)}) collective-permute-start(f32[2,2,1,32,1024]{4,3,2,1,0:T(8,128)} %get-tuple-element.11.late_ref), channel_id=1, source_target_pairs={{0,8},{8,16},{16,24},{24,32},{32,40},{40,48},{48,56},{56,64},{64,7... | collective-permute-start | bytes 1572872 | tf_op jit(solution)/shard_map/ppermute | solution.py:229
  86.0 3.1 %second_transform.5 = (f32[2,2,1,32,1024]{4,3,2,1,0:T(8,128)S(1)}, f32[2,2,1,32,1024]{4,3,2,1,0:T(8,128)}) custom-call(f32[8,2,1,32,512]{4,3,2,1,0:T(8,128)} %all-to-all-done.3.piece_ref, bf16[4,256,512]{2,1,0:T(8,128)(2,1)S(1)} %copy-done.2, bf16[4,256,512]{2,1,0:T(8,128)(2,1)S(1)} %copy-done.4), custom_call_target="tpu_custom_call" | custom-call | flops 805306368 | bytes 4194304 | tf_op jit(solution)/shard_map/second_transform/pallas_call | solution.py:129
  89.0 1.3 collective-permute-start.2
  90.3 4.8 %collective-permute-start.3 = (f32[2,2,1,32,1024]{4,3,2,1,0:T(8,128)}, f32[2,2,1,32,1024]{4,3,2,1,0:T(8,128)}, u32[]{:S(2)}, u32[]{:S(2)}) collective-permute-start(f32[2,2,1,32,1024]{4,3,2,1,0:T(8,128)} %get-tuple-element.13.late_ref), channel_id=1, source_target_pairs={{0,8},{8,16},{16,24},{24,32},{32,40},{40,48},{48,56},{56,64},{64,7... | collective-permute-start | bytes 1572872 | tf_op jit(solution)/shard_map/ppermute | solution.py:229
  95.5 0.9 collective-permute-done.1.left_ref
  96.3 2.9 %partial_lags.4 = f32[4,8,1,4,8,128]{5,4,3,2,1,0:T(8,128)} custom-call(f32[2]{0:T(128)S(1)} %add_convert_fusion.ends_ref, f32[2,2,1,32,1024]{4,3,2,1,0:T(8,128)} %get-tuple-element.10.early_ref, f32[2,2,1,32,1024]{4,3,2,1,0:T(8,128)} %get-tuple-element.11.late_ref, f32[2,2,1,32,1024]{4,3,2,1,0:T(8,128)} %collective-permute-done.right_ref, ...), custom_call_target="tpu_custom_call" | custom-call | flops 3276800 | bytes 2621440 | tf_op jit(solution)/shard_map/partial_lags/pallas_call | solution.py:180
  99.2 11.0 %all-to-all-start.1 = ((f32[4,8,1,4,8,128]{5,4,3,2,1,0:T(8,128)}), f32[4,8,1,4,8,128]{5,4,3,2,1,0:T(8,128)}, u32[]{:S(2)}, u32[]{:S(2)}) async-start(f32[4,8,1,4,8,128]{5,4,3,2,1,0:T(8,128)} %partial_lags.4), calls=%async_computation.1 | async-start | bytes 1048576 | tf_op jit(solution)/shard_map/all_to_all | solution.py:231
  110.2 3.3 %second_transform.6 = (f32[2,2,1,32,1024]{4,3,2,1,0:T(8,128)}, f32[2,2,1,32,1024]{4,3,2,1,0:T(8,128)}) custom-call(f32[8,2,1,32,512]{4,3,2,1,0:T(8,128)} %all-to-all-done.6.piece_ref, bf16[4,256,512]{2,1,0:T(8,128)(2,1)S(1)} %copy-done.2, bf16[4,256,512]{2,1,0:T(8,128)(2,1)S(1)} %copy-done.4), custom_call_target="tpu_custom_call" | custom-call | flops 805306368 | bytes 4194304 | tf_op jit(solution)/shard_map/second_transform/pallas_call | solution.py:129
  113.5 1.3 collective-permute-start.4
  114.8 4.8 %collective-permute-start.5 = (f32[2,2,1,32,1024]{4,3,2,1,0:T(8,128)}, f32[2,2,1,32,1024]{4,3,2,1,0:T(8,128)}, u32[]{:S(2)}, u32[]{:S(2)}) collective-permute-start(f32[2,2,1,32,1024]{4,3,2,1,0:T(8,128)} %get-tuple-element.15.late_ref), channel_id=1, source_target_pairs={{0,8},{8,16},{16,24},{24,32},{32,40},{40,48},{48,56},{56,64},{64,7... | collective-permute-start | bytes 1572872 | tf_op jit(solution)/shard_map/ppermute | solution.py:229
  119.6 2.7 %partial_lags.5 = f32[4,8,1,4,8,128]{5,4,3,2,1,0:T(8,128)} custom-call(f32[2]{0:T(128)S(1)} %add_convert_fusion.ends_ref, f32[2,2,1,32,1024]{4,3,2,1,0:T(8,128)S(1)} %get-tuple-element.12.early_ref, f32[2,2,1,32,1024]{4,3,2,1,0:T(8,128)} %get-tuple-element.13.late_ref, f32[2,2,1,32,1024]{4,3,2,1,0:T(8,128)} %collective-permute-done.2.right_ref, ...), custom_call_target="tpu_custom_call" | custom-call | flops 3276800 | bytes 2621440 | tf_op jit(solution)/shard_map/partial_lags/pallas_call | solution.py:180
  122.3 1.2 all-to-all-done.1
  123.4 4.2 %all-to-all-start.4 = ((f32[4,8,1,4,8,128]{5,4,3,2,1,0:T(8,128)}), f32[4,8,1,4,8,128]{5,4,3,2,1,0:T(8,128)}, u32[]{:S(2)}, u32[]{:S(2)}) async-start(f32[4,8,1,4,8,128]{5,4,3,2,1,0:T(8,128)} %partial_lags.5), calls=%async_computation.4 | async-start | bytes 1048576 | tf_op jit(solution)/shard_map/all_to_all | solution.py:231
  127.6 3.1 %second_transform.7 = (f32[2,2,1,32,1024]{4,3,2,1,0:T(8,128)S(1)}, f32[2,2,1,32,1024]{4,3,2,1,0:T(8,128)}) custom-call(f32[8,2,1,32,512]{4,3,2,1,0:T(8,128)} %all-to-all-done.9.piece_ref, bf16[4,256,512]{2,1,0:T(8,128)(2,1)S(1)} %copy-done.2, bf16[4,256,512]{2,1,0:T(8,128)(2,1)S(1)} %copy-done.4), custom_call_target="tpu_custom_call" | custom-call | flops 805306368 | bytes 4194304 | tf_op jit(solution)/shard_map/second_transform/pallas_call | solution.py:129
  130.6 1.3 collective-permute-start.6
  131.9 4.0 %collective-permute-start.7 = (f32[2,2,1,32,1024]{4,3,2,1,0:T(8,128)}, f32[2,2,1,32,1024]{4,3,2,1,0:T(8,128)S(1)}, u32[]{:S(2)}, u32[]{:S(2)}) collective-permute-start(f32[2,2,1,32,1024]{4,3,2,1,0:T(8,128)} %get-tuple-element.17.late_ref), channel_id=1, source_target_pairs={{0,8},{8,16},{16,24},{24,32},{32,40},{40,48},{48,56},{56,64},{64,7... | collective-permute-start | bytes 1572872 | tf_op jit(solution)/shard_map/ppermute | solution.py:229
  136.0 2.9 %partial_lags.6 = f32[4,8,1,4,8,128]{5,4,3,2,1,0:T(8,128)} custom-call(f32[2]{0:T(128)S(1)} %add_convert_fusion.ends_ref, f32[2,2,1,32,1024]{4,3,2,1,0:T(8,128)} %get-tuple-element.14.early_ref, f32[2,2,1,32,1024]{4,3,2,1,0:T(8,128)} %get-tuple-element.15.late_ref, f32[2,2,1,32,1024]{4,3,2,1,0:T(8,128)} %collective-permute-done.4.right_ref, ...), custom_call_target="tpu_custom_call" | custom-call | flops 3276800 | bytes 2621440 | tf_op jit(solution)/shard_map/partial_lags/pallas_call | solution.py:180
  138.8 2.9 %all-to-all-done.4 = f32[4,8,1,4,8,128]{5,4,3,2,1,0:T(8,128)} async-done(((f32[4,8,1,4,8,128]{5,4,3,2,1,0:T(8,128)}), f32[4,8,1,4,8,128]{5,4,3,2,1,0:T(8,128)}, u32[]{:S(2)}, u32[]{:S(2)}) %all-to-all-start.4) | async-done | bytes 524320 | tf_op jit(solution)/shard_map/all_to_all | solution.py:231
  141.8 3.5 %all-to-all-start.7 = ((f32[4,8,1,4,8,128]{5,4,3,2,1,0:T(8,128)}), f32[4,8,1,4,8,128]{5,4,3,2,1,0:T(8,128)S(1)}, u32[]{:S(2)}, u32[]{:S(2)}) async-start(f32[4,8,1,4,8,128]{5,4,3,2,1,0:T(8,128)} %partial_lags.6), calls=%async_computation.7 | async-start | bytes 1048576 | tf_op jit(solution)/shard_map/all_to_all | solution.py:231
  145.5 2.4 partial_lags.7
  147.9 11.5 %all-to-all-done.7 = f32[4,8,1,4,8,128]{5,4,3,2,1,0:T(8,128)S(1)} async-done(((f32[4,8,1,4,8,128]{5,4,3,2,1,0:T(8,128)}), f32[4,8,1,4,8,128]{5,4,3,2,1,0:T(8,128)S(1)}, u32[]{:S(2)}, u32[]{:S(2)}) %all-to-all-start.7) | async-done | bytes 524320 | tf_op jit(solution)/shard_map/all_to_all | solution.py:231
  159.3 3.5 %all-to-all-start.10 = ((f32[4,8,1,4,8,128]{5,4,3,2,1,0:T(8,128)}), f32[4,8,1,4,8,128]{5,4,3,2,1,0:T(8,128)S(1)}, u32[]{:S(2)}, u32[]{:S(2)}) async-start(f32[4,8,1,4,8,128]{5,4,3,2,1,0:T(8,128)} %partial_lags.7), calls=%async_computation.10 | async-start | bytes 1048576 | tf_op jit(solution)/shard_map/all_to_all | solution.py:231
  162.8 1.8 reduce_sum.107
  164.6 7.3 %all-to-all-done.10 = f32[4,8,1,4,8,128]{5,4,3,2,1,0:T(8,128)S(1)} async-done(((f32[4,8,1,4,8,128]{5,4,3,2,1,0:T(8,128)}), f32[4,8,1,4,8,128]{5,4,3,2,1,0:T(8,128)S(1)}, u32[]{:S(2)}, u32[]{:S(2)}) %all-to-all-start.10) | async-done | bytes 524320 | tf_op jit(solution)/shard_map/all_to_all | solution.py:231
  171.9 3.4 %all-to-all-start.2 = ((f32[8,1,4,8,128]{4,3,2,1,0:T(8,128)}), f32[8,1,4,8,128]{4,3,2,1,0:T(8,128)S(1)}, u32[]{:S(2)}, u32[]{:S(2)}) async-start(f32[8,1,4,8,128]{4,3,2,1,0:T(8,128)} %bitcast.2), calls=%async_computation.2 | async-start | bytes 262144 | tf_op jit(solution)/shard_map/all_to_all | solution.py:232
  175.2 1.7 reduce_sum.110
  177.0 6.2 %all-to-all-done.2 = f32[8,1,4,8,128]{4,3,2,1,0:T(8,128)S(1)} async-done(((f32[8,1,4,8,128]{4,3,2,1,0:T(8,128)}), f32[8,1,4,8,128]{4,3,2,1,0:T(8,128)S(1)}, u32[]{:S(2)}, u32[]{:S(2)}) %all-to-all-start.2) | async-done | bytes 131104 | tf_op jit(solution)/shard_map/all_to_all | solution.py:232
  183.2 3.4 %all-to-all-start.5 = ((f32[8,1,4,8,128]{4,3,2,1,0:T(8,128)}), f32[8,1,4,8,128]{4,3,2,1,0:T(8,128)S(1)}, u32[]{:S(2)}, u32[]{:S(2)}) async-start(f32[8,1,4,8,128]{4,3,2,1,0:T(8,128)} %bitcast.3), calls=%async_computation.5 | async-start | bytes 262144 | tf_op jit(solution)/shard_map/all_to_all | solution.py:232
  187.3 7.2 %all-to-all-done.5 = f32[8,1,4,8,128]{4,3,2,1,0:T(8,128)S(1)} async-done(((f32[8,1,4,8,128]{4,3,2,1,0:T(8,128)}), f32[8,1,4,8,128]{4,3,2,1,0:T(8,128)S(1)}, u32[]{:S(2)}, u32[]{:S(2)}) %all-to-all-start.5) | async-done | bytes 131104 | tf_op jit(solution)/shard_map/all_to_all | solution.py:232
  194.5 3.4 %all-to-all-start.8 = ((f32[8,1,4,8,128]{4,3,2,1,0:T(8,128)}), f32[8,1,4,8,128]{4,3,2,1,0:T(8,128)S(1)}, u32[]{:S(2)}, u32[]{:S(2)}) async-start(f32[8,1,4,8,128]{4,3,2,1,0:T(8,128)} %bitcast.4), calls=%async_computation.8 | async-start | bytes 262144 | tf_op jit(solution)/shard_map/all_to_all | solution.py:232
  198.6 7.1 %all-to-all-done.8 = f32[8,1,4,8,128]{4,3,2,1,0:T(8,128)S(1)} async-done(((f32[8,1,4,8,128]{4,3,2,1,0:T(8,128)}), f32[8,1,4,8,128]{4,3,2,1,0:T(8,128)S(1)}, u32[]{:S(2)}, u32[]{:S(2)}) %all-to-all-start.8) | async-done | bytes 131104 | tf_op jit(solution)/shard_map/all_to_all | solution.py:232
  205.7 3.6 %all-to-all-start.11 = ((f32[8,1,4,8,128]{4,3,2,1,0:T(8,128)}), f32[8,1,4,8,128]{4,3,2,1,0:T(8,128)S(1)}, u32[]{:S(2)}, u32[]{:S(2)}) async-start(f32[8,1,4,8,128]{4,3,2,1,0:T(8,128)} %bitcast.5), calls=%async_computation.11 | async-start | bytes 262144 | tf_op jit(solution)/shard_map/all_to_all | solution.py:232
  210.0 1.4 convert_reduce_fusion
  211.8 5.2 %all-to-all-done.11 = f32[8,1,4,8,128]{4,3,2,1,0:T(8,128)S(1)} async-done(((f32[8,1,4,8,128]{4,3,2,1,0:T(8,128)}), f32[8,1,4,8,128]{4,3,2,1,0:T(8,128)S(1)}, u32[]{:S(2)}, u32[]{:S(2)}) %all-to-all-start.11) | async-done | bytes 131104 | tf_op jit(solution)/shard_map/all_to_all | solution.py:232
  217.1 0.8 copy.13
  218.0 1.7 reshape_reshape.3
  219.7 1.5 fusion.1
  221.2 14.5 %all_to_all.70 = f32[8,5,128]{2,1,0:T(8,128)S(1)} all-to-all(f32[8,5,128]{2,1,0:T(8,128)S(1)} %broadcast_in_dim.7), channel_id=1, replica_groups=mesh['tm_0'=4,'tm_1'=8,'row_0'=4,'row_1'=2] {'row_0','row_1'}, dimensions={0} | all-to-all | bytes 40960 | tf_op jit(solution)/shard_map/all_to_all | solution.py:205
  236.4 3.9 %all-to-all-start.13 = ((f32[32,5,128]{2,1,0:T(8,128)}), f32[32,5,128]{2,1,0:T(8,128)S(1)}, u32[]{:S(2)}, u32[]{:S(2)}) async-start(f32[32,5,128]{2,1,0:T(8,128)} %broadcast_in_dim.8), calls=%async_computation.13 | async-start | bytes 262144 | tf_op jit(solution)/shard_map/all_to_all | solution.py:205
  240.3 2.3 reshape.36
  242.5 6.9 %all-to-all-done.13 = f32[32,5,128]{2,1,0:T(8,128)S(1)} async-done(((f32[32,5,128]{2,1,0:T(8,128)}), f32[32,5,128]{2,1,0:T(8,128)S(1)}, u32[]{:S(2)}, u32[]{:S(2)}) %all-to-all-start.13) | async-done | bytes 81952 | tf_op jit(solution)/shard_map/all_to_all | solution.py:205
  (45 shorter events, 4.6 us)
Async XLA Ops:
  0.6 197.2 %copy-start = (s32[1024,128]{1,0:T(8,128)S(1)}, s32[1024,128]{1,0:T(8,128)}, u32[]{:S(2)}) copy-start(s32[1024,128]{1,0:T(8,128)} %param.6) | copy-start | bytes 1572868
  0.6 1.3 copy-start.1
  1.9 1.2 copy-start.3
  3.2 2.2 copy-start.5
  7.5 1.0 copy-start.12
  8.4 7.5 %copy-start.2 = (bf16[4,256,512]{2,1,0:T(8,128)(2,1)S(1)}, bf16[4,256,512]{2,1,0:T(8,128)(2,1)}, u32[]{:S(2)}) copy-start(bf16[4,256,512]{2,1,0:T(8,128)(2,1)} %constant.30.clone.high_ref) | copy-start | bytes 3145732
  8.4 7.5 %copy-start.4 = (bf16[4,256,512]{2,1,0:T(8,128)(2,1)S(1)}, bf16[4,256,512]{2,1,0:T(8,128)(2,1)}, u32[]{:S(2)}) copy-start(bf16[4,256,512]{2,1,0:T(8,128)(2,1)} %constant.31.clone.low_ref) | copy-start | bytes 3145732
  8.4 22.7 %all-to-all-start = ((f32[8,2,1,32,512]{4,3,2,1,0:T(8,128)}), f32[8,2,1,32,512]{4,3,2,1,0:T(8,128)}, u32[]{:S(2)}, u32[]{:S(2)}) async-start(f32[8,2,1,32,512]{4,3,2,1,0:T(8,128)} %copy-done.12), calls=%async_computation | async-start | bytes 2097152 | tf_op jit(solution)/shard_map/all_to_all | solution.py:226
  16.0 2.2 copy-start.6
  20.3 1.0 copy-start.10
  31.2 20.2 %all-to-all-start.3 = ((f32[8,2,1,32,512]{4,3,2,1,0:T(8,128)}), f32[8,2,1,32,512]{4,3,2,1,0:T(8,128)}, u32[]{:S(2)}, u32[]{:S(2)}) async-start(f32[8,2,1,32,512]{4,3,2,1,0:T(8,128)} %copy-done.10), calls=%async_computation.3 | async-start | bytes 2097152 | tf_op jit(solution)/shard_map/all_to_all | solution.py:226
  36.2 2.2 copy-start.7
  40.5 1.0 copy-start.11
  51.4 20.2 %all-to-all-start.6 = ((f32[8,2,1,32,512]{4,3,2,1,0:T(8,128)}), f32[8,2,1,32,512]{4,3,2,1,0:T(8,128)}, u32[]{:S(2)}, u32[]{:S(2)}) async-start(f32[8,2,1,32,512]{4,3,2,1,0:T(8,128)} %copy-done.11), calls=%async_computation.6 | async-start | bytes 2097152 | tf_op jit(solution)/shard_map/all_to_all | solution.py:226
  56.4 2.2 copy-start.8
  60.7 1.0 copy-start.9
  71.6 27.6 %all-to-all-start.9 = ((f32[8,2,1,32,512]{4,3,2,1,0:T(8,128)}), f32[8,2,1,32,512]{4,3,2,1,0:T(8,128)}, u32[]{:S(2)}, u32[]{:S(2)}) async-start(f32[8,2,1,32,512]{4,3,2,1,0:T(8,128)} %copy-done.9), calls=%async_computation.9 | async-start | bytes 2097152 | tf_op jit(solution)/shard_map/all_to_all | solution.py:226
  79.9 15.6 %collective-permute-start = (f32[2,2,1,32,1024]{4,3,2,1,0:T(8,128)}, f32[2,2,1,32,1024]{4,3,2,1,0:T(8,128)}, u32[]{:S(2)}, u32[]{:S(2)}) collective-permute-start(f32[2,2,1,32,1024]{4,3,2,1,0:T(8,128)} %get-tuple-element.10.early_ref), channel_id=1, source_target_pairs={{8,0},{16,8},{24,16},{32,24},{40,32},{48,40},{56,48},{64,56},{72,6... | collective-permute-start | bytes 1572872 | tf_op jit(solution)/shard_map/ppermute | solution.py:228
  81.2 15.2 %collective-permute-start.1 = (f32[2,2,1,32,1024]{4,3,2,1,0:T(8,128)}, f32[2,2,1,32,1024]{4,3,2,1,0:T(8,128)}, u32[]{:S(2)}, u32[]{:S(2)}) collective-permute-start(f32[2,2,1,32,1024]{4,3,2,1,0:T(8,128)} %get-tuple-element.11.late_ref), channel_id=1, source_target_pairs={{0,8},{8,16},{16,24},{24,32},{32,40},{40,48},{48,56},{56,64},{64,7... | collective-permute-start | bytes 1572872 | tf_op jit(solution)/shard_map/ppermute | solution.py:229
  89.0 30.5 %collective-permute-start.2 = (f32[2,2,1,32,1024]{4,3,2,1,0:T(8,128)S(1)}, f32[2,2,1,32,1024]{4,3,2,1,0:T(8,128)}, u32[]{:S(2)}, u32[]{:S(2)}) collective-permute-start(f32[2,2,1,32,1024]{4,3,2,1,0:T(8,128)S(1)} %get-tuple-element.12.early_ref), channel_id=1, source_target_pairs={{8,0},{16,8},{24,16},{32,24},{40,32},{48,40},{56,48},{64,56},{72,6... | collective-permute-start | bytes 1572872 | tf_op jit(solution)/shard_map/ppermute | solution.py:228
  90.3 29.3 %collective-permute-start.3 = (f32[2,2,1,32,1024]{4,3,2,1,0:T(8,128)}, f32[2,2,1,32,1024]{4,3,2,1,0:T(8,128)}, u32[]{:S(2)}, u32[]{:S(2)}) collective-permute-start(f32[2,2,1,32,1024]{4,3,2,1,0:T(8,128)} %get-tuple-element.13.late_ref), channel_id=1, source_target_pairs={{0,8},{8,16},{16,24},{24,32},{32,40},{40,48},{48,56},{56,64},{64,7... | collective-permute-start | bytes 1572872 | tf_op jit(solution)/shard_map/ppermute | solution.py:229
  99.2 24.2 %all-to-all-start.1 = ((f32[4,8,1,4,8,128]{5,4,3,2,1,0:T(8,128)}), f32[4,8,1,4,8,128]{5,4,3,2,1,0:T(8,128)}, u32[]{:S(2)}, u32[]{:S(2)}) async-start(f32[4,8,1,4,8,128]{5,4,3,2,1,0:T(8,128)} %partial_lags.4), calls=%async_computation.1 | async-start | bytes 1048576 | tf_op jit(solution)/shard_map/all_to_all | solution.py:231
  113.5 22.5 %collective-permute-start.4 = (f32[2,2,1,32,1024]{4,3,2,1,0:T(8,128)}, f32[2,2,1,32,1024]{4,3,2,1,0:T(8,128)}, u32[]{:S(2)}, u32[]{:S(2)}) collective-permute-start(f32[2,2,1,32,1024]{4,3,2,1,0:T(8,128)} %get-tuple-element.14.early_ref), channel_id=1, source_target_pairs={{8,0},{16,8},{24,16},{32,24},{40,32},{48,40},{56,48},{64,56},{72,6... | collective-permute-start | bytes 1572872 | tf_op jit(solution)/shard_map/ppermute | solution.py:228
  114.8 21.2 %collective-permute-start.5 = (f32[2,2,1,32,1024]{4,3,2,1,0:T(8,128)}, f32[2,2,1,32,1024]{4,3,2,1,0:T(8,128)}, u32[]{:S(2)}, u32[]{:S(2)}) collective-permute-start(f32[2,2,1,32,1024]{4,3,2,1,0:T(8,128)} %get-tuple-element.15.late_ref), channel_id=1, source_target_pairs={{0,8},{8,16},{16,24},{24,32},{32,40},{40,48},{48,56},{56,64},{64,7... | collective-permute-start | bytes 1572872 | tf_op jit(solution)/shard_map/ppermute | solution.py:229
  123.4 18.3 %all-to-all-start.4 = ((f32[4,8,1,4,8,128]{5,4,3,2,1,0:T(8,128)}), f32[4,8,1,4,8,128]{5,4,3,2,1,0:T(8,128)}, u32[]{:S(2)}, u32[]{:S(2)}) async-start(f32[4,8,1,4,8,128]{5,4,3,2,1,0:T(8,128)} %partial_lags.5), calls=%async_computation.4 | async-start | bytes 1048576 | tf_op jit(solution)/shard_map/all_to_all | solution.py:231
  130.6 14.6 %collective-permute-start.6 = (f32[2,2,1,32,1024]{4,3,2,1,0:T(8,128)S(1)}, f32[2,2,1,32,1024]{4,3,2,1,0:T(8,128)S(1)}, u32[]{:S(2)}, u32[]{:S(2)}) collective-permute-start(f32[2,2,1,32,1024]{4,3,2,1,0:T(8,128)S(1)} %get-tuple-element.16.early_ref), channel_id=1, source_target_pairs={{8,0},{16,8},{24,16},{32,24},{40,32},{48,40},{56,48},{64,56},{72,6... | collective-permute-start | bytes 1572872 | tf_op jit(solution)/shard_map/ppermute | solution.py:228
  131.9 13.6 %collective-permute-start.7 = (f32[2,2,1,32,1024]{4,3,2,1,0:T(8,128)}, f32[2,2,1,32,1024]{4,3,2,1,0:T(8,128)S(1)}, u32[]{:S(2)}, u32[]{:S(2)}) collective-permute-start(f32[2,2,1,32,1024]{4,3,2,1,0:T(8,128)} %get-tuple-element.17.late_ref), channel_id=1, source_target_pairs={{0,8},{8,16},{16,24},{24,32},{32,40},{40,48},{48,56},{56,64},{64,7... | collective-permute-start | bytes 1572872 | tf_op jit(solution)/shard_map/ppermute | solution.py:229
  141.8 17.6 %all-to-all-start.7 = ((f32[4,8,1,4,8,128]{5,4,3,2,1,0:T(8,128)}), f32[4,8,1,4,8,128]{5,4,3,2,1,0:T(8,128)S(1)}, u32[]{:S(2)}, u32[]{:S(2)}) async-start(f32[4,8,1,4,8,128]{5,4,3,2,1,0:T(8,128)} %partial_lags.6), calls=%async_computation.7 | async-start | bytes 1048576 | tf_op jit(solution)/shard_map/all_to_all | solution.py:231
  159.3 12.5 %all-to-all-start.10 = ((f32[4,8,1,4,8,128]{5,4,3,2,1,0:T(8,128)}), f32[4,8,1,4,8,128]{5,4,3,2,1,0:T(8,128)S(1)}, u32[]{:S(2)}, u32[]{:S(2)}) async-start(f32[4,8,1,4,8,128]{5,4,3,2,1,0:T(8,128)} %partial_lags.7), calls=%async_computation.10 | async-start | bytes 1048576 | tf_op jit(solution)/shard_map/all_to_all | solution.py:231
  171.9 11.3 %all-to-all-start.2 = ((f32[8,1,4,8,128]{4,3,2,1,0:T(8,128)}), f32[8,1,4,8,128]{4,3,2,1,0:T(8,128)S(1)}, u32[]{:S(2)}, u32[]{:S(2)}) async-start(f32[8,1,4,8,128]{4,3,2,1,0:T(8,128)} %bitcast.2), calls=%async_computation.2 | async-start | bytes 262144 | tf_op jit(solution)/shard_map/all_to_all | solution.py:232
  183.2 11.3 %all-to-all-start.5 = ((f32[8,1,4,8,128]{4,3,2,1,0:T(8,128)}), f32[8,1,4,8,128]{4,3,2,1,0:T(8,128)S(1)}, u32[]{:S(2)}, u32[]{:S(2)}) async-start(f32[8,1,4,8,128]{4,3,2,1,0:T(8,128)} %bitcast.3), calls=%async_computation.5 | async-start | bytes 262144 | tf_op jit(solution)/shard_map/all_to_all | solution.py:232
  194.5 11.2 %all-to-all-start.8 = ((f32[8,1,4,8,128]{4,3,2,1,0:T(8,128)}), f32[8,1,4,8,128]{4,3,2,1,0:T(8,128)S(1)}, u32[]{:S(2)}, u32[]{:S(2)}) async-start(f32[8,1,4,8,128]{4,3,2,1,0:T(8,128)} %bitcast.4), calls=%async_computation.8 | async-start | bytes 262144 | tf_op jit(solution)/shard_map/all_to_all | solution.py:232
  205.7 11.2 %all-to-all-start.11 = ((f32[8,1,4,8,128]{4,3,2,1,0:T(8,128)}), f32[8,1,4,8,128]{4,3,2,1,0:T(8,128)S(1)}, u32[]{:S(2)}, u32[]{:S(2)}) async-start(f32[8,1,4,8,128]{4,3,2,1,0:T(8,128)} %bitcast.5), calls=%async_computation.11 | async-start | bytes 262144 | tf_op jit(solution)/shard_map/all_to_all | solution.py:232
  236.4 13.0 %all-to-all-start.13 = ((f32[32,5,128]{2,1,0:T(8,128)}), f32[32,5,128]{2,1,0:T(8,128)S(1)}, u32[]{:S(2)}, u32[]{:S(2)}) async-start(f32[32,5,128]{2,1,0:T(8,128)} %broadcast_in_dim.8), calls=%async_computation.13 | async-start | bytes 262144 | tf_op jit(solution)/shard_map/all_to_all | solution.py:205
where the time goes:
time: 252 us; the launch traced here: 250 us
  waiting for transfers between devices  86.6 us (34%)
  starting transfers between devices  85.7 us (34%)
  Pallas kernels  31.9 us (13%)
  local copies, waits for them, and re-layouts  21 us (8%)
  blocking collectives  14.5 us (6%)
  other arithmetic  7.9 us (3%)
    all_to_all x4, waiting for transfers between devices, body(): piece = lax.all_to_all(piece, ROW, 0, 0, tiled=True)  29.8 us
    all_to_all x4, waiting for transfers between devices, body(): part = jnp.sum(lax.all_to_all(part, 'tm_1', 0, 0, tiled=True), axis=0)  25.7 us
    all_to_all x4, waiting for transfers between devices, body(): part = jnp.sum(lax.all_to_all(part, 'tm_0', 0, 0, tiled=True), axis=0)  22.8 us
    all_to_all x4, starting transfers between devices, body(): piece = lax.all_to_all(piece, ROW, 0, 0, tiled=True)  22.5 us
    all_to_all x4, starting transfers between devices, body(): part = jnp.sum(lax.all_to_all(part, 'tm_0', 0, 0, tiled=True), axis=0)  22.1 us
    ppermute x4, starting transfers between devices, body(): left = lax.ppermute(late, TM, to_right)  18.4 us
    unnamed x26, local copies, waits for them, and re-layouts  15.2 us
    all_to_all x1, blocking collectives, sum_everywhere(): value = jnp.sum(lax.all_to_all(copies, axes, 0, 0, tiled=True), axis=0)  14.5 us
  transfers between devices with their start and end apart: 21, of which 15 were waited for; matrix products, arithmetic and copies ran while one was open for 4% of the time, Pallas kernels for 12%

commit v1 on v0

v1 whole, which is shorter than its diff:
```python
import functools
import math

import jax
import jax.numpy as jnp
import ml_dtypes
import numpy as np
from jax import lax
from jax.experimental import pallas as pl
from jax.experimental.pallas import tpu as pltpu
from jax.sharding import Mesh
from jax.sharding import PartitionSpec as P

N = 1024
LAGS = 4
CYCLES = 128
FRAMES = 128
RADIX = 4
SUB = N // RADIX
OWN = 4
CHUNKS = ((0, 1), (2,), (3,))
ROW = ("row_0", "row_1")
TM = ("tm_0", "tm_1")
YROW = ("tm_0", "row_0", "row_1")

f32 = jnp.float32
bf16 = jnp.bfloat16


def dft_tables():
    freq = 4 * np.arange(SUB)[None, :, None] + np.arange(RADIX)[:, None, None]
    phase = (freq * np.arange(SUB)[None, None, :]) % N
    angle = phase * (2.0 * math.pi / N)
    table = np.concatenate([np.cos(angle), np.sin(angle)], axis=2) / 32.0
    high = table.astype(ml_dtypes.bfloat16)
    low = (table - high.astype(np.float64)).astype(ml_dtypes.bfloat16)
    return high, low


def butterfly(parts_re, parts_im, p):
    (a, b, c, d), (e, f, g, h) = parts_re, parts_im
    if p == 0:
        return (a + c) + (b + d), (e + g) + (f + h)
    if p == 2:
        return (a + c) - (b + d), (e + g) - (f + h)
    if p == 1:
        return (a - c) + (f - h), (e - g) - (b - d)
    return (a - c) - (f - h), (e - g) + (b - d)


def split(z):
    high = z.astype(bf16)
    return high, (z - high.astype(f32)).astype(bf16)


def stacked(zr, zi):
    return jnp.concatenate(
        [jnp.concatenate([zr, zi], axis=1), jnp.concatenate([zi, -zr], axis=1)], axis=0
    )


def nt(a, b):
    return lax.dot_general(a, b, (((1,), (1,)), ((), ())), preferred_element_type=f32)


def first_kernel(residues, movie_ref, high_ref, low_ref, out_ref):
    parts = [[movie_ref[c, 0, :, q * SUB:(q + 1) * SUB] for q in range(RADIX)] for c in range(2)]
    for j, p in enumerate(residues):
        zr, zi = butterfly(parts[0], parts[1], p)
        zh, zl = split(stacked(zr, zi))
        th, tl = high_ref[p], low_ref[p]
        got = nt(th, zh) + nt(tl, zh) + nt(th, zl)
        for c in range(2):
            piece = got[:, c * 128:(c + 1) * 128].reshape(8, 4, 8, 128)
            for y in range(4):
                out_ref[y, :, c, j] = piece[:, y]


def first_transform(movie, high, low, residues):
    count = len(residues)
    table = pl.BlockSpec((RADIX, SUB, 2 * SUB), lambda f: (0, 0, 0))
    return pl.pallas_call(
        functools.partial(first_kernel, residues),
        grid=(OWN,),
        in_specs=[pl.BlockSpec((2, 1, 128, N), lambda f: (0, f, 0, 0)), table, table],
        out_specs=pl.BlockSpec((4, 8, 2, count, 8, 128), lambda f: (0, 0, 0, 0, 0, f)),
        out_shape=jax.ShapeDtypeStruct((4, 8, 2, count, 8, OWN * 128), f32),
        compiler_params=pltpu.CompilerParams(vmem_limit_bytes=24 << 20),
        cost_estimate=pl.CostEstimate(
            flops=count * 6 * 256 * 512 * 1024, bytes_accessed=(4 + count) << 20, transcendentals=0
        ),
        name="first_transform",
    )(movie, high, low)


def second_kernel(count, piece_ref, high_ref, low_ref, early_ref, late_ref):
    for j in range(count):

        def part(c, q):
            return jnp.concatenate(
                [
                    jnp.concatenate(
                        [
                            piece_ref[y, 2 * q + h, c, j, :, f * 128:(f + 1) * 128]
                            for f in range(OWN)
                            for y in range(4)
                        ],
                        axis=0,
                    )
                    for h in range(2)
                ],
                axis=1,
            )

        parts = [[part(c, q) for q in range(RADIX)] for c in range(2)]
        for p in range(RADIX):
            zr, zi = butterfly(parts[0], parts[1], p)
            zh, zl = split(stacked(zr, zi))
            th, tl = high_ref[p], low_ref[p]
            got = nt(zh, th) + nt(zh, tl) + nt(zl, th)
            for c in range(2):
                for f in range(OWN):
                    ref = early_ref if f < 2 else late_ref
                    ref[f % 2, c, j, :, p * SUB:(p + 1) * SUB] = got[
                        (c * OWN + f) * 32:(c * OWN + f + 1) * 32
                    ]


def second_transform(piece, high, low, count):
    half = jax.ShapeDtypeStruct((2, 2, count, 32, N), f32)
    return pl.pallas_call(
        functools.partial(second_kernel, count),
        out_shape=(half, half),
        compiler_params=pltpu.CompilerParams(vmem_limit_bytes=40 << 20),
        cost_estimate=pl.CostEstimate(
            flops=count * 6 * 256 * 512 * 1024, bytes_accessed=(2 + 2 * count) << 20, transcendentals=0
        ),
        name="second_transform",
    )(piece, high, low)


def lag_kernel(
    count, final, ends_ref, early_ref, late_ref, right_ref, left_ref, label_ref, before_ref,
    out_ref, cycle_ref, lags_ref
):
    at_end, at_start = ends_ref[0], ends_ref[1]
    has_right = 1.0 - at_end.astype(f32)
    has_left = 1.0 - at_start.astype(f32)
    cycle_row = lax.broadcasted_iota(jnp.int32, (CYCLES, SUB), 0)
    sub_row = lax.broadcasted_iota(jnp.int32, (32, CYCLES), 0) % 8
    ones = jnp.ones((16, SUB), bf16)
    cycle_sums = jnp.zeros((32, CYCLES), f32)
    cycle_counts = jnp.zeros((16, CYCLES), f32)
    for j in range(count):
        for b in range(8):
            lanes = slice(b * 128, (b + 1) * 128)
            sums = [0.0] * LAGS
            for y in range(4):
                own_rows = slice(y * 8, (y + 1) * 8)
                right_rows = pl.ds(pl.multiple_of(8 * jnp.minimum(y + at_end, 3), 8), 8)
                left_rows = pl.ds(pl.multiple_of(8 * jnp.maximum(y - at_start, 0), 8), 8)
                frames = {}
                for f in range(2):
                    frames[f] = [early_ref[f, c, j, own_rows, lanes] for c in range(2)]
                    frames[2 + f] = [late_ref[f, c, j, own_rows, lanes] for c in range(2)]
                    frames[4 + f] = [right_ref[f, c, j, right_rows, lanes] for c in range(2)]
                    frames[f - 2] = [left_ref[f, c, j, left_rows, lanes] for c in range(2)]

                def total(pairs):
                    terms = []
                    for s, t in pairs:
                        dr = frames[t][0] - frames[s][0]
                        di = frames[t][1] - frames[s][1]
                        terms.append(dr * dr + di * di)
                    return functools.reduce(lambda x, z: x + z, terms)

                for lag in range(1, LAGS + 1):
                    own = [(s, s + lag) for s in range(OWN) if s + lag < OWN]
                    right = [(s, s + lag) for s in range(OWN) if 4 <= s + lag < 6]
                    left = [(s, s + lag) for s in (-2, -1) if s + lag in (2, 3)]
                    terms = [sums[lag - 1]]
                    if own:
                        terms.append(total(own))
                    terms.append(total(right) * has_right if y == 3 else total(right))
                    if left:
                        terms.append(total(left) * has_left if y == 0 else total(left))
                    sums[lag - 1] = functools.reduce(lambda x, z: x + z, terms)
            p, h = b // 2, b % 2
            for lag in range(1, LAGS + 1):
                lags_ref[p * 32 + (lag - 1) * 8:p * 32 + lag * 8, h * 128:(h + 1) * 128] = sums[
                    lag - 1
                ] * (1.0 / float(FRAMES - lag))
        for h in range(2):
            block = lags_ref[:, h * 128:(h + 1) * 128].T
            out_ref[16 * h:16 * h + 16, j] = block.reshape(16, 8, 128)
        for p in range(RADIX):
            dh, dl = split(lags_ref[p * 32:(p + 1) * 32, :])
            rows = jnp.concatenate([dh, dl, ones], axis=0)
            for k in range(8):
                chosen = jnp.where(cycle_row == label_ref[j, p, k:k + 1, :], 1.0, 0.0).astype(bf16)
                got = nt(rows, chosen)
                cycle_sums += jnp.where(sub_row == k, got[:32] + got[32:64], 0.0)
                cycle_counts += got[64:]
    tile = jnp.concatenate(
        [
            jnp.sum(cycle_sums.reshape(LAGS, 8, CYCLES), axis=1),
            cycle_counts[:1] * 0.125,
            jnp.zeros((3, CYCLES), f32),
        ],
        axis=0,
    ) + before_ref[...]
    cycle_ref[...] = tile
    if final:
        for m in range(32):
            out_ref[m, count] = tile


def partial_lags(ends, early, late, right, left, labels, before, count, final):
    vmem = pl.BlockSpec(memory_space=pltpu.VMEM)
    return pl.pallas_call(
        functools.partial(lag_kernel, count, final),
        in_specs=[pl.BlockSpec(memory_space=pltpu.SMEM)] + [vmem] * 6,
        out_specs=(vmem, vmem),
        out_shape=(
            jax.ShapeDtypeStruct((32, count + int(final), 8, 128), f32),
            jax.ShapeDtypeStruct((8, CYCLES), f32),
        ),
        scratch_shapes=[pltpu.VMEM((128, SUB), f32)],
        compiler_params=pltpu.CompilerParams(vmem_limit_bytes=24 << 20),
        cost_estimate=pl.CostEstimate(
            flops=count * 64 * 80 * 256 * 128, bytes_accessed=count * 5 << 19, transcendentals=0
        ),
        name="partial_lags",
    )(ends, early, late, right, left, labels, before)


def body(movie, cycle_label, valid_mask):
    high, low = dft_tables()
    high, low = jnp.asarray(high), jnp.asarray(low)
    z_count = lax.axis_size("tm_1")
    z_place = lax.axis_index("tm_1")
    ends = jnp.stack([z_place == z_count - 1, z_place == 0]).astype(jnp.int32)
    labels = jnp.where(valid_mask == 1, cycle_label, -1)
    labels = lax.dynamic_slice_in_dim(labels, lax.axis_index("tm_0") * 32, 32, 1)
    labels = labels.reshape(SUB, RADIX, 8, RADIX).transpose(3, 1, 2, 0)
    to_left = [(i, (i - 1) % z_count) for i in range(z_count)]
    to_right = [(i, (i + 1) % z_count) for i in range(z_count)]
    cycles = jnp.zeros((8, CYCLES), f32)
    slabs = []
    done = []
    for index, residues in enumerate(CHUNKS):
        count = len(residues)
        final = index == len(CHUNKS) - 1
        piece = first_transform(movie, high, low, residues)
        if index >= 2:
            piece, done[index - 2] = lax.optimization_barrier((piece, done[index - 2]))
        piece = piece.reshape((32,) + piece.shape[2:])
        piece = lax.all_to_all(piece, YROW, 0, 0, tiled=True)
        piece = piece.reshape((4, 8) + piece.shape[1:])
        early, late = second_transform(piece, high, low, count)
        done.append((early, late))
    for index, residues in enumerate(CHUNKS):
        count = len(residues)
        final = index == len(CHUNKS) - 1
        early, late = done[index]
        right = lax.ppermute(early, "tm_1", to_left)
        left = lax.ppermute(late, "tm_1", to_right)
        part, cycles = partial_lags(
            ends, early, late, right, left, labels[residues[0]:residues[-1] + 1], cycles, count, final
        )
        part = lax.all_to_all(part, TM, 0, 0, tiled=True)
        if final:
            cycles = jnp.sum(part[:, count], axis=0)
        slabs.append(jnp.sum(part[:, :count].reshape(4, 8, count, 8, 128), axis=1))
    slab = jnp.concatenate(slabs, axis=1).reshape(4, RADIX, 8, RADIX, LAGS, 8)
    image_structure = jnp.transpose(slab, (4, 2, 3, 0, 5, 1)).reshape(LAGS, 32, 128)
    copies = jnp.broadcast_to(cycles[None], (8,) + cycles.shape)
    sums = jnp.sum(lax.all_to_all(copies, ROW, 0, 0, tiled=True), axis=0)
    cycle_curve = sums[:LAGS] / jnp.maximum(sums[LAGS], 1.0)[None, :]
    return (cycle_curve, image_structure)


def solution(mesh):
    torus = Mesh(mesh.devices.reshape(4, 8, 4, 2), ("tm_0", "tm_1", "row_0", "row_1"))
    placed = (P(None, TM, ROW, None), P(None, ROW), P(None, ROW))
    return jax.shard_map(
        body, mesh=torus, in_specs=placed, out_specs=(P(), P(None, TM, ROW)), check_vma=False
    )
```

time: 252 us -> 173 us (0.69)
  waiting for transfers between devices: 86.6 us -> 52.1 us
  starting transfers between devices: 85.7 us -> 58.6 us
  blocking collectives: 14.5 us -> 0 us
  local copies, waits for them, and re-layouts: 21 us -> 28.2 us
  other arithmetic: 7.9 us -> 3.38 us
  Pallas kernels: 31.9 us -> 28.6 us
    all_to_all x13 -> x7, waiting for transfers between devices: 85.2 us -> 41.1 us  [the longest x3 24.3 us: body(): piece = lax.all_to_all(piece, YROW, 0, 0, tiled=True)]
    all_to_all x13 -> x7, starting transfers between devices: 62.1 us -> 47.1 us  [the longest x3 20.8 us: body(): piece = lax.all_to_all(piece, YROW, 0, 0, tiled=True)]
    all_to_all x1 -> x0, blocking collectives: 14.5 us -> none  [sum_everywhere(): value = jnp.sum(lax.all_to_all(copies, axes, 0, 0, tiled=True), axis=0)]
    ppermute x8 -> x6, starting transfers between devices: 23.5 us -> 11.5 us  [the longest x3 11.5 us: body(): right = lax.ppermute(early, 'tm_1', to_left)]
    ppermute x8 -> x6, waiting for transfers between devices: 1.39 us -> 10.9 us  [the longest x3 6.51 us: body(): right = lax.ppermute(early, 'tm_1', to_left)]
    reshape x1 -> x3, local copies, waits for them, and re-layouts: 2.28 us -> 9.58 us  [the longest x2 7.3 us: body(): labels = labels.reshape(SUB, RADIX, 8, RADIX).transpose(3, 1, 2, 0)]
    reduce_sum x11 -> x4, other arithmetic: 6.4 us -> 0.05 us  [the longest x3 0.04 us: body(): slabs.append(jnp.sum(part[:, :count].reshape(4, 8, count, 8, 128), axis=1))]
    pallas_call x4 -> x3, Pallas kernels: 12.7 us -> 8.89 us  [second_transform(): pl.pallas_call(functools.partial(second_kernel, count), out_shape=(half,...]
  transfers between devices with their start and end apart: 21 -> 13, of which waited for: 15 -> 10; matrix products, arithmetic and copies ran while one was open for 4% -> 10% of each run, Pallas kernels for 12% -> 15%
where the time goes in v1:
time: 173 us; the launch traced here: 172 us
  starting transfers between devices  58.6 us (34%)
  waiting for transfers between devices  52.1 us (30%)
  Pallas kernels  28.6 us (17%)
  local copies, waits for them, and re-layouts  28.2 us (16%)
  other arithmetic  3.38 us (2%)
    all_to_all x3, waiting for transfers between devices, body(): piece = lax.all_to_all(piece, YROW, 0, 0, tiled=True)  24.3 us
    all_to_all x3, starting transfers between devices, body(): piece = lax.all_to_all(piece, YROW, 0, 0, tiled=True)  20.8 us
    all_to_all x3, waiting for transfers between devices, body(): part = lax.all_to_all(part, TM, 0, 0, tiled=True)  16.8 us
    all_to_all x3, starting transfers between devices, body(): part = lax.all_to_all(part, TM, 0, 0, tiled=True)  14.4 us
    unnamed x22, local copies, waits for them, and re-layouts  13.5 us
    all_to_all x1, starting transfers between devices, body(): sums = jnp.sum(lax.all_to_all(copies, ROW, 0, 0, tiled=True), axis=0)  11.9 us
    pallas_call x3, Pallas kernels, partial_lags(): pl.pallas_call(functools.partial(lag_kernel, count, final), in_specs=[pl....  11.6 us
    ppermute x3, starting transfers between devices, body(): right = lax.ppermute(early, 'tm_1', to_left)  11.5 us
  transfers between devices with their start and end apart: 13, of which 10 were waited for; matrix products, arithmetic and copies ran while one was open for 10% of the time, Pallas kernels for 15%

profile of v1, /device:TPU:1, one launch (start us, length us, event | category | flops | bytes accessed | tf_op | source)
XLA Modules:
  0.0 171.8 jit_solution(6138032590450270468)
XLA Ops:
  0.6 0.0 copy-start
  0.6 2.2 %copy-done = f32[2,4,128,1024]{3,2,1,0:T(8,128)S(1)} copy-done((f32[2,4,128,1024]{3,2,1,0:T(8,128)S(1)}, f32[2,4,128,1024]{3,2,1,0:T(8,128)}, u32[]{:S(2)}) %copy-start) | copy-done | bytes 4194328
  2.8 1.2 copy-done.3
  4.0 1.2 copy-done.5
  5.3 3.0 %first_transform.4 = f32[4,8,2,2,8,512]{5,4,3,2,1,0:T(8,128)S(1)} custom-call(f32[2,4,128,1024]{3,2,1,0:T(8,128)S(1)} %copy-done, bf16[4,256,512]{2,1,0:T(8,128)(2,1)S(1)} %copy-done.3, bf16[4,256,512]{2,1,0:T(8,128)(2,1)S(1)} %copy-done.5), custom_call_target="tpu_custom_call" | custom-call | flops 1610612736 | bytes 6291456 | tf_op jit(solution)/shard_map/first_transform/pallas_call | solution.py:82
  8.3 0.0 copy-start.7
  8.3 1.3 copy-done.7
  9.6 8.8 %all-to-all-start = ((f32[32,2,2,8,512]{4,3,2,1,0:T(8,128)}), f32[32,2,2,8,512]{4,3,2,1,0:T(8,128)}, u32[]{:S(2)}, u32[]{:S(2)}) async-start(f32[32,2,2,8,512]{4,3,2,1,0:T(8,128)} %bitcast.31), calls=%async_computation | async-start | bytes 4194304 | tf_op jit(solution)/shard_map/all_to_all | solution.py:258
  18.4 0.0 copy-done.4
  18.4 0.0 copy-done.6
  18.4 0.0 copy-start.1
  18.4 2.2 %copy-done.1 = f32[2,4,128,1024]{3,2,1,0:T(8,128)S(1)} copy-done((f32[2,4,128,1024]{3,2,1,0:T(8,128)S(1)}, f32[2,4,128,1024]{3,2,1,0:T(8,128)}, u32[]{:S(2)}) %copy-start.1) | copy-done | bytes 4194328
  20.6 2.1 %first_transform.5 = f32[4,8,2,1,8,512]{5,4,3,2,1,0:T(8,128)S(1)} custom-call(f32[2,4,128,1024]{3,2,1,0:T(8,128)S(1)} %copy-done.1, bf16[4,256,512]{2,1,0:T(8,128)(2,1)S(1)} %copy-done.4, bf16[4,256,512]{2,1,0:T(8,128)(2,1)S(1)} %copy-done.6), custom_call_target="tpu_custom_call" | custom-call | flops 805306368 | bytes 5242880 | tf_op jit(solution)/shard_map/first_transform/pallas_call | solution.py:82
  22.7 0.0 copy-start.10
  22.7 1.0 copy-done.10
  23.7 22.6 %all-to-all-done = f32[32,2,2,8,512]{4,3,2,1,0:T(8,128)} async-done(((f32[32,2,2,8,512]{4,3,2,1,0:T(8,128)}), f32[32,2,2,8,512]{4,3,2,1,0:T(8,128)}, u32[]{:S(2)}, u32[]{:S(2)}) %all-to-all-start) | async-done | bytes 2097184 | tf_op jit(solution)/shard_map/all_to_all | solution.py:258
  46.3 6.0 %all-to-all-start.2 = ((f32[32,2,1,8,512]{4,3,1,2,0:T(8,128)}), f32[32,2,1,8,512]{4,3,1,2,0:T(8,128)S(1)}, u32[]{:S(2)}, u32[]{:S(2)}) async-start(f32[32,2,1,8,512]{4,3,1,2,0:T(8,128)} %bitcast.34), calls=%async_computation.2 | async-start | bytes 2097152 | tf_op jit(solution)/shard_map/all_to_all | solution.py:258
  52.3 0.0 copy-start.2
  52.3 2.2 %copy-done.2 = f32[2,4,128,1024]{3,2,1,0:T(8,128)S(1)} copy-done((f32[2,4,128,1024]{3,2,1,0:T(8,128)S(1)}, f32[2,4,128,1024]{3,2,1,0:T(8,128)}, u32[]{:S(2)}) %copy-start.2) | copy-done | bytes 4194328
  54.5 3.0 %first_transform.3 = f32[4,8,2,1,8,512]{5,4,3,2,1,0:T(8,128)} custom-call(f32[2,4,128,1024]{3,2,1,0:T(8,128)S(1)} %copy-done.2, bf16[4,256,512]{2,1,0:T(8,128)(2,1)S(1)} %copy-done.4, bf16[4,256,512]{2,1,0:T(8,128)(2,1)S(1)} %copy-done.6), custom_call_target="tpu_custom_call" | custom-call | flops 805306368 | bytes 5242880 | tf_op jit(solution)/shard_map/first_transform/pallas_call | solution.py:82
  57.5 4.8 %second_transform.3 = (f32[2,2,2,32,1024]{4,3,2,1,0:T(8,128)}, f32[2,2,2,32,1024]{4,3,2,1,0:T(8,128)}) custom-call(f32[4,8,2,2,8,512]{5,4,3,2,1,0:T(8,128)} %bitcast.3.piece_ref, bf16[4,256,512]{2,1,0:T(8,128)(2,1)S(1)} %copy-done.4, bf16[4,256,512]{2,1,0:T(8,128)(2,1)S(1)} %copy-done.6), custom_call_target="tpu_custom_call" | custom-call | flops 1610612736 | bytes 6291456 | tf_op jit(solution)/shard_map/second_transform/pallas_call | solution.py:131
  62.3 5.6 %collective-permute-start.4 = (f32[2,2,2,32,1024]{4,3,2,1,0:T(8,128)}, f32[2,2,2,32,1024]{4,3,2,1,0:T(8,128)}, u32[]{:S(2)}, u32[]{:S(2)}) collective-permute-start(f32[2,2,2,32,1024]{4,3,2,1,0:T(8,128)} %get-tuple-element.23.early_ref), channel_id=1, source_target_pairs={{0,56},{8,0},{16,8},{24,16},{32,24},{40,32},{48,40},{56,48},{1,57}... | collective-permute-start | bytes 3145736 | tf_op jit(solution)/shard_map/ppermute | solution.py:266
  67.9 0.0 collective-permute-start.5
  67.9 1.7 all-to-all-done.2
  69.6 1.0 copy-done.8
  70.5 6.1 %all-to-all-start.1 = ((f32[32,2,1,8,512]{4,3,1,2,0:T(8,128)}), f32[32,2,1,8,512]{4,3,1,2,0:T(8,128)S(1)}, u32[]{:S(2)}, u32[]{:S(2)}) async-start(f32[32,2,1,8,512]{4,3,1,2,0:T(8,128)} %bitcast.5), calls=%async_computation.1 | async-start | bytes 2097152 | tf_op jit(solution)/shard_map/all_to_all | solution.py:258
  76.6 0.0 copy-start.9
  76.7 1.2 copy-done.9
  77.9 2.0 %second_transform.5 = (f32[2,2,1,32,1024]{4,3,2,1,0:T(8,128)}, f32[2,2,1,32,1024]{4,3,2,1,0:T(8,128)}) custom-call(f32[4,8,2,1,8,512]{5,4,3,2,1,0:T(8,128)S(1)} %bitcast.33, bf16[4,256,512]{2,1,0:T(8,128)(2,1)S(1)} %copy-done.4, bf16[4,256,512]{2,1,0:T(8,128)(2,1)S(1)} %copy-done.6), custom_call_target="tpu_custom_call" | custom-call | flops 805306368 | bytes 4194304 | tf_op jit(solution)/shard_map/second_transform/pallas_call | solution.py:131
  79.9 3.5 %collective-permute-start.2 = (f32[2,2,1,32,1024]{4,3,2,1,0:T(8,128)}, f32[2,2,1,32,1024]{4,3,2,1,0:T(8,128)}, u32[]{:S(2)}, u32[]{:S(2)}) collective-permute-start(f32[2,2,1,32,1024]{4,3,2,1,0:T(8,128)} %get-tuple-element.21.early_ref), channel_id=1, source_target_pairs={{0,56},{8,0},{16,8},{24,16},{32,24},{40,32},{48,40},{56,48},{1,57}... | collective-permute-start | bytes 1572872 | tf_op jit(solution)/shard_map/ppermute | solution.py:266
  83.3 0.0 collective-permute-start.3
  83.4 2.3 %dynamic-slice_select_fusion = s32[1024,32]{1,0:T(8,128)} fusion(s32[1024,128]{1,0:T(8,128)} %param.6, s32[]{:T(128)S(6)} %select_n.8, s32[1024,128]{1,0:T(8,128)} %param.7), kind=kLoop, calls=%fused_computation.1 | loop fusion | flops 65536 | bytes 393220 | tf_op jit(solution)/shard_map/jit(_where)/select_n | solution.py:243
  85.7 3.7 %reshape.57 = s32[256,4,8,4]{3,2,1,0:T(8,128)} reshape(s32[1024,32]{1,0:T(8,128)} %dynamic-slice_select_fusion) | data formatting | bytes 262144 | tf_op jit(solution)/shard_map/reshape | solution.py:245
  89.4 3.6 %copy.21 = s32[256,4,8,4]{0,2,1,3:T(8,128)S(1)} copy(s32[256,4,8,4]{3,2,1,0:T(8,128)} %reshape.57) | data formatting | bytes 262144 | tf_op jit(solution)/shard_map/reshape | solution.py:245
  93.0 0.1 add_convert_fusion.ends_ref
  93.1 0.0 collective-permute-done.4.right_ref
  93.1 0.4 collective-permute-done.5.left_ref
  93.5 5.1 %partial_lags.3 = (f32[32,2,8,128]{3,2,1,0:T(8,128)}, f32[8,128]{1,0:T(8,128)S(1)}) custom-call(s32[2]{0:T(128)S(1)} %add_convert_fusion.ends_ref, f32[2,2,2,32,1024]{4,3,2,1,0:T(8,128)} %get-tuple-element.23.early_ref, f32[2,2,2,32,1024]{4,3,2,1,0:T(8,128)} %get-tuple-element.24.late_ref, f32[2,2,2,32,1024]{4,3,2,1,0:T(8,128)} %collective-permute-done.4.right_ref, ...), custom_call_target="tpu_custom_call" | custom-call | flops 335544320 | bytes 5242880 | tf_op jit(solution)/shard_map/partial_lags/pallas_call | solution.py:220
  98.6 3.0 %collective-permute-done.2.right_ref = f32[2,2,1,32,1024]{4,3,2,1,0:T(8,128)} collective-permute-done((f32[2,2,1,32,1024]{4,3,2,1,0:T(8,128)}, f32[2,2,1,32,1024]{4,3,2,1,0:T(8,128)}, u32[]{:S(2)}, u32[]{:S(2)}) %collective-permute-start.2) | collective-permute-done | bytes 524320 | tf_op jit(solution)/shard_map/ppermute | solution.py:266
  101.6 3.1 %collective-permute-done.3.left_ref = f32[2,2,1,32,1024]{4,3,2,1,0:T(8,128)} collective-permute-done((f32[2,2,1,32,1024]{4,3,2,1,0:T(8,128)}, f32[2,2,1,32,1024]{4,3,2,1,0:T(8,128)}, u32[]{:S(2)}, u32[]{:S(2)}) %collective-permute-start.3) | collective-permute-done | bytes 524320 | tf_op jit(solution)/shard_map/ppermute | solution.py:267
  104.7 3.4 %partial_lags.4 = (f32[32,1,8,128]{3,2,1,0:T(8,128)}, f32[8,128]{1,0:T(8,128)S(1)}) custom-call(s32[2]{0:T(128)S(1)} %add_convert_fusion.ends_ref, f32[2,2,1,32,1024]{4,3,2,1,0:T(8,128)} %get-tuple-element.21.early_ref, f32[2,2,1,32,1024]{4,3,2,1,0:T(8,128)} %get-tuple-element.22.late_ref, f32[2,2,1,32,1024]{4,3,2,1,0:T(8,128)} %collective-permute-done.2.right_ref, ...), custom_call_target="tpu_custom_call" | custom-call | flops 167772160 | bytes 2621440 | tf_op jit(solution)/shard_map/partial_lags/pallas_call | solution.py:220
  108.0 0.0 all-to-all-done.1
  108.1 5.9 %all-to-all-start.6 = ((f32[32,1,8,128]{3,2,1,0:T(8,128)}), f32[32,1,8,128]{3,2,1,0:T(8,128)S(1)}, u32[]{:S(2)}, u32[]{:S(2)}) async-start(f32[32,1,8,128]{3,2,1,0:T(8,128)} %get-tuple-element.29), calls=%async_computation.6 | async-start | bytes 262144 | tf_op jit(solution)/shard_map/all_to_all | solution.py:271
  114.0 2.0 %second_transform.4 = (f32[2,2,1,32,1024]{4,3,2,1,0:T(8,128)}, f32[2,2,1,32,1024]{4,3,2,1,0:T(8,128)}) custom-call(f32[4,8,2,1,8,512]{5,4,3,2,1,0:T(8,128)S(1)} %bitcast.32, bf16[4,256,512]{2,1,0:T(8,128)(2,1)S(1)} %copy-done.4, bf16[4,256,512]{2,1,0:T(8,128)(2,1)S(1)} %copy-done.6), custom_call_target="tpu_custom_call" | custom-call | flops 805306368 | bytes 4194304 | tf_op jit(solution)/shard_map/second_transform/pallas_call | solution.py:131
  116.0 2.4 %collective-permute-start = (f32[2,2,1,32,1024]{4,3,2,1,0:T(8,128)}, f32[2,2,1,32,1024]{4,3,2,1,0:T(8,128)S(1)}, u32[]{:S(2)}, u32[]{:S(2)}) collective-permute-start(f32[2,2,1,32,1024]{4,3,2,1,0:T(8,128)} %get-tuple-element.19.early_ref), channel_id=1, source_target_pairs={{0,56},{8,0},{16,8},{24,16},{32,24},{40,32},{48,40},{56,48},{1,57}... | collective-permute-start | bytes 1572872 | tf_op jit(solution)/shard_map/ppermute | solution.py:266
  118.4 0.0 collective-permute-start.1
  118.4 4.7 %all-to-all-done.6 = f32[32,1,8,128]{3,2,1,0:T(8,128)S(1)} async-done(((f32[32,1,8,128]{3,2,1,0:T(8,128)}), f32[32,1,8,128]{3,2,1,0:T(8,128)S(1)}, u32[]{:S(2)}, u32[]{:S(2)}) %all-to-all-start.6) | async-done | bytes 131104 | tf_op jit(solution)/shard_map/all_to_all | solution.py:271
  123.1 3.9 %all-to-all-start.5 = ((f32[32,2,8,128]{3,2,1,0:T(8,128)}), f32[32,2,8,128]{3,2,1,0:T(8,128)S(1)}, u32[]{:S(2)}, u32[]{:S(2)}) async-start(f32[32,2,8,128]{3,2,1,0:T(8,128)} %get-tuple-element.28), calls=%async_computation.5 | async-start | bytes 524288 | tf_op jit(solution)/shard_map/all_to_all | solution.py:271
  127.0 3.5 %collective-permute-done.right_ref = f32[2,2,1,32,1024]{4,3,2,1,0:T(8,128)S(1)} collective-permute-done((f32[2,2,1,32,1024]{4,3,2,1,0:T(8,128)}, f32[2,2,1,32,1024]{4,3,2,1,0:T(8,128)S(1)}, u32[]{:S(2)}, u32[]{:S(2)}) %collective-permute-start) | collective-permute-done | bytes 524320 | tf_op jit(solution)/shard_map/ppermute | solution.py:266
  130.5 1.0 collective-permute-done.1.left_ref
  131.5 3.2 %partial_lags.5 = (f32[32,2,8,128]{3,2,1,0:T(8,128)}, f32[8,128]{1,0:T(8,128)}) custom-call(s32[2]{0:T(128)S(1)} %add_convert_fusion.ends_ref, f32[2,2,1,32,1024]{4,3,2,1,0:T(8,128)} %get-tuple-element.19.early_ref, f32[2,2,1,32,1024]{4,3,2,1,0:T(8,128)} %get-tuple-element.20.late_ref, f32[2,2,1,32,1024]{4,3,2,1,0:T(8,128)S(1)} %collective-permute-done.right_ref, ...), custom_call_target="tpu_custom_call" | custom-call | flops 167772160 | bytes 2621440 | tf_op jit(solution)/shard_map/partial_lags/pallas_call | solution.py:220
  134.6 3.6 %all-to-all-done.5 = f32[32,2,8,128]{3,2,1,0:T(8,128)S(1)} async-done(((f32[32,2,8,128]{3,2,1,0:T(8,128)}), f32[32,2,8,128]{3,2,1,0:T(8,128)S(1)}, u32[]{:S(2)}, u32[]{:S(2)}) %all-to-all-start.5) | async-done | bytes 262176 | tf_op jit(solution)/shard_map/all_to_all | solution.py:271
  138.2 4.6 %all-to-all-start.3 = ((f32[32,2,8,128]{3,2,1,0:T(8,128)}), f32[32,2,8,128]{3,2,1,0:T(8,128)S(1)}, u32[]{:S(2)}, u32[]{:S(2)}) async-start(f32[32,2,8,128]{3,2,1,0:T(8,128)} %get-tuple-element.27), calls=%async_computation.3 | async-start | bytes 524288 | tf_op jit(solution)/shard_map/all_to_all | solution.py:271
  142.8 0.3 concatenate.11
  143.2 0.6 concatenate.10
  143.8 8.6 %all-to-all-done.3 = f32[32,2,8,128]{3,2,1,0:T(8,128)S(1)} async-done(((f32[32,2,8,128]{3,2,1,0:T(8,128)}), f32[32,2,8,128]{3,2,1,0:T(8,128)S(1)}, u32[]{:S(2)}, u32[]{:S(2)}) %all-to-all-start.3) | async-done | bytes 262176 | tf_op jit(solution)/shard_map/all_to_all | solution.py:271
  152.5 0.3 concatenate.12
  152.8 0.6 broadcast_in_dim.16
  153.5 11.9 %all-to-all-start.4 = ((f32[8,8,128]{2,1,0:T(8,128)}), f32[8,8,128]{2,1,0:T(8,128)S(1)}, u32[]{:S(2)}, u32[]{:S(2)}) async-start(f32[8,8,128]{2,1,0:T(8,128)} %broadcast_in_dim.16), calls=%async_computation.4 | async-start | bytes 65536 | tf_op jit(solution)/shard_map/all_to_all | solution.py:278
  165.4 0.3 maximum_bitcast_fusion
  165.7 3.2 %copy.25 = f32[4,8,4,4,8,4]{5,4,3,2,1,0:T(8,128)S(1)} copy(f32[4,8,4,4,8,4]{4,0,2,1,5,3:T(4,128)S(1)} %maximum_bitcast_fusion) | data formatting | bytes 131072 | tf_op jit(solution)/shard_map/transpose | solution.py:276
  168.9 2.3 %reshape.56 = f32[4,32,128]{2,1,0:T(8,128)} reshape(f32[4,8,4,4,8,4]{5,4,3,2,1,0:T(8,128)S(1)} %copy.25) | data formatting | bytes 131072 | tf_op jit(solution)/shard_map/reshape | solution.py:276
  171.1 0.0 all-to-all-done.4
  171.2 0.6 slice_divide_fusion
  (14 shorter events, 0.1 us)
Async XLA Ops:
  0.6 2.2 %copy-start = (f32[2,4,128,1024]{3,2,1,0:T(8,128)S(1)}, f32[2,4,128,1024]{3,2,1,0:T(8,128)}, u32[]{:S(2)}) copy-start(f32[2,4,128,1024]{3,2,1,0:T(8,128)} %movie_ref.5) | copy-start | bytes 12582916
  2.8 1.2 copy-start.3
  4.0 1.2 copy-start.5
  8.3 1.3 copy-start.7
  9.6 8.8 %copy-start.4 = (bf16[4,256,512]{2,1,0:T(8,128)(2,1)S(1)}, bf16[4,256,512]{2,1,0:T(8,128)(2,1)}, u32[]{:S(2)}) copy-start(bf16[4,256,512]{2,1,0:T(8,128)(2,1)} %constant.31.clone.high_ref) | copy-start | bytes 3145732
  9.6 8.8 %copy-start.6 = (bf16[4,256,512]{2,1,0:T(8,128)(2,1)S(1)}, bf16[4,256,512]{2,1,0:T(8,128)(2,1)}, u32[]{:S(2)}) copy-start(bf16[4,256,512]{2,1,0:T(8,128)(2,1)} %constant.32.clone.low_ref) | copy-start | bytes 3145732
  9.6 36.7 %all-to-all-start = ((f32[32,2,2,8,512]{4,3,2,1,0:T(8,128)}), f32[32,2,2,8,512]{4,3,2,1,0:T(8,128)}, u32[]{:S(2)}, u32[]{:S(2)}) async-start(f32[32,2,2,8,512]{4,3,2,1,0:T(8,128)} %bitcast.31), calls=%async_computation | async-start | bytes 4194304 | tf_op jit(solution)/shard_map/all_to_all | solution.py:258
  18.4 2.2 %copy-start.1 = (f32[2,4,128,1024]{3,2,1,0:T(8,128)S(1)}, f32[2,4,128,1024]{3,2,1,0:T(8,128)}, u32[]{:S(2)}) copy-start(f32[2,4,128,1024]{3,2,1,0:T(8,128)} %movie_ref.5) | copy-start | bytes 12582916
  22.7 1.0 copy-start.10
  46.3 23.3 %all-to-all-start.2 = ((f32[32,2,1,8,512]{4,3,1,2,0:T(8,128)}), f32[32,2,1,8,512]{4,3,1,2,0:T(8,128)S(1)}, u32[]{:S(2)}, u32[]{:S(2)}) async-start(f32[32,2,1,8,512]{4,3,1,2,0:T(8,128)} %bitcast.34), calls=%async_computation.2 | async-start | bytes 2097152 | tf_op jit(solution)/shard_map/all_to_all | solution.py:258
  52.3 2.2 %copy-start.2 = (f32[2,4,128,1024]{3,2,1,0:T(8,128)S(1)}, f32[2,4,128,1024]{3,2,1,0:T(8,128)}, u32[]{:S(2)}) copy-start(f32[2,4,128,1024]{3,2,1,0:T(8,128)} %movie_ref.5) | copy-start | bytes 12582916
  62.3 30.8 %collective-permute-start.4 = (f32[2,2,2,32,1024]{4,3,2,1,0:T(8,128)}, f32[2,2,2,32,1024]{4,3,2,1,0:T(8,128)}, u32[]{:S(2)}, u32[]{:S(2)}) collective-permute-start(f32[2,2,2,32,1024]{4,3,2,1,0:T(8,128)} %get-tuple-element.23.early_ref), channel_id=1, source_target_pairs={{0,56},{8,0},{16,8},{24,16},{32,24},{40,32},{48,40},{56,48},{1,57}... | collective-permute-start | bytes 3145736 | tf_op jit(solution)/shard_map/ppermute | solution.py:266
  67.9 25.6 %collective-permute-start.5 = (f32[2,2,2,32,1024]{4,3,2,1,0:T(8,128)}, f32[2,2,2,32,1024]{4,3,2,1,0:T(8,128)}, u32[]{:S(2)}, u32[]{:S(2)}) collective-permute-start(f32[2,2,2,32,1024]{4,3,2,1,0:T(8,128)} %get-tuple-element.24.late_ref), channel_id=1, source_target_pairs={{0,8},{8,16},{16,24},{24,32},{32,40},{40,48},{48,56},{56,0},{1,9},... | collective-permute-start | bytes 3145736 | tf_op jit(solution)/shard_map/ppermute | solution.py:267
  69.6 1.0 copy-start.8
  70.5 37.5 %all-to-all-start.1 = ((f32[32,2,1,8,512]{4,3,1,2,0:T(8,128)}), f32[32,2,1,8,512]{4,3,1,2,0:T(8,128)S(1)}, u32[]{:S(2)}, u32[]{:S(2)}) async-start(f32[32,2,1,8,512]{4,3,1,2,0:T(8,128)} %bitcast.5), calls=%async_computation.1 | async-start | bytes 2097152 | tf_op jit(solution)/shard_map/all_to_all | solution.py:258
  76.6 1.2 copy-start.9
  79.9 21.7 %collective-permute-start.2 = (f32[2,2,1,32,1024]{4,3,2,1,0:T(8,128)}, f32[2,2,1,32,1024]{4,3,2,1,0:T(8,128)}, u32[]{:S(2)}, u32[]{:S(2)}) collective-permute-start(f32[2,2,1,32,1024]{4,3,2,1,0:T(8,128)} %get-tuple-element.21.early_ref), channel_id=1, source_target_pairs={{0,56},{8,0},{16,8},{24,16},{32,24},{40,32},{48,40},{56,48},{1,57}... | collective-permute-start | bytes 1572872 | tf_op jit(solution)/shard_map/ppermute | solution.py:266
  83.3 21.3 %collective-permute-start.3 = (f32[2,2,1,32,1024]{4,3,2,1,0:T(8,128)}, f32[2,2,1,32,1024]{4,3,2,1,0:T(8,128)}, u32[]{:S(2)}, u32[]{:S(2)}) collective-permute-start(f32[2,2,1,32,1024]{4,3,2,1,0:T(8,128)} %get-tuple-element.22.late_ref), channel_id=1, source_target_pairs={{0,8},{8,16},{16,24},{24,32},{32,40},{40,48},{48,56},{56,0},{1,9},... | collective-permute-start | bytes 1572872 | tf_op jit(solution)/shard_map/ppermute | solution.py:267
  108.1 15.1 %all-to-all-start.6 = ((f32[32,1,8,128]{3,2,1,0:T(8,128)}), f32[32,1,8,128]{3,2,1,0:T(8,128)S(1)}, u32[]{:S(2)}, u32[]{:S(2)}) async-start(f32[32,1,8,128]{3,2,1,0:T(8,128)} %get-tuple-element.29), calls=%async_computation.6 | async-start | bytes 262144 | tf_op jit(solution)/shard_map/all_to_all | solution.py:271
  116.0 14.5 %collective-permute-start = (f32[2,2,1,32,1024]{4,3,2,1,0:T(8,128)}, f32[2,2,1,32,1024]{4,3,2,1,0:T(8,128)S(1)}, u32[]{:S(2)}, u32[]{:S(2)}) collective-permute-start(f32[2,2,1,32,1024]{4,3,2,1,0:T(8,128)} %get-tuple-element.19.early_ref), channel_id=1, source_target_pairs={{0,56},{8,0},{16,8},{24,16},{32,24},{40,32},{48,40},{56,48},{1,57}... | collective-permute-start | bytes 1572872 | tf_op jit(solution)/shard_map/ppermute | solution.py:266
  118.4 13.0 %collective-permute-start.1 = (f32[2,2,1,32,1024]{4,3,2,1,0:T(8,128)}, f32[2,2,1,32,1024]{4,3,2,1,0:T(8,128)S(1)}, u32[]{:S(2)}, u32[]{:S(2)}) collective-permute-start(f32[2,2,1,32,1024]{4,3,2,1,0:T(8,128)} %get-tuple-element.20.late_ref), channel_id=1, source_target_pairs={{0,8},{8,16},{16,24},{24,32},{32,40},{40,48},{48,56},{56,0},{1,9},... | collective-permute-start | bytes 1572872 | tf_op jit(solution)/shard_map/ppermute | solution.py:267
  123.1 15.1 %all-to-all-start.5 = ((f32[32,2,8,128]{3,2,1,0:T(8,128)}), f32[32,2,8,128]{3,2,1,0:T(8,128)S(1)}, u32[]{:S(2)}, u32[]{:S(2)}) async-start(f32[32,2,8,128]{3,2,1,0:T(8,128)} %get-tuple-element.28), calls=%async_computation.5 | async-start | bytes 524288 | tf_op jit(solution)/shard_map/all_to_all | solution.py:271
  138.2 14.3 %all-to-all-start.3 = ((f32[32,2,8,128]{3,2,1,0:T(8,128)}), f32[32,2,8,128]{3,2,1,0:T(8,128)S(1)}, u32[]{:S(2)}, u32[]{:S(2)}) async-start(f32[32,2,8,128]{3,2,1,0:T(8,128)} %get-tuple-element.27), calls=%async_computation.3 | async-start | bytes 524288 | tf_op jit(solution)/shard_map/all_to_all | solution.py:271
  153.5 17.7 %all-to-all-start.4 = ((f32[8,8,128]{2,1,0:T(8,128)}), f32[8,8,128]{2,1,0:T(8,128)S(1)}, u32[]{:S(2)}, u32[]{:S(2)}) async-start(f32[8,8,128]{2,1,0:T(8,128)} %broadcast_in_dim.16), calls=%async_computation.4 | async-start | bytes 65536 | tf_op jit(solution)/shard_map/all_to_all | solution.py:278

commit v2 on v1

--- a/solution.py
+++ b/solution.py
@@ -18,6 +18,7 @@
 RADIX = 4
 SUB = N // RADIX
 OWN = 4
+REST_VMEM, SECOND_VMEM, LAG_VMEM = 56, 24, 24
 CHUNKS = ((0, 1), (2,), (3,))
 ROW = ("row_0", "row_1")
 TM = ("tm_0", "tm_1")
@@ -63,12 +64,13 @@
     return lax.dot_general(a, b, (((1,), (1,)), ((), ())), preferred_element_type=f32)
 
 
-def first_kernel(residues, movie_ref, high_ref, low_ref, out_ref):
+def first_kernel(residues, movie_ref, high_ref, low_ref, *refs):
+    out_ref = refs[-1]
     parts = [[movie_ref[c, 0, :, q * SUB:(q + 1) * SUB] for q in range(RADIX)] for c in range(2)]
     for j, p in enumerate(residues):
         zr, zi = butterfly(parts[0], parts[1], p)
         zh, zl = split(stacked(zr, zi))
-        th, tl = high_ref[p], low_ref[p]
+        th, tl = high_ref[j], low_ref[j]
         got = nt(th, zh) + nt(tl, zh) + nt(th, zl)
         for c in range(2):
             piece = got[:, c * 128:(c + 1) * 128].reshape(8, 4, 8, 128)
@@ -76,24 +78,28 @@
                 out_ref[y, :, c, j] = piece[:, y]
 
 
-def first_transform(movie, high, low, residues):
+def first_transform(movie, high, low, residues, after):
     count = len(residues)
-    table = pl.BlockSpec((RADIX, SUB, 2 * SUB), lambda f: (0, 0, 0))
+    place = residues[0] // count
+    table = pl.BlockSpec((count, SUB, 2 * SUB), lambda f: (place, 0, 0))
+    order = [pl.BlockSpec(memory_space=pl.ANY)] * len(after)
     return pl.pallas_call(
         functools.partial(first_kernel, residues),
         grid=(OWN,),
-        in_specs=[pl.BlockSpec((2, 1, 128, N), lambda f: (0, f, 0, 0)), table, table],
+        in_specs=[pl.BlockSpec((2, 1, 128, N), lambda f: (0, f, 0, 0)), table, table] + order,
         out_specs=pl.BlockSpec((4, 8, 2, count, 8, 128), lambda f: (0, 0, 0, 0, 0, f)),
         out_shape=jax.ShapeDtypeStruct((4, 8, 2, count, 8, OWN * 128), f32),
-        compiler_params=pltpu.CompilerParams(vmem_limit_bytes=24 << 20),
+        compiler_params=pltpu.CompilerParams(vmem_limit_bytes=(56 if residues[0] == 0 else REST_VMEM) << 20),
         cost_estimate=pl.CostEstimate(
-            flops=count * 6 * 256 * 512 * 1024, bytes_accessed=(4 + count) << 20, transcendentals=0
+            flops=1024, bytes_accessed=1024, transcendentals=0
         ),
         name="first_transform",
-    )(movie, high, low)
-
-
-def second_kernel(count, piece_ref, high_ref, low_ref, early_ref, late_ref):
+    )(movie, high, low, *after)
+
+
+def second_kernel(count, piece_ref, high_ref, low_ref, *refs):
+    early_ref, late_ref, token_ref = refs[-3:]
+    token_ref[...] = jnp.zeros_like(token_ref)
     for j in range(count):
 
         def part(c, q):
@@ -126,23 +132,28 @@
                     ]
 
 
-def second_transform(piece, high, low, count):
+def second_transform(piece, high, low, count, after):
+    vmem = pl.BlockSpec(memory_space=pltpu.VMEM)
     half = jax.ShapeDtypeStruct((2, 2, count, 32, N), f32)
     return pl.pallas_call(
         functools.partial(second_kernel, count),
-        out_shape=(half, half),
-        compiler_params=pltpu.CompilerParams(vmem_limit_bytes=40 << 20),
+        in_specs=[vmem] * 3 + [pl.BlockSpec(memory_space=pl.ANY)] * len(after),
+        out_shape=(half, half, jax.ShapeDtypeStruct((8, 128), f32)),
+        compiler_params=pltpu.CompilerParams(vmem_limit_bytes=SECOND_VMEM << 20),
         cost_estimate=pl.CostEstimate(
-            flops=count * 6 * 256 * 512 * 1024, bytes_accessed=(2 + 2 * count) << 20, transcendentals=0
+            flops=1024, bytes_accessed=1024, transcendentals=0
         ),
         name="second_transform",
-    )(piece, high, low)
+    )(piece, high, low, *after)
 
 
 def lag_kernel(
-    count, final, ends_ref, early_ref, late_ref, right_ref, left_ref, label_ref, before_ref,
-    out_ref, cycle_ref, lags_ref
+    count, carried, final, ends_ref, early_ref, late_ref, right_ref, left_ref, label_ref, before_ref,
+    *refs
 ):
+    out_ref, cycle_ref, lags_ref = refs[-3:]
+    if carried:
+        out_ref[:, count:count + carried] = refs[0][...]
     at_end, at_start = ends_ref[0], ends_ref[1]
     has_right = 1.0 - at_end.astype(f32)
     has_left = 1.0 - at_start.astype(f32)
@@ -212,26 +223,64 @@
     cycle_ref[...] = tile
     if final:
         for m in range(32):
-            out_ref[m, count] = tile
-
-
-def partial_lags(ends, early, late, right, left, labels, before, count, final):
+            out_ref[m, count + carried] = tile
+
+
+def partial_lags(ends, early, late, right, left, labels, before, carry, after, final):
+    count = early.shape[2]
+    carried = sum(c.shape[1] for c in carry)
     vmem = pl.BlockSpec(memory_space=pltpu.VMEM)
     return pl.pallas_call(
-        functools.partial(lag_kernel, count, final),
-        in_specs=[pl.BlockSpec(memory_space=pltpu.SMEM)] + [vmem] * 6,
+        functools.partial(lag_kernel, count, carried, final),
+        in_specs=[pl.BlockSpec(memory_space=pltpu.SMEM)]
+        + [vmem] * (6 + len(carry))
+        + [pl.BlockSpec(memory_space=pl.ANY)] * len(after),
         out_specs=(vmem, vmem),
         out_shape=(
-            jax.ShapeDtypeStruct((32, count + int(final), 8, 128), f32),
+            jax.ShapeDtypeStruct((32, count + carried + int(final), 8, 128), f32),
             jax.ShapeDtypeStruct((8, CYCLES), f32),
         ),
         scratch_shapes=[pltpu.VMEM((128, SUB), f32)],
-        compiler_params=pltpu.CompilerParams(vmem_limit_bytes=24 << 20),
+        compiler_params=pltpu.CompilerParams(vmem_limit_bytes=LAG_VMEM << 20),
         cost_estimate=pl.CostEstimate(
-            flops=count * 64 * 80 * 256 * 128, bytes_accessed=count * 5 << 19, transcendentals=0
+            flops=1024, bytes_accessed=1024, transcendentals=0
         ),
         name="partial_lags",
-    )(ends, early, late, right, left, labels, before)
+    )(ends, early, late, right, left, labels, before, *carry, *after)
+
+
+def settle_kernel(places, *refs):
+    out_ref = refs[-1]
+    lane = lax.broadcasted_iota(jnp.int32, (8, 128), 1)
+    from_lane = (lane % 32) // 4
+    tiles = []
+    for y in range(4):
+        for p in range(RADIX):
+            which, j = places[p]
+            tile = refs[which][8 * y, j]
+            for z in range(1, 8):
+                tile = tile + refs[which][8 * y + z, j]
+            tiles.append((tile, (lane // 32 == y) & (lane % 4 == p)))
+    for q in range(RADIX):
+        for lag in range(LAGS):
+            index = from_lane + (q * 32 + lag * 8)
+            out = jnp.zeros((8, 128), f32)
+            for tile, here in tiles:
+                out = jnp.where(here, jnp.take_along_axis(tile, index, axis=1), out)
+            out_ref[lag, pl.ds(q, 8, stride=4), :] = out
+
+
+def settle(sums_0, sums_1):
+    places = {}
+    for j, p in enumerate(CHUNKS[0]):
+        places[p] = (0, j)
+    for j, p in enumerate(CHUNKS[2] + CHUNKS[1]):
+        places[p] = (1, j)
+    return pl.pallas_call(
+        functools.partial(settle_kernel, places),
+        out_shape=jax.ShapeDtypeStruct((LAGS, 32, 128), f32),
+        name="settle",
+    )(sums_0, sums_1)
 
 
 def body(movie, cycle_label, valid_mask):
@@ -245,39 +294,50 @@
     labels = labels.reshape(SUB, RADIX, 8, RADIX).transpose(3, 1, 2, 0)
     to_left = [(i, (i - 1) % z_count) for i in range(z_count)]
     to_right = [(i, (i + 1) % z_count) for i in range(z_count)]
+    spectra = []
     cycles = jnp.zeros((8, CYCLES), f32)
-    slabs = []
-    done = []
-    for index, residues in enumerate(CHUNKS):
-        count = len(residues)
+
+    def halo(index):
+        early, late, _ = spectra[index]
+        return lax.ppermute(early, "tm_1", to_left), lax.ppermute(late, "tm_1", to_right)
+
+    def lags_of(index, beside, carry, cycles, after):
         final = index == len(CHUNKS) - 1
-        piece = first_transform(movie, high, low, residues)
-        if index >= 2:
-            piece, done[index - 2] = lax.optimization_barrier((piece, done[index - 2]))
-        piece = piece.reshape((32,) + piece.shape[2:])
-        piece = lax.all_to_all(piece, YROW, 0, 0, tiled=True)
-        piece = piece.reshape((4, 8) + piece.shape[1:])
-        early, late = second_transform(piece, high, low, count)
-        done.append((early, late))
-    for index, residues in enumerate(CHUNKS):
-        count = len(residues)
-        final = index == len(CHUNKS) - 1
-        early, late = done[index]
-        right = lax.ppermute(early, "tm_1", to_left)
-        left = lax.ppermute(late, "tm_1", to_right)
-        part, cycles = partial_lags(
-            ends, early, late, right, left, labels[residues[0]:residues[-1] + 1], cycles, count, final
-        )
-        part = lax.all_to_all(part, TM, 0, 0, tiled=True)
-        if final:
-            cycles = jnp.sum(part[:, count], axis=0)
-        slabs.append(jnp.sum(part[:, :count].reshape(4, 8, count, 8, 128), axis=1))
-    slab = jnp.concatenate(slabs, axis=1).reshape(4, RADIX, 8, RADIX, LAGS, 8)
-    image_structure = jnp.transpose(slab, (4, 2, 3, 0, 5, 1)).reshape(LAGS, 32, 128)
+        early, late, _ = spectra[index]
+        residues = CHUNKS[index]
+        chosen = labels[residues[0]:residues[-1] + 1]
+        return partial_lags(ends, early, late, *beside, chosen, cycles, carry, after, final)
+
+    def transform_rows(index, after):
+        return first_transform(movie, high, low, CHUNKS[index], after)
+
+    def exchange(piece):
+        piece = lax.all_to_all(piece.reshape((32,) + piece.shape[2:]), YROW, 0, 0, tiled=True)
+        return piece.reshape((4, 8) + piece.shape[1:])
+
+    def transform_columns(piece, index, after):
+        spectra.append(second_transform(piece, high, low, len(CHUNKS[index]), after))
+
+    piece = exchange(transform_rows(0, []))
+    piece_1 = exchange(transform_rows(1, [labels]))
+    transform_columns(piece, 0, [])
+    halo_0 = halo(0)
+    piece_2 = exchange(transform_rows(2, [spectra[0][2]]))
+    transform_columns(piece_1, 1, [])
+    halo_1 = halo(1)
+    part_0, cycles = lags_of(0, halo_0, [], cycles, [spectra[1][2]])
+    transform_columns(piece_2, 2, [cycles])
+    halo_2 = halo(2)
+    sums_0 = lax.all_to_all(part_0, TM, 0, 0, tiled=True)
+    part_1, cycles = lags_of(1, halo_1, [], cycles, [spectra[2][2]])
+    part_2, _ = lags_of(2, halo_2, [part_1], cycles, [])
+    part_2, sums_0 = lax.optimization_barrier((part_2, sums_0))
+    sums_1 = lax.all_to_all(part_2, TM, 0, 0, tiled=True)
+    cycles = jnp.sum(sums_1[:, -1], axis=0)
     copies = jnp.broadcast_to(cycles[None], (8,) + cycles.shape)
-    sums = jnp.sum(lax.all_to_all(copies, ROW, 0, 0, tiled=True), axis=0)
-    cycle_curve = sums[:LAGS] / jnp.maximum(sums[LAGS], 1.0)[None, :]
-    return (cycle_curve, image_structure)
+    cycles = jnp.sum(lax.all_to_all(copies, ROW, 0, 0, tiled=True), axis=0)
+    cycle_curve = cycles[:LAGS] / jnp.maximum(cycles[LAGS], 1.0)[None, :]
+    return (cycle_curve, settle(sums_0, sums_1))
 
 
 def solution(mesh):

time: 173 us -> 148 us (0.86)
  local copies, waits for them, and re-layouts: 28.2 us -> 8.09 us
  waiting for transfers between devices: 52.1 us -> 33.3 us
  blocking collectives: 0 us -> 18.2 us
  starting transfers between devices: 58.6 us -> 47.2 us
  Pallas kernels: 28.6 us -> 39 us
  other arithmetic: 3.38 us -> 1.05 us
    all_to_all x7 -> x5, waiting for transfers between devices: 41.1 us -> 19.4 us  [the longest x3 16.8 us: exchange(): lax.all_to_all(piece.reshape((32,) + piece.shape[2:]), YROW, 0, 0, tiled=...]
    all_to_all x0 -> x1, blocking collectives: none -> 18.2 us  [body(): sums_1 = lax.all_to_all(part_2, TM, 0, 0, tiled=True)]
    unnamed x22 -> x18, local copies, waits for them, and re-layouts: 13.5 us -> 0.62 us
    all_to_all x7 -> x5, starting transfers between devices: 47.1 us -> 35 us  [the longest x3 21.4 us: exchange(): lax.all_to_all(piece.reshape((32,) + piece.shape[2:]), YROW, 0, 0, tiled=...]
    pallas_call x3, Pallas kernels: 8.11 us -> 16.1 us  [first_transform(): pl.pallas_call(functools.partial(first_kernel, residues), grid=(OWN,), in...]
    transpose x1 -> x0, local copies, waits for them, and re-layouts: 3.2 us -> none  [body(): jnp.transpose(slab, (4, 2, 3, 0, 5, 1)).reshape(LAGS, 32, 128)]
    ppermute x6, waiting for transfers between devices: 10.9 us -> 13.9 us  [the longest x3 9.48 us: halo(): lax.ppermute(early, 'tm_1', to_left)]
    pallas_call x6 -> x7, Pallas kernels: 20.5 us -> 22.9 us  [the longest x3 10.7 us: partial_lags(): pl.pallas_call(functools.partial(lag_kernel, count, carried, final), in_s...]
  transfers between devices with their start and end apart: 13 -> 11, of which waited for: 10 -> 7; matrix products, arithmetic and copies ran while one was open for 10% -> 5% of each run, Pallas kernels for 15% -> 22%
where the time goes in v2:
time: 148 us
  starting transfers between devices  47.2 us (32%)
  Pallas kernels  39 us (26%)
  waiting for transfers between devices  33.3 us (22%)
  blocking collectives  18.2 us (12%)
  local copies, waits for them, and re-layouts  8.09 us (5%)
    all_to_all x3, starting transfers between devices, exchange(): lax.all_to_all(piece.reshape((32,) + piece.shape[2:]), YROW, 0, 0, tiled=...  21.4 us
    all_to_all x1, blocking collectives, body(): sums_1 = lax.all_to_all(part_2, TM, 0, 0, tiled=True)  18.2 us
    all_to_all x3, waiting for transfers between devices, exchange(): lax.all_to_all(piece.reshape((32,) + piece.shape[2:]), YROW, 0, 0, tiled=...  16.8 us
    pallas_call x3, Pallas kernels, first_transform(): pl.pallas_call(functools.partial(first_kernel, residues), grid=(OWN,), in...  16.1 us
    ppermute x3, starting transfers between devices, halo(): lax.ppermute(early, 'tm_1', to_left)  12.2 us
    pallas_call x3, Pallas kernels, partial_lags(): pl.pallas_call(functools.partial(lag_kernel, count, carried, final), in_s...  10.7 us
    pallas_call x3, Pallas kernels, second_transform(): pl.pallas_call(functools.partial(second_kernel, count), in_specs=[vmem] *...  10.1 us
    ppermute x3, waiting for transfers between devices, halo(): lax.ppermute(early, 'tm_1', to_left)  9.48 us
  transfers between devices with their start and end apart: 11, of which 7 were waited for; matrix products, arithmetic and copies ran while one was open for 5% of the time, Pallas kernels for 22%

profile of v2, /device:TPU:1, one launch (start us, length us, event | category | flops | bytes accessed | tf_op | source)
XLA Modules:
  0.0 147.6 jit_solution(1970691763694754403)
XLA Ops:
  0.6 5.8 %first_transform.3 = f32[4,8,2,2,8,512]{5,4,3,2,1,0:T(8,128)} custom-call(f32[2,4,128,1024]{3,2,1,0:T(8,128)} %movie_ref.5, bf16[4,256,512]{2,1,0:T(8,128)(2,1)} %constant.31.clone.high_ref, bf16[4,256,512]{2,1,0:T(8,128)(2,1)} %constant.32.clone.low_ref), custom_call_target="tpu_custom_call" | custom-call | flops 1024 | bytes 1024 | tf_op jit(solution)/shard_map/first_transform/pallas_call | solution.py:86
  6.4 0.0 copy-start.7
  6.4 0.0 copy-start.8
  6.4 8.8 %all-to-all-start = ((f32[32,2,2,8,512]{4,3,2,1,0:T(8,128)}), f32[32,2,2,8,512]{4,3,2,1,0:T(8,128)}, u32[]{:S(2)}, u32[]{:S(2)}) async-start(f32[32,2,2,8,512]{4,3,2,1,0:T(8,128)} %bitcast.16), calls=%async_computation | async-start | bytes 4194304 | tf_op jit(solution)/shard_map/all_to_all | solution.py:315
  15.2 0.0 copy-done.7
  15.2 0.0 copy-done.8
  15.2 0.3 dynamic-slice_select_fusion
  15.6 2.6 %reshape.33 = s32[256,4,8,4]{3,2,1,0:T(8,128)} reshape(s32[1024,32]{1,0:T(8,128)S(1)} %dynamic-slice_select_fusion) | data formatting | bytes 262144 | tf_op jit(solution)/shard_map/reshape | solution.py:294
  18.1 4.2 %copy.15 = s32[256,4,8,4]{0,2,1,3:T(8,128)} copy(s32[256,4,8,4]{3,2,1,0:T(8,128)} %reshape.33) | data formatting | bytes 262144 | tf_op jit(solution)/shard_map/reshape | solution.py:294
  22.4 0.0 copy-start
  22.4 0.0 copy-start.2
  22.4 5.1 %first_transform.5 = f32[4,8,2,1,8,512]{5,4,3,2,1,0:T(8,128)} custom-call(f32[2,4,128,1024]{3,2,1,0:T(8,128)} %movie_ref.5, bf16[4,256,512]{2,1,0:T(8,128)(2,1)} %constant.31.clone.high_ref, bf16[4,256,512]{2,1,0:T(8,128)(2,1)} %constant.32.clone.low_ref, s32[4,4,8,256]{3,2,1,0:T(8,128)} %bitcast.19), custom_call_target="tpu_custom_call" | custom-call | flops 1024 | bytes 1024 | tf_op jit(solution)/shard_map/first_transform/pallas_call | solution.py:86
  27.5 15.6 %all-to-all-done = f32[32,2,2,8,512]{4,3,2,1,0:T(8,128)} async-done(((f32[32,2,2,8,512]{4,3,2,1,0:T(8,128)}), f32[32,2,2,8,512]{4,3,2,1,0:T(8,128)}, u32[]{:S(2)}, u32[]{:S(2)}) %all-to-all-start) | async-done | bytes 2097184 | tf_op jit(solution)/shard_map/all_to_all | solution.py:315
  43.1 6.0 %all-to-all-start.2 = ((f32[32,2,1,8,512]{4,3,1,2,0:T(8,128)}), f32[32,2,1,8,512]{4,3,1,2,0:T(8,128)S(1)}, u32[]{:S(2)}, u32[]{:S(2)}) async-start(f32[32,2,1,8,512]{4,3,1,2,0:T(8,128)} %bitcast.18), calls=%async_computation.2 | async-start | bytes 2097152 | tf_op jit(solution)/shard_map/all_to_all | solution.py:315
  49.1 0.0 copy-done
  49.1 0.0 copy-done.2
  49.1 4.8 %second_transform.3 = (f32[2,2,2,32,1024]{4,3,2,1,0:T(8,128)}, f32[2,2,2,32,1024]{4,3,2,1,0:T(8,128)}, f32[8,128]{1,0:T(8,128)S(1)}) custom-call(f32[4,8,2,2,8,512]{5,4,3,2,1,0:T(8,128)} %bitcast.3.piece_ref, bf16[4,256,512]{2,1,0:T(8,128)(2,1)S(1)} %copy-done, bf16[4,256,512]{2,1,0:T(8,128)(2,1)S(1)} %copy-done.2), custom_call_target="tpu_custom_call" | custom-call | flops 1024 | bytes 1024 | tf_op jit(solution)/shard_map/second_transform/pallas_call | solution.py:138
  53.9 0.0 copy-start.4
  53.9 0.6 copy-done.4
  54.5 5.6 %collective-permute-start = (f32[2,2,2,32,1024]{4,3,2,1,0:T(8,128)}, f32[2,2,2,32,1024]{4,3,2,1,0:T(8,128)}, u32[]{:S(2)}, u32[]{:S(2)}) collective-permute-start(f32[2,2,2,32,1024]{4,3,2,1,0:T(8,128)} %get-tuple-element.19.early_ref), channel_id=1, source_target_pairs={{0,56},{8,0},{16,8},{24,16},{32,24},{40,32},{48,40},{56,48},{1,57}... | collective-permute-start | bytes 3145736 | tf_op jit(solution)/shard_map/ppermute | solution.py:302
  60.1 0.0 collective-permute-start.1
  60.1 0.0 copy-start.6
  60.1 0.0 copy-start.1
  60.1 0.0 copy-start.3
  60.1 5.1 %first_transform.4 = f32[4,8,2,1,8,512]{5,4,3,2,1,0:T(8,128)} custom-call(f32[2,4,128,1024]{3,2,1,0:T(8,128)} %movie_ref.5, bf16[4,256,512]{2,1,0:T(8,128)(2,1)} %constant.31.clone.high_ref, bf16[4,256,512]{2,1,0:T(8,128)(2,1)} %constant.32.clone.low_ref, f32[8,128]{1,0:T(8,128)} %copy-done.4), custom_call_target="tpu_custom_call" | custom-call | flops 1024 | bytes 1024 | tf_op jit(solution)/shard_map/first_transform/pallas_call | solution.py:86
  65.2 1.1 all-to-all-done.2
  66.4 6.7 %all-to-all-start.1 = ((f32[32,2,1,8,512]{4,3,1,2,0:T(8,128)}), f32[32,2,1,8,512]{4,3,1,2,0:T(8,128)}, u32[]{:S(2)}, u32[]{:S(2)}) async-start(f32[32,2,1,8,512]{4,3,1,2,0:T(8,128)} %bitcast.17), calls=%async_computation.1 | async-start | bytes 2097152 | tf_op jit(solution)/shard_map/all_to_all | solution.py:315
  73.1 0.0 copy-done.6
  73.1 0.1 add_convert_fusion.ends_ref
  73.2 0.0 copy-done.1
  73.2 0.0 copy-done.3
  73.2 2.0 %second_transform.4 = (f32[2,2,1,32,1024]{4,3,2,1,0:T(8,128)}, f32[2,2,1,32,1024]{4,3,2,1,0:T(8,128)}, f32[8,128]{1,0:T(8,128)S(1)}) custom-call(f32[4,8,2,1,8,512]{5,4,3,2,1,0:T(8,128)S(1)} %bitcast.15, bf16[4,256,512]{2,1,0:T(8,128)(2,1)S(1)} %copy-done.1, bf16[4,256,512]{2,1,0:T(8,128)(2,1)S(1)} %copy-done.3), custom_call_target="tpu_custom_call" | custom-call | flops 1024 | bytes 1024 | tf_op jit(solution)/shard_map/second_transform/pallas_call | solution.py:138
  75.2 3.5 %collective-permute-start.4 = (f32[2,2,1,32,1024]{4,3,2,1,0:T(8,128)}, f32[2,2,1,32,1024]{4,3,2,1,0:T(8,128)S(1)}, u32[]{:S(2)}, u32[]{:S(2)}) collective-permute-start(f32[2,2,1,32,1024]{4,3,2,1,0:T(8,128)} %get-tuple-element.25.early_ref), channel_id=1, source_target_pairs={{0,56},{8,0},{16,8},{24,16},{32,24},{40,32},{48,40},{56,48},{1,57}... | collective-permute-start | bytes 1572872 | tf_op jit(solution)/shard_map/ppermute | solution.py:302
  78.8 0.0 collective-permute-start.5
  78.8 3.8 %collective-permute-done.right_ref = f32[2,2,2,32,1024]{4,3,2,1,0:T(8,128)} collective-permute-done((f32[2,2,2,32,1024]{4,3,2,1,0:T(8,128)}, f32[2,2,2,32,1024]{4,3,2,1,0:T(8,128)}, u32[]{:S(2)}, u32[]{:S(2)}) %collective-permute-start) | collective-permute-done | bytes 1048608 | tf_op jit(solution)/shard_map/ppermute | solution.py:302
  82.6 3.1 %collective-permute-done.1.left_ref = f32[2,2,2,32,1024]{4,3,2,1,0:T(8,128)} collective-permute-done((f32[2,2,2,32,1024]{4,3,2,1,0:T(8,128)}, f32[2,2,2,32,1024]{4,3,2,1,0:T(8,128)}, u32[]{:S(2)}, u32[]{:S(2)}) %collective-permute-start.1) | collective-permute-done | bytes 1048608 | tf_op jit(solution)/shard_map/ppermute | solution.py:302
  85.7 5.1 %partial_lags.3 = (f32[32,2,8,128]{3,2,1,0:T(8,128)}, f32[8,128]{1,0:T(8,128)S(1)}) custom-call(s32[2]{0:T(128)S(1)} %add_convert_fusion.ends_ref, f32[2,2,2,32,1024]{4,3,2,1,0:T(8,128)} %get-tuple-element.19.early_ref, f32[2,2,2,32,1024]{4,3,2,1,0:T(8,128)} %get-tuple-element.20.late_ref, f32[2,2,2,32,1024]{4,3,2,1,0:T(8,128)} %collective-permute-done.right_ref, ...), custom_call_target="tpu_custom_call" | custom-call | flops 1024 | bytes 1024 | tf_op jit(solution)/shard_map/partial_lags/pallas_call | solution.py:233
  90.8 0.0 all-to-all-done.1
  90.8 3.3 %second_transform.5 = (f32[2,2,1,32,1024]{4,3,2,1,0:T(8,128)}, f32[2,2,1,32,1024]{4,3,2,1,0:T(8,128)}, f32[8,128]{1,0:T(8,128)S(1)}) custom-call(f32[4,8,2,1,8,512]{5,4,3,2,1,0:T(8,128)} %bitcast.6.piece_ref, bf16[4,256,512]{2,1,0:T(8,128)(2,1)S(1)} %copy-done.1, bf16[4,256,512]{2,1,0:T(8,128)(2,1)S(1)} %copy-done.3, ...), custom_call_target="tpu_custom_call" | custom-call | flops 1024 | bytes 1024 | tf_op jit(solution)/shard_map/second_transform/pallas_call | solution.py:138
  94.1 3.1 %collective-permute-start.2 = (f32[2,2,1,32,1024]{4,3,2,1,0:T(8,128)}, f32[2,2,1,32,1024]{4,3,2,1,0:T(8,128)S(1)}, u32[]{:S(2)}, u32[]{:S(2)}) collective-permute-start(f32[2,2,1,32,1024]{4,3,2,1,0:T(8,128)} %get-tuple-element.23.early_ref), channel_id=1, source_target_pairs={{0,56},{8,0},{16,8},{24,16},{32,24},{40,32},{48,40},{56,48},{1,57}... | collective-permute-start | bytes 1572872 | tf_op jit(solution)/shard_map/ppermute | solution.py:302
  97.2 0.0 collective-permute-start.3
  97.2 5.3 %all-to-all-start.3 = ((f32[32,2,8,128]{3,2,1,0:T(8,128)}), f32[32,2,8,128]{3,2,1,0:T(8,128)}, u32[]{:S(2)}, u32[]{:S(2)}) async-start(f32[32,2,8,128]{3,2,1,0:T(8,128)} %get-tuple-element.31), calls=%async_computation.3 | async-start | bytes 524288 | tf_op jit(solution)/shard_map/all_to_all | solution.py:331
  102.6 0.0 collective-permute-done.4.right_ref
  102.6 0.0 collective-permute-done.5.left_ref
  102.6 2.5 %partial_lags.4 = (f32[32,1,8,128]{3,2,1,0:T(8,128)S(1)}, f32[8,128]{1,0:T(8,128)S(1)}) custom-call(s32[2]{0:T(128)S(1)} %add_convert_fusion.ends_ref, f32[2,2,1,32,1024]{4,3,2,1,0:T(8,128)} %get-tuple-element.25.early_ref, f32[2,2,1,32,1024]{4,3,2,1,0:T(8,128)} %get-tuple-element.26.late_ref, f32[2,2,1,32,1024]{4,3,2,1,0:T(8,128)S(1)} %collective-permute-done.4.right_ref, ...), custom_call_target="tpu_custom_call" | custom-call | flops 1024 | bytes 1024 | tf_op jit(solution)/shard_map/partial_lags/pallas_call | solution.py:233
  105.1 5.6 %collective-permute-done.2.right_ref = f32[2,2,1,32,1024]{4,3,2,1,0:T(8,128)S(1)} collective-permute-done((f32[2,2,1,32,1024]{4,3,2,1,0:T(8,128)}, f32[2,2,1,32,1024]{4,3,2,1,0:T(8,128)S(1)}, u32[]{:S(2)}, u32[]{:S(2)}) %collective-permute-start.2) | collective-permute-done | bytes 524320 | tf_op jit(solution)/shard_map/ppermute | solution.py:302
  110.7 1.3 collective-permute-done.3.left_ref
  112.0 3.1 %partial_lags.5 = (f32[32,3,8,128]{3,2,1,0:T(8,128)S(1)}, f32[8,128]{1,0:T(8,128)}) custom-call(s32[2]{0:T(128)S(1)} %add_convert_fusion.ends_ref, f32[2,2,1,32,1024]{4,3,2,1,0:T(8,128)} %get-tuple-element.23.early_ref, f32[2,2,1,32,1024]{4,3,2,1,0:T(8,128)} %get-tuple-element.24.late_ref, f32[2,2,1,32,1024]{4,3,2,1,0:T(8,128)S(1)} %collective-permute-done.2.right_ref, ...), custom_call_target="tpu_custom_call" | custom-call | flops 1024 | bytes 1024 | tf_op jit(solution)/shard_map/partial_lags/pallas_call | solution.py:233
  115.1 0.0 all-to-all-done.3.refs_0_
  115.1 18.2 %all_to_all.30.refs_1_ = f32[32,3,8,128]{3,2,1,0:T(8,128)S(1)} all-to-all(f32[32,3,8,128]{3,2,1,0:T(8,128)S(1)} %get-tuple-element.32), channel_id=1, replica_groups=mesh['tm_0'=4,'tm_1'=8,'row_0'=4,'row_1'=2] {'tm_0','tm_1'}, dimensions={0} | all-to-all | bytes 786432 | tf_op jit(solution)/shard_map/all_to_all | solution.py:335
  133.3 0.0 copy-start.5
  133.4 0.7 broadcast_in_dim.16
  134.1 8.2 %all-to-all-start.5 = ((f32[8,8,128]{2,1,0:T(8,128)}), f32[8,8,128]{2,1,0:T(8,128)S(1)}, u32[]{:S(2)}, u32[]{:S(2)}) async-start(f32[8,8,128]{2,1,0:T(8,128)} %broadcast_in_dim.16), calls=%async_computation.5 | async-start | bytes 65536 | tf_op jit(solution)/shard_map/all_to_all | solution.py:338
  142.3 0.0 copy-done.5
  142.3 2.1 %settle.1 = f32[4,32,128]{2,1,0:T(8,128)} custom-call(f32[32,2,8,128]{3,2,1,0:T(8,128)} %all-to-all-done.3.refs_0_, f32[32,3,8,128]{3,2,1,0:T(8,128)} %copy-done.5), custom_call_target="tpu_custom_call" | custom-call | tf_op jit(solution)/shard_map/settle/pallas_call | solution.py:279
  144.4 2.6 %all-to-all-done.5 = f32[8,8,128]{2,1,0:T(8,128)S(1)} async-done(((f32[8,8,128]{2,1,0:T(8,128)}), f32[8,8,128]{2,1,0:T(8,128)S(1)}, u32[]{:S(2)}, u32[]{:S(2)}) %all-to-all-start.5) | async-done | bytes 32800 | tf_op jit(solution)/shard_map/all_to_all | solution.py:338
  147.0 0.6 slice_divide_fusion
  (6 shorter events, 0.1 us)
Async XLA Ops:
  6.4 8.8 %copy-start.7 = (s32[1024,128]{1,0:T(8,128)S(1)}, s32[1024,128]{1,0:T(8,128)}, u32[]{:S(2)}) copy-start(s32[1024,128]{1,0:T(8,128)} %param.6) | copy-start | bytes 1572868
  6.4 8.8 %copy-start.8 = (s32[1024,128]{1,0:T(8,128)S(1)}, s32[1024,128]{1,0:T(8,128)}, u32[]{:S(2)}) copy-start(s32[1024,128]{1,0:T(8,128)} %param.7) | copy-start | bytes 1572868
  6.4 36.7 %all-to-all-start = ((f32[32,2,2,8,512]{4,3,2,1,0:T(8,128)}), f32[32,2,2,8,512]{4,3,2,1,0:T(8,128)}, u32[]{:S(2)}, u32[]{:S(2)}) async-start(f32[32,2,2,8,512]{4,3,2,1,0:T(8,128)} %bitcast.16), calls=%async_computation | async-start | bytes 4194304 | tf_op jit(solution)/shard_map/all_to_all | solution.py:315
  22.4 26.7 %copy-start = (bf16[4,256,512]{2,1,0:T(8,128)(2,1)S(1)}, bf16[4,256,512]{2,1,0:T(8,128)(2,1)}, u32[]{:S(2)}) copy-start(bf16[4,256,512]{2,1,0:T(8,128)(2,1)} %constant.31.clone.high_ref) | copy-start | bytes 3145732
  22.4 26.7 %copy-start.2 = (bf16[4,256,512]{2,1,0:T(8,128)(2,1)S(1)}, bf16[4,256,512]{2,1,0:T(8,128)(2,1)}, u32[]{:S(2)}) copy-start(bf16[4,256,512]{2,1,0:T(8,128)(2,1)} %constant.32.clone.low_ref) | copy-start | bytes 3145732
  43.1 23.3 %all-to-all-start.2 = ((f32[32,2,1,8,512]{4,3,1,2,0:T(8,128)}), f32[32,2,1,8,512]{4,3,1,2,0:T(8,128)S(1)}, u32[]{:S(2)}, u32[]{:S(2)}) async-start(f32[32,2,1,8,512]{4,3,1,2,0:T(8,128)} %bitcast.18), calls=%async_computation.2 | async-start | bytes 2097152 | tf_op jit(solution)/shard_map/all_to_all | solution.py:315
  53.9 0.6 copy-start.4
  54.5 28.1 %collective-permute-start = (f32[2,2,2,32,1024]{4,3,2,1,0:T(8,128)}, f32[2,2,2,32,1024]{4,3,2,1,0:T(8,128)}, u32[]{:S(2)}, u32[]{:S(2)}) collective-permute-start(f32[2,2,2,32,1024]{4,3,2,1,0:T(8,128)} %get-tuple-element.19.early_ref), channel_id=1, source_target_pairs={{0,56},{8,0},{16,8},{24,16},{32,24},{40,32},{48,40},{56,48},{1,57}... | collective-permute-start | bytes 3145736 | tf_op jit(solution)/shard_map/ppermute | solution.py:302
  60.1 25.6 %collective-permute-start.1 = (f32[2,2,2,32,1024]{4,3,2,1,0:T(8,128)}, f32[2,2,2,32,1024]{4,3,2,1,0:T(8,128)}, u32[]{:S(2)}, u32[]{:S(2)}) collective-permute-start(f32[2,2,2,32,1024]{4,3,2,1,0:T(8,128)} %get-tuple-element.20.late_ref), channel_id=1, source_target_pairs={{0,8},{8,16},{16,24},{24,32},{32,40},{40,48},{48,56},{56,0},{1,9},... | collective-permute-start | bytes 3145736 | tf_op jit(solution)/shard_map/ppermute | solution.py:302
  60.1 13.0 %copy-start.6 = (s32[256,4,8,4]{0,2,1,3:T(8,128)S(1)}, s32[256,4,8,4]{0,2,1,3:T(8,128)}, u32[]{:S(2)}) copy-start(s32[256,4,8,4]{0,2,1,3:T(8,128)} %copy.15) | copy-start | bytes 393220
  60.1 13.1 %copy-start.1 = (bf16[4,256,512]{2,1,0:T(8,128)(2,1)S(1)}, bf16[4,256,512]{2,1,0:T(8,128)(2,1)}, u32[]{:S(2)}) copy-start(bf16[4,256,512]{2,1,0:T(8,128)(2,1)} %constant.31.clone.high_ref) | copy-start | bytes 3145732
  60.1 13.1 %copy-start.3 = (bf16[4,256,512]{2,1,0:T(8,128)(2,1)S(1)}, bf16[4,256,512]{2,1,0:T(8,128)(2,1)}, u32[]{:S(2)}) copy-start(bf16[4,256,512]{2,1,0:T(8,128)(2,1)} %constant.32.clone.low_ref) | copy-start | bytes 3145732
  66.4 24.4 %all-to-all-start.1 = ((f32[32,2,1,8,512]{4,3,1,2,0:T(8,128)}), f32[32,2,1,8,512]{4,3,1,2,0:T(8,128)}, u32[]{:S(2)}, u32[]{:S(2)}) async-start(f32[32,2,1,8,512]{4,3,1,2,0:T(8,128)} %bitcast.17), calls=%async_computation.1 | async-start | bytes 2097152 | tf_op jit(solution)/shard_map/all_to_all | solution.py:315
  75.2 27.3 %collective-permute-start.4 = (f32[2,2,1,32,1024]{4,3,2,1,0:T(8,128)}, f32[2,2,1,32,1024]{4,3,2,1,0:T(8,128)S(1)}, u32[]{:S(2)}, u32[]{:S(2)}) collective-permute-start(f32[2,2,1,32,1024]{4,3,2,1,0:T(8,128)} %get-tuple-element.25.early_ref), channel_id=1, source_target_pairs={{0,56},{8,0},{16,8},{24,16},{32,24},{40,32},{48,40},{56,48},{1,57}... | collective-permute-start | bytes 1572872 | tf_op jit(solution)/shard_map/ppermute | solution.py:302
  78.8 23.8 %collective-permute-start.5 = (f32[2,2,1,32,1024]{4,3,2,1,0:T(8,128)}, f32[2,2,1,32,1024]{4,3,2,1,0:T(8,128)S(1)}, u32[]{:S(2)}, u32[]{:S(2)}) collective-permute-start(f32[2,2,1,32,1024]{4,3,2,1,0:T(8,128)} %get-tuple-element.26.late_ref), channel_id=1, source_target_pairs={{0,8},{8,16},{16,24},{24,32},{32,40},{40,48},{48,56},{56,0},{1,9},... | collective-permute-start | bytes 1572872 | tf_op jit(solution)/shard_map/ppermute | solution.py:302
  94.1 16.6 %collective-permute-start.2 = (f32[2,2,1,32,1024]{4,3,2,1,0:T(8,128)}, f32[2,2,1,32,1024]{4,3,2,1,0:T(8,128)S(1)}, u32[]{:S(2)}, u32[]{:S(2)}) collective-permute-start(f32[2,2,1,32,1024]{4,3,2,1,0:T(8,128)} %get-tuple-element.23.early_ref), channel_id=1, source_target_pairs={{0,56},{8,0},{16,8},{24,16},{32,24},{40,32},{48,40},{56,48},{1,57}... | collective-permute-start | bytes 1572872 | tf_op jit(solution)/shard_map/ppermute | solution.py:302
  97.2 14.8 %collective-permute-start.3 = (f32[2,2,1,32,1024]{4,3,2,1,0:T(8,128)}, f32[2,2,1,32,1024]{4,3,2,1,0:T(8,128)S(1)}, u32[]{:S(2)}, u32[]{:S(2)}) collective-permute-start(f32[2,2,1,32,1024]{4,3,2,1,0:T(8,128)} %get-tuple-element.24.late_ref), channel_id=1, source_target_pairs={{0,8},{8,16},{16,24},{24,32},{32,40},{40,48},{48,56},{56,0},{1,9},... | collective-permute-start | bytes 1572872 | tf_op jit(solution)/shard_map/ppermute | solution.py:302
  97.2 17.9 %all-to-all-start.3 = ((f32[32,2,8,128]{3,2,1,0:T(8,128)}), f32[32,2,8,128]{3,2,1,0:T(8,128)}, u32[]{:S(2)}, u32[]{:S(2)}) async-start(f32[32,2,8,128]{3,2,1,0:T(8,128)} %get-tuple-element.31), calls=%async_computation.3 | async-start | bytes 524288 | tf_op jit(solution)/shard_map/all_to_all | solution.py:331
  133.3 8.9 %copy-start.5 = (f32[32,3,8,128]{3,2,1,0:T(8,128)}, f32[32,3,8,128]{3,2,1,0:T(8,128)S(1)}, u32[]{:S(2)}) copy-start(f32[32,3,8,128]{3,2,1,0:T(8,128)S(1)} %all_to_all.30.refs_1_) | copy-start | bytes 1179652
  134.1 12.9 %all-to-all-start.5 = ((f32[8,8,128]{2,1,0:T(8,128)}), f32[8,8,128]{2,1,0:T(8,128)S(1)}, u32[]{:S(2)}, u32[]{:S(2)}) async-start(f32[8,8,128]{2,1,0:T(8,128)} %broadcast_in_dim.16), calls=%async_computation.5 | async-start | bytes 65536 | tf_op jit(solution)/shard_map/all_to_all | solution.py:338

commit v3 on v2

--- a/solution.py
+++ b/solution.py
@@ -18,7 +18,7 @@
 RADIX = 4
 SUB = N // RADIX
 OWN = 4
-REST_VMEM, SECOND_VMEM, LAG_VMEM = 56, 24, 24
+REST_VMEM, SECOND_VMEM, LAG_VMEM = 56, 16, 16
 CHUNKS = ((0, 1), (2,), (3,))
 ROW = ("row_0", "row_1")
 TM = ("tm_0", "tm_1")
@@ -133,16 +133,26 @@
 
 
 def second_transform(piece, high, low, count, after):
-    vmem = pl.BlockSpec(memory_space=pltpu.VMEM)
-    half = jax.ShapeDtypeStruct((2, 2, count, 32, N), f32)
+    whole = (2, 2, count, 32, N)
+    table = pl.BlockSpec((RADIX, SUB, 2 * SUB), lambda j: (0, 0, 0))
+    out = pl.BlockSpec((2, 2, 1, 32, N), lambda j: (0, 0, j, 0, 0))
     return pl.pallas_call(
-        functools.partial(second_kernel, count),
-        in_specs=[vmem] * 3 + [pl.BlockSpec(memory_space=pl.ANY)] * len(after),
-        out_shape=(half, half, jax.ShapeDtypeStruct((8, 128), f32)),
+        functools.partial(second_kernel, 1),
+        grid=(count,),
+        in_specs=[
+            pl.BlockSpec((4, 8, 2, 1, 8, OWN * 128), lambda j: (0, 0, 0, j, 0, 0)),
+            table,
+            table,
+        ]
+        + [pl.BlockSpec(memory_space=pl.ANY)] * len(after),
+        out_specs=(out, out, pl.BlockSpec((8, 128), lambda j: (0, 0))),
+        out_shape=(
+            jax.ShapeDtypeStruct(whole, f32),
+            jax.ShapeDtypeStruct(whole, f32),
+            jax.ShapeDtypeStruct((8, 128), f32),
+        ),
         compiler_params=pltpu.CompilerParams(vmem_limit_bytes=SECOND_VMEM << 20),
-        cost_estimate=pl.CostEstimate(
-            flops=1024, bytes_accessed=1024, transcendentals=0
-        ),
+        cost_estimate=pl.CostEstimate(flops=1024, bytes_accessed=1024, transcendentals=0),
         name="second_transform",
     )(piece, high, low, *after)
 

time: 148 us -> 148 us (level)
  no operation moved by 1% of the time
where the time goes in v3:
time: 148 us
  starting transfers between devices  47.6 us (32%)
  Pallas kernels  38.5 us (26%)
  waiting for transfers between devices  33.3 us (22%)
  blocking collectives  18.2 us (12%)
  local copies, waits for them, and re-layouts  8.09 us (5%)
    all_to_all x3, starting transfers between devices, exchange(): lax.all_to_all(piece.reshape((32,) + piece.shape[2:]), YROW, 0, 0, tiled=...  21 us
    all_to_all x1, blocking collectives, body(): sums_1 = lax.all_to_all(part_2, TM, 0, 0, tiled=True)  18.2 us
    all_to_all x3, waiting for transfers between devices, exchange(): lax.all_to_all(piece.reshape((32,) + piece.shape[2:]), YROW, 0, 0, tiled=...  17.2 us
    pallas_call x3, Pallas kernels, first_transform(): pl.pallas_call(functools.partial(first_kernel, residues), grid=(OWN,), in...  16 us
    ppermute x3, starting transfers between devices, halo(): lax.ppermute(early, 'tm_1', to_left)  13.1 us
    pallas_call x3, Pallas kernels, partial_lags(): pl.pallas_call(functools.partial(lag_kernel, count, carried, final), in_s...  10.7 us
    pallas_call x3, Pallas kernels, second_transform(): pl.pallas_call(functools.partial(second_kernel, 1), grid=(count,), in_spe...  9.67 us
    ppermute x3, waiting for transfers between devices, halo(): lax.ppermute(early, 'tm_1', to_left)  9.03 us
  transfers between devices with their start and end apart: 11, of which 7 were waited for; matrix products, arithmetic and copies ran while one was open for 5% of the time, Pallas kernels for 22%

profile of v3, /device:TPU:1, one launch (start us, length us, event | category | flops | bytes accessed | tf_op | source)
XLA Modules:
  0.0 147.6 jit_solution(6316392916755175569)
XLA Ops:
  0.6 5.8 %first_transform.3 = f32[4,8,2,2,8,512]{5,4,3,2,1,0:T(8,128)} custom-call(f32[2,4,128,1024]{3,2,1,0:T(8,128)} %movie_ref.5, bf16[4,256,512]{2,1,0:T(8,128)(2,1)} %constant.31.clone.high_ref, bf16[4,256,512]{2,1,0:T(8,128)(2,1)} %constant.32.clone.low_ref), custom_call_target="tpu_custom_call" | custom-call | flops 1024 | bytes 1024 | tf_op jit(solution)/shard_map/first_transform/pallas_call | solution.py:86
  6.4 0.0 copy-start.7
  6.4 0.0 copy-start.8
  6.4 8.8 %all-to-all-start = ((f32[32,2,2,8,512]{4,3,2,1,0:T(8,128)}), f32[32,2,2,8,512]{4,3,2,1,0:T(8,128)}, u32[]{:S(2)}, u32[]{:S(2)}) async-start(f32[32,2,2,8,512]{4,3,2,1,0:T(8,128)} %bitcast.16), calls=%async_computation | async-start | bytes 4194304 | tf_op jit(solution)/shard_map/all_to_all | solution.py:325
  15.2 0.0 copy-done.7
  15.2 0.0 copy-done.8
  15.2 0.3 dynamic-slice_select_fusion
  15.6 2.6 %reshape.33 = s32[256,4,8,4]{3,2,1,0:T(8,128)} reshape(s32[1024,32]{1,0:T(8,128)S(1)} %dynamic-slice_select_fusion) | data formatting | bytes 262144 | tf_op jit(solution)/shard_map/reshape | solution.py:304
  18.1 4.2 %copy.15 = s32[256,4,8,4]{0,2,1,3:T(8,128)} copy(s32[256,4,8,4]{3,2,1,0:T(8,128)} %reshape.33) | data formatting | bytes 262144 | tf_op jit(solution)/shard_map/reshape | solution.py:304
  22.4 0.0 copy-start
  22.4 0.0 copy-start.2
  22.4 5.1 %first_transform.5 = f32[4,8,2,1,8,512]{5,4,3,2,1,0:T(8,128)} custom-call(f32[2,4,128,1024]{3,2,1,0:T(8,128)} %movie_ref.5, bf16[4,256,512]{2,1,0:T(8,128)(2,1)} %constant.31.clone.high_ref, bf16[4,256,512]{2,1,0:T(8,128)(2,1)} %constant.32.clone.low_ref, s32[4,4,8,256]{3,2,1,0:T(8,128)} %bitcast.19), custom_call_target="tpu_custom_call" | custom-call | flops 1024 | bytes 1024 | tf_op jit(solution)/shard_map/first_transform/pallas_call | solution.py:86
  27.5 15.6 %all-to-all-done = f32[32,2,2,8,512]{4,3,2,1,0:T(8,128)} async-done(((f32[32,2,2,8,512]{4,3,2,1,0:T(8,128)}), f32[32,2,2,8,512]{4,3,2,1,0:T(8,128)}, u32[]{:S(2)}, u32[]{:S(2)}) %all-to-all-start) | async-done | bytes 2097184 | tf_op jit(solution)/shard_map/all_to_all | solution.py:325
  43.1 6.0 %all-to-all-start.2 = ((f32[32,2,1,8,512]{4,3,1,2,0:T(8,128)}), f32[32,2,1,8,512]{4,3,1,2,0:T(8,128)S(1)}, u32[]{:S(2)}, u32[]{:S(2)}) async-start(f32[32,2,1,8,512]{4,3,1,2,0:T(8,128)} %bitcast.18), calls=%async_computation.2 | async-start | bytes 2097152 | tf_op jit(solution)/shard_map/all_to_all | solution.py:325
  49.1 0.0 copy-done
  49.1 0.0 copy-done.2
  49.1 4.4 %second_transform.3 = (f32[2,2,2,32,1024]{4,3,2,1,0:T(8,128)}, f32[2,2,2,32,1024]{4,3,2,1,0:T(8,128)}, f32[8,128]{1,0:T(8,128)S(1)}) custom-call(f32[4,8,2,2,8,512]{5,4,3,2,1,0:T(8,128)} %bitcast.3.piece_ref, bf16[4,256,512]{2,1,0:T(8,128)(2,1)S(1)} %copy-done, bf16[4,256,512]{2,1,0:T(8,128)(2,1)S(1)} %copy-done.2), custom_call_target="tpu_custom_call" | custom-call | flops 1024 | bytes 1024 | tf_op jit(solution)/shard_map/second_transform/pallas_call | solution.py:139
  53.5 0.0 copy-start.4
  53.5 0.6 copy-done.4
  54.1 5.6 %collective-permute-start = (f32[2,2,2,32,1024]{4,3,2,1,0:T(8,128)}, f32[2,2,2,32,1024]{4,3,2,1,0:T(8,128)}, u32[]{:S(2)}, u32[]{:S(2)}) collective-permute-start(f32[2,2,2,32,1024]{4,3,2,1,0:T(8,128)} %get-tuple-element.19.early_ref), channel_id=1, source_target_pairs={{0,56},{8,0},{16,8},{24,16},{32,24},{40,32},{48,40},{56,48},{1,57}... | collective-permute-start | bytes 3145736 | tf_op jit(solution)/shard_map/ppermute | solution.py:312
  59.6 0.0 collective-permute-start.1
  59.6 0.0 copy-start.6
  59.6 0.0 copy-start.1
  59.6 0.0 copy-start.3
  59.6 5.1 %first_transform.4 = f32[4,8,2,1,8,512]{5,4,3,2,1,0:T(8,128)} custom-call(f32[2,4,128,1024]{3,2,1,0:T(8,128)} %movie_ref.5, bf16[4,256,512]{2,1,0:T(8,128)(2,1)} %constant.31.clone.high_ref, bf16[4,256,512]{2,1,0:T(8,128)(2,1)} %constant.32.clone.low_ref, f32[8,128]{1,0:T(8,128)} %copy-done.4), custom_call_target="tpu_custom_call" | custom-call | flops 1024 | bytes 1024 | tf_op jit(solution)/shard_map/first_transform/pallas_call | solution.py:86
  64.8 1.6 %all-to-all-done.2 = f32[32,2,1,8,512]{4,3,1,2,0:T(8,128)S(1)} async-done(((f32[32,2,1,8,512]{4,3,1,2,0:T(8,128)}), f32[32,2,1,8,512]{4,3,1,2,0:T(8,128)S(1)}, u32[]{:S(2)}, u32[]{:S(2)}) %all-to-all-start.2) | async-done | bytes 1048608 | tf_op jit(solution)/shard_map/all_to_all | solution.py:325
  66.4 6.2 %all-to-all-start.1 = ((f32[32,2,1,8,512]{4,3,1,2,0:T(8,128)}), f32[32,2,1,8,512]{4,3,1,2,0:T(8,128)}, u32[]{:S(2)}, u32[]{:S(2)}) async-start(f32[32,2,1,8,512]{4,3,1,2,0:T(8,128)} %bitcast.17), calls=%async_computation.1 | async-start | bytes 2097152 | tf_op jit(solution)/shard_map/all_to_all | solution.py:325
  72.6 0.0 copy-done.6
  72.7 0.1 add_convert_fusion.ends_ref
  72.7 0.0 copy-done.1
  72.7 0.0 copy-done.3
  72.7 2.0 %second_transform.4 = (f32[2,2,1,32,1024]{4,3,2,1,0:T(8,128)}, f32[2,2,1,32,1024]{4,3,2,1,0:T(8,128)}, f32[8,128]{1,0:T(8,128)S(1)}) custom-call(f32[4,8,2,1,8,512]{5,4,3,2,1,0:T(8,128)S(1)} %bitcast.15, bf16[4,256,512]{2,1,0:T(8,128)(2,1)S(1)} %copy-done.1, bf16[4,256,512]{2,1,0:T(8,128)(2,1)S(1)} %copy-done.3), custom_call_target="tpu_custom_call" | custom-call | flops 1024 | bytes 1024 | tf_op jit(solution)/shard_map/second_transform/pallas_call | solution.py:139
  74.8 4.0 %collective-permute-start.4 = (f32[2,2,1,32,1024]{4,3,2,1,0:T(8,128)}, f32[2,2,1,32,1024]{4,3,2,1,0:T(8,128)S(1)}, u32[]{:S(2)}, u32[]{:S(2)}) collective-permute-start(f32[2,2,1,32,1024]{4,3,2,1,0:T(8,128)} %get-tuple-element.25.early_ref), channel_id=1, source_target_pairs={{0,56},{8,0},{16,8},{24,16},{32,24},{40,32},{48,40},{56,48},{1,57}... | collective-permute-start | bytes 1572872 | tf_op jit(solution)/shard_map/ppermute | solution.py:312
  78.8 0.0 collective-permute-start.5
  78.8 3.4 %collective-permute-done.right_ref = f32[2,2,2,32,1024]{4,3,2,1,0:T(8,128)} collective-permute-done((f32[2,2,2,32,1024]{4,3,2,1,0:T(8,128)}, f32[2,2,2,32,1024]{4,3,2,1,0:T(8,128)}, u32[]{:S(2)}, u32[]{:S(2)}) %collective-permute-start) | collective-permute-done | bytes 1048608 | tf_op jit(solution)/shard_map/ppermute | solution.py:312
  82.1 3.1 %collective-permute-done.1.left_ref = f32[2,2,2,32,1024]{4,3,2,1,0:T(8,128)} collective-permute-done((f32[2,2,2,32,1024]{4,3,2,1,0:T(8,128)}, f32[2,2,2,32,1024]{4,3,2,1,0:T(8,128)}, u32[]{:S(2)}, u32[]{:S(2)}) %collective-permute-start.1) | collective-permute-done | bytes 1048608 | tf_op jit(solution)/shard_map/ppermute | solution.py:312
  85.2 5.1 %partial_lags.3 = (f32[32,2,8,128]{3,2,1,0:T(8,128)}, f32[8,128]{1,0:T(8,128)S(1)}) custom-call(s32[2]{0:T(128)S(1)} %add_convert_fusion.ends_ref, f32[2,2,2,32,1024]{4,3,2,1,0:T(8,128)} %get-tuple-element.19.early_ref, f32[2,2,2,32,1024]{4,3,2,1,0:T(8,128)} %get-tuple-element.20.late_ref, f32[2,2,2,32,1024]{4,3,2,1,0:T(8,128)} %collective-permute-done.right_ref, ...), custom_call_target="tpu_custom_call" | custom-call | flops 1024 | bytes 1024 | tf_op jit(solution)/shard_map/partial_lags/pallas_call | solution.py:243
  90.4 0.0 all-to-all-done.1
  90.4 3.3 %second_transform.5 = (f32[2,2,1,32,1024]{4,3,2,1,0:T(8,128)}, f32[2,2,1,32,1024]{4,3,2,1,0:T(8,128)}, f32[8,128]{1,0:T(8,128)S(1)}) custom-call(f32[4,8,2,1,8,512]{5,4,3,2,1,0:T(8,128)} %bitcast.6.piece_ref, bf16[4,256,512]{2,1,0:T(8,128)(2,1)S(1)} %copy-done.1, bf16[4,256,512]{2,1,0:T(8,128)(2,1)S(1)} %copy-done.3, ...), custom_call_target="tpu_custom_call" | custom-call | flops 1024 | bytes 1024 | tf_op jit(solution)/shard_map/second_transform/pallas_call | solution.py:139
  93.6 3.6 %collective-permute-start.2 = (f32[2,2,1,32,1024]{4,3,2,1,0:T(8,128)}, f32[2,2,1,32,1024]{4,3,2,1,0:T(8,128)S(1)}, u32[]{:S(2)}, u32[]{:S(2)}) collective-permute-start(f32[2,2,1,32,1024]{4,3,2,1,0:T(8,128)} %get-tuple-element.23.early_ref), channel_id=1, source_target_pairs={{0,56},{8,0},{16,8},{24,16},{32,24},{40,32},{48,40},{56,48},{1,57}... | collective-permute-start | bytes 1572872 | tf_op jit(solution)/shard_map/ppermute | solution.py:312
  97.2 0.0 collective-permute-start.3
  97.2 5.3 %all-to-all-start.3 = ((f32[32,2,8,128]{3,2,1,0:T(8,128)}), f32[32,2,8,128]{3,2,1,0:T(8,128)}, u32[]{:S(2)}, u32[]{:S(2)}) async-start(f32[32,2,8,128]{3,2,1,0:T(8,128)} %get-tuple-element.31), calls=%async_computation.3 | async-start | bytes 524288 | tf_op jit(solution)/shard_map/all_to_all | solution.py:341
  102.6 0.0 collective-permute-done.4.right_ref
  102.6 0.0 collective-permute-done.5.left_ref
  102.6 2.5 %partial_lags.4 = (f32[32,1,8,128]{3,2,1,0:T(8,128)S(1)}, f32[8,128]{1,0:T(8,128)S(1)}) custom-call(s32[2]{0:T(128)S(1)} %add_convert_fusion.ends_ref, f32[2,2,1,32,1024]{4,3,2,1,0:T(8,128)} %get-tuple-element.25.early_ref, f32[2,2,1,32,1024]{4,3,2,1,0:T(8,128)} %get-tuple-element.26.late_ref, f32[2,2,1,32,1024]{4,3,2,1,0:T(8,128)S(1)} %collective-permute-done.4.right_ref, ...), custom_call_target="tpu_custom_call" | custom-call | flops 1024 | bytes 1024 | tf_op jit(solution)/shard_map/partial_lags/pallas_call | solution.py:243
  105.1 5.6 %collective-permute-done.2.right_ref = f32[2,2,1,32,1024]{4,3,2,1,0:T(8,128)S(1)} collective-permute-done((f32[2,2,1,32,1024]{4,3,2,1,0:T(8,128)}, f32[2,2,1,32,1024]{4,3,2,1,0:T(8,128)S(1)}, u32[]{:S(2)}, u32[]{:S(2)}) %collective-permute-start.2) | collective-permute-done | bytes 524320 | tf_op jit(solution)/shard_map/ppermute | solution.py:312
  110.7 1.3 collective-permute-done.3.left_ref
  112.0 3.1 %partial_lags.5 = (f32[32,3,8,128]{3,2,1,0:T(8,128)S(1)}, f32[8,128]{1,0:T(8,128)}) custom-call(s32[2]{0:T(128)S(1)} %add_convert_fusion.ends_ref, f32[2,2,1,32,1024]{4,3,2,1,0:T(8,128)} %get-tuple-element.23.early_ref, f32[2,2,1,32,1024]{4,3,2,1,0:T(8,128)} %get-tuple-element.24.late_ref, f32[2,2,1,32,1024]{4,3,2,1,0:T(8,128)S(1)} %collective-permute-done.2.right_ref, ...), custom_call_target="tpu_custom_call" | custom-call | flops 1024 | bytes 1024 | tf_op jit(solution)/shard_map/partial_lags/pallas_call | solution.py:243
  115.1 0.0 all-to-all-done.3.refs_0_
  115.1 18.2 %all_to_all.30.refs_1_ = f32[32,3,8,128]{3,2,1,0:T(8,128)S(1)} all-to-all(f32[32,3,8,128]{3,2,1,0:T(8,128)S(1)} %get-tuple-element.32), channel_id=1, replica_groups=mesh['tm_0'=4,'tm_1'=8,'row_0'=4,'row_1'=2] {'tm_0','tm_1'}, dimensions={0} | all-to-all | bytes 786432 | tf_op jit(solution)/shard_map/all_to_all | solution.py:345
  133.3 0.0 copy-start.5
  133.4 0.7 broadcast_in_dim.16
  134.1 8.2 %all-to-all-start.5 = ((f32[8,8,128]{2,1,0:T(8,128)}), f32[8,8,128]{2,1,0:T(8,128)S(1)}, u32[]{:S(2)}, u32[]{:S(2)}) async-start(f32[8,8,128]{2,1,0:T(8,128)} %broadcast_in_dim.16), calls=%async_computation.5 | async-start | bytes 65536 | tf_op jit(solution)/shard_map/all_to_all | solution.py:348
  142.3 0.0 copy-done.5
  142.3 2.1 %settle.1 = f32[4,32,128]{2,1,0:T(8,128)} custom-call(f32[32,2,8,128]{3,2,1,0:T(8,128)} %all-to-all-done.3.refs_0_, f32[32,3,8,128]{3,2,1,0:T(8,128)} %copy-done.5), custom_call_target="tpu_custom_call" | custom-call | tf_op jit(solution)/shard_map/settle/pallas_call | solution.py:289
  144.4 2.6 %all-to-all-done.5 = f32[8,8,128]{2,1,0:T(8,128)S(1)} async-done(((f32[8,8,128]{2,1,0:T(8,128)}), f32[8,8,128]{2,1,0:T(8,128)S(1)}, u32[]{:S(2)}, u32[]{:S(2)}) %all-to-all-start.5) | async-done | bytes 32800 | tf_op jit(solution)/shard_map/all_to_all | solution.py:348
  147.0 0.6 slice_divide_fusion
  (6 shorter events, 0.1 us)
Async XLA Ops:
  6.4 8.8 %copy-start.7 = (s32[1024,128]{1,0:T(8,128)S(1)}, s32[1024,128]{1,0:T(8,128)}, u32[]{:S(2)}) copy-start(s32[1024,128]{1,0:T(8,128)} %param.6) | copy-start | bytes 1572868
  6.4 8.8 %copy-start.8 = (s32[1024,128]{1,0:T(8,128)S(1)}, s32[1024,128]{1,0:T(8,128)}, u32[]{:S(2)}) copy-start(s32[1024,128]{1,0:T(8,128)} %param.7) | copy-start | bytes 1572868
  6.4 36.7 %all-to-all-start = ((f32[32,2,2,8,512]{4,3,2,1,0:T(8,128)}), f32[32,2,2,8,512]{4,3,2,1,0:T(8,128)}, u32[]{:S(2)}, u32[]{:S(2)}) async-start(f32[32,2,2,8,512]{4,3,2,1,0:T(8,128)} %bitcast.16), calls=%async_computation | async-start | bytes 4194304 | tf_op jit(solution)/shard_map/all_to_all | solution.py:325
  22.4 26.7 %copy-start = (bf16[4,256,512]{2,1,0:T(8,128)(2,1)S(1)}, bf16[4,256,512]{2,1,0:T(8,128)(2,1)}, u32[]{:S(2)}) copy-start(bf16[4,256,512]{2,1,0:T(8,128)(2,1)} %constant.31.clone.high_ref) | copy-start | bytes 3145732
  22.4 26.7 %copy-start.2 = (bf16[4,256,512]{2,1,0:T(8,128)(2,1)S(1)}, bf16[4,256,512]{2,1,0:T(8,128)(2,1)}, u32[]{:S(2)}) copy-start(bf16[4,256,512]{2,1,0:T(8,128)(2,1)} %constant.32.clone.low_ref) | copy-start | bytes 3145732
  43.1 23.3 %all-to-all-start.2 = ((f32[32,2,1,8,512]{4,3,1,2,0:T(8,128)}), f32[32,2,1,8,512]{4,3,1,2,0:T(8,128)S(1)}, u32[]{:S(2)}, u32[]{:S(2)}) async-start(f32[32,2,1,8,512]{4,3,1,2,0:T(8,128)} %bitcast.18), calls=%async_computation.2 | async-start | bytes 2097152 | tf_op jit(solution)/shard_map/all_to_all | solution.py:325
  53.5 0.6 copy-start.4
  54.1 28.1 %collective-permute-start = (f32[2,2,2,32,1024]{4,3,2,1,0:T(8,128)}, f32[2,2,2,32,1024]{4,3,2,1,0:T(8,128)}, u32[]{:S(2)}, u32[]{:S(2)}) collective-permute-start(f32[2,2,2,32,1024]{4,3,2,1,0:T(8,128)} %get-tuple-element.19.early_ref), channel_id=1, source_target_pairs={{0,56},{8,0},{16,8},{24,16},{32,24},{40,32},{48,40},{56,48},{1,57}... | collective-permute-start | bytes 3145736 | tf_op jit(solution)/shard_map/ppermute | solution.py:312
  59.6 25.6 %collective-permute-start.1 = (f32[2,2,2,32,1024]{4,3,2,1,0:T(8,128)}, f32[2,2,2,32,1024]{4,3,2,1,0:T(8,128)}, u32[]{:S(2)}, u32[]{:S(2)}) collective-permute-start(f32[2,2,2,32,1024]{4,3,2,1,0:T(8,128)} %get-tuple-element.20.late_ref), channel_id=1, source_target_pairs={{0,8},{8,16},{16,24},{24,32},{32,40},{40,48},{48,56},{56,0},{1,9},... | collective-permute-start | bytes 3145736 | tf_op jit(solution)/shard_map/ppermute | solution.py:312
  59.6 13.0 %copy-start.6 = (s32[256,4,8,4]{0,2,1,3:T(8,128)S(1)}, s32[256,4,8,4]{0,2,1,3:T(8,128)}, u32[]{:S(2)}) copy-start(s32[256,4,8,4]{0,2,1,3:T(8,128)} %copy.15) | copy-start | bytes 393220
  59.6 13.1 %copy-start.1 = (bf16[4,256,512]{2,1,0:T(8,128)(2,1)S(1)}, bf16[4,256,512]{2,1,0:T(8,128)(2,1)}, u32[]{:S(2)}) copy-start(bf16[4,256,512]{2,1,0:T(8,128)(2,1)} %constant.31.clone.high_ref) | copy-start | bytes 3145732
  59.6 13.1 %copy-start.3 = (bf16[4,256,512]{2,1,0:T(8,128)(2,1)S(1)}, bf16[4,256,512]{2,1,0:T(8,128)(2,1)}, u32[]{:S(2)}) copy-start(bf16[4,256,512]{2,1,0:T(8,128)(2,1)} %constant.32.clone.low_ref) | copy-start | bytes 3145732
  66.4 24.0 %all-to-all-start.1 = ((f32[32,2,1,8,512]{4,3,1,2,0:T(8,128)}), f32[32,2,1,8,512]{4,3,1,2,0:T(8,128)}, u32[]{:S(2)}, u32[]{:S(2)}) async-start(f32[32,2,1,8,512]{4,3,1,2,0:T(8,128)} %bitcast.17), calls=%async_computation.1 | async-start | bytes 2097152 | tf_op jit(solution)/shard_map/all_to_all | solution.py:325
  74.8 27.8 %collective-permute-start.4 = (f32[2,2,1,32,1024]{4,3,2,1,0:T(8,128)}, f32[2,2,1,32,1024]{4,3,2,1,0:T(8,128)S(1)}, u32[]{:S(2)}, u32[]{:S(2)}) collective-permute-start(f32[2,2,1,32,1024]{4,3,2,1,0:T(8,128)} %get-tuple-element.25.early_ref), channel_id=1, source_target_pairs={{0,56},{8,0},{16,8},{24,16},{32,24},{40,32},{48,40},{56,48},{1,57}... | collective-permute-start | bytes 1572872 | tf_op jit(solution)/shard_map/ppermute | solution.py:312
  78.8 23.8 %collective-permute-start.5 = (f32[2,2,1,32,1024]{4,3,2,1,0:T(8,128)}, f32[2,2,1,32,1024]{4,3,2,1,0:T(8,128)S(1)}, u32[]{:S(2)}, u32[]{:S(2)}) collective-permute-start(f32[2,2,1,32,1024]{4,3,2,1,0:T(8,128)} %get-tuple-element.26.late_ref), channel_id=1, source_target_pairs={{0,8},{8,16},{16,24},{24,32},{32,40},{40,48},{48,56},{56,0},{1,9},... | collective-permute-start | bytes 1572872 | tf_op jit(solution)/shard_map/ppermute | solution.py:312
  93.6 17.1 %collective-permute-start.2 = (f32[2,2,1,32,1024]{4,3,2,1,0:T(8,128)}, f32[2,2,1,32,1024]{4,3,2,1,0:T(8,128)S(1)}, u32[]{:S(2)}, u32[]{:S(2)}) collective-permute-start(f32[2,2,1,32,1024]{4,3,2,1,0:T(8,128)} %get-tuple-element.23.early_ref), channel_id=1, source_target_pairs={{0,56},{8,0},{16,8},{24,16},{32,24},{40,32},{48,40},{56,48},{1,57}... | collective-permute-start | bytes 1572872 | tf_op jit(solution)/shard_map/ppermute | solution.py:312
  97.2 14.8 %collective-permute-start.3 = (f32[2,2,1,32,1024]{4,3,2,1,0:T(8,128)}, f32[2,2,1,32,1024]{4,3,2,1,0:T(8,128)S(1)}, u32[]{:S(2)}, u32[]{:S(2)}) collective-permute-start(f32[2,2,1,32,1024]{4,3,2,1,0:T(8,128)} %get-tuple-element.24.late_ref), channel_id=1, source_target_pairs={{0,8},{8,16},{16,24},{24,32},{32,40},{40,48},{48,56},{56,0},{1,9},... | collective-permute-start | bytes 1572872 | tf_op jit(solution)/shard_map/ppermute | solution.py:312
  97.2 17.9 %all-to-all-start.3 = ((f32[32,2,8,128]{3,2,1,0:T(8,128)}), f32[32,2,8,128]{3,2,1,0:T(8,128)}, u32[]{:S(2)}, u32[]{:S(2)}) async-start(f32[32,2,8,128]{3,2,1,0:T(8,128)} %get-tuple-element.31), calls=%async_computation.3 | async-start | bytes 524288 | tf_op jit(solution)/shard_map/all_to_all | solution.py:341
  133.3 8.9 %copy-start.5 = (f32[32,3,8,128]{3,2,1,0:T(8,128)}, f32[32,3,8,128]{3,2,1,0:T(8,128)S(1)}, u32[]{:S(2)}) copy-start(f32[32,3,8,128]{3,2,1,0:T(8,128)S(1)} %all_to_all.30.refs_1_) | copy-start | bytes 1179652
  134.1 12.9 %all-to-all-start.5 = ((f32[8,8,128]{2,1,0:T(8,128)}), f32[8,8,128]{2,1,0:T(8,128)S(1)}, u32[]{:S(2)}, u32[]{:S(2)}) async-start(f32[8,8,128]{2,1,0:T(8,128)} %broadcast_in_dim.16), calls=%async_computation.5 | async-start | bytes 65536 | tf_op jit(solution)/shard_map/all_to_all | solution.py:348

commit v4 on v3

--- a/solution.py
+++ b/solution.py
@@ -22,7 +22,7 @@
 CHUNKS = ((0, 1), (2,), (3,))
 ROW = ("row_0", "row_1")
 TM = ("tm_0", "tm_1")
-YROW = ("tm_0", "row_0", "row_1")
+ROWY = ("row_0", "row_1", "tm_0")
 
 f32 = jnp.float32
 bf16 = jnp.bfloat16
@@ -73,9 +73,7 @@
         th, tl = high_ref[j], low_ref[j]
         got = nt(th, zh) + nt(tl, zh) + nt(th, zl)
         for c in range(2):
-            piece = got[:, c * 128:(c + 1) * 128].reshape(8, 4, 8, 128)
-            for y in range(4):
-                out_ref[y, :, c, j] = piece[:, y]
+            out_ref[:, :, c, j] = got[:, c * 128:(c + 1) * 128].reshape(8, 4, 8, 128)
 
 
 def first_transform(movie, high, low, residues, after):
@@ -87,8 +85,8 @@
         functools.partial(first_kernel, residues),
         grid=(OWN,),
         in_specs=[pl.BlockSpec((2, 1, 128, N), lambda f: (0, f, 0, 0)), table, table] + order,
-        out_specs=pl.BlockSpec((4, 8, 2, count, 8, 128), lambda f: (0, 0, 0, 0, 0, f)),
-        out_shape=jax.ShapeDtypeStruct((4, 8, 2, count, 8, OWN * 128), f32),
+        out_specs=pl.BlockSpec((8, 4, 2, count, 8, 128), lambda f: (0, 0, 0, 0, 0, f)),
+        out_shape=jax.ShapeDtypeStruct((8, 4, 2, count, 8, OWN * 128), f32),
         compiler_params=pltpu.CompilerParams(vmem_limit_bytes=(56 if residues[0] == 0 else REST_VMEM) << 20),
         cost_estimate=pl.CostEstimate(
             flops=1024, bytes_accessed=1024, transcendentals=0
@@ -107,7 +105,7 @@
                 [
                     jnp.concatenate(
                         [
-                            piece_ref[y, 2 * q + h, c, j, :, f * 128:(f + 1) * 128]
+                            piece_ref[2 * q + h, y, c, j, :, f * 128:(f + 1) * 128]
                             for f in range(OWN)
                             for y in range(4)
                         ],
@@ -140,7 +138,7 @@
         functools.partial(second_kernel, 1),
         grid=(count,),
         in_specs=[
-            pl.BlockSpec((4, 8, 2, 1, 8, OWN * 128), lambda j: (0, 0, 0, j, 0, 0)),
+            pl.BlockSpec((8, 4, 2, 1, 8, OWN * 128), lambda j: (0, 0, 0, j, 0, 0)),
             table,
             table,
         ]
@@ -322,8 +320,8 @@
         return first_transform(movie, high, low, CHUNKS[index], after)
 
     def exchange(piece):
-        piece = lax.all_to_all(piece.reshape((32,) + piece.shape[2:]), YROW, 0, 0, tiled=True)
-        return piece.reshape((4, 8) + piece.shape[1:])
+        piece = lax.all_to_all(piece.reshape((32,) + piece.shape[2:]), ROWY, 0, 0, tiled=True)
+        return piece.reshape((8, 4) + piece.shape[1:])
 
     def transform_columns(piece, index, after):
         spectra.append(second_transform(piece, high, low, len(CHUNKS[index]), after))

time: 148 us -> 145 us (0.980)
  waiting for transfers between devices: 33.3 us -> 31.4 us
  blocking collectives: 18.2 us -> 16.6 us
    all_to_all x3, waiting for transfers between devices: 17.2 us -> 15.4 us  [exchange(): lax.all_to_all(piece.reshape((32,) + piece.shape[2:]), ROWY, 0, 0, tiled=...]
    all_to_all x1, blocking collectives: 18.2 us -> 16.6 us  [body(): sums_1 = lax.all_to_all(part_2, TM, 0, 0, tiled=True)]
    ppermute x3, starting transfers between devices: 13.1 us -> 11.6 us  [halo(): lax.ppermute(early, 'tm_1', to_left)]
  transfers between devices with their start and end apart: 11 -> 11, of which waited for: 7 -> 8; matrix products, arithmetic and copies ran while one was open for 5% -> 5% of each run, Pallas kernels for 22% -> 23%
where the time goes in v4:
time: 145 us
  starting transfers between devices  48.1 us (33%)
  Pallas kernels  38.5 us (27%)
  waiting for transfers between devices  31.4 us (22%)
  blocking collectives  16.6 us (11%)
  local copies, waits for them, and re-layouts  8.09 us (6%)
    all_to_all x3, starting transfers between devices, exchange(): lax.all_to_all(piece.reshape((32,) + piece.shape[2:]), ROWY, 0, 0, tiled=...  21.8 us
    all_to_all x1, blocking collectives, body(): sums_1 = lax.all_to_all(part_2, TM, 0, 0, tiled=True)  16.6 us
    pallas_call x3, Pallas kernels, first_transform(): pl.pallas_call(functools.partial(first_kernel, residues), grid=(OWN,), in...  16.1 us
    all_to_all x3, waiting for transfers between devices, exchange(): lax.all_to_all(piece.reshape((32,) + piece.shape[2:]), ROWY, 0, 0, tiled=...  15.4 us
    ppermute x3, starting transfers between devices, halo(): lax.ppermute(early, 'tm_1', to_left)  11.6 us
    pallas_call x3, Pallas kernels, partial_lags(): pl.pallas_call(functools.partial(lag_kernel, count, carried, final), in_s...  10.7 us
    pallas_call x3, Pallas kernels, second_transform(): pl.pallas_call(functools.partial(second_kernel, 1), grid=(count,), in_spe...  9.67 us
    all_to_all x1, starting transfers between devices, body(): cycles = jnp.sum(lax.all_to_all(copies, ROW, 0, 0, tiled=True), axis=0)  9.11 us
  transfers between devices with their start and end apart: 11, of which 8 were waited for; matrix products, arithmetic and copies ran while one was open for 5% of the time, Pallas kernels for 23%

profile of v4, /device:TPU:1, one launch (start us, length us, event | category | flops | bytes accessed | tf_op | source)
XLA Modules:
  0.0 144.5 jit_solution(5824555273331553157)
XLA Ops:
  0.6 5.8 %first_transform.3 = f32[8,4,2,2,8,512]{5,4,3,2,1,0:T(8,128)} custom-call(f32[2,4,128,1024]{3,2,1,0:T(8,128)} %movie_ref.5, bf16[4,256,512]{2,1,0:T(8,128)(2,1)} %constant.31.clone.high_ref, bf16[4,256,512]{2,1,0:T(8,128)(2,1)} %constant.32.clone.low_ref), custom_call_target="tpu_custom_call" | custom-call | flops 1024 | bytes 1024 | tf_op jit(solution)/shard_map/first_transform/pallas_call | solution.py:84
  6.4 0.0 copy-start.7
  6.4 0.0 copy-start.8
  6.4 8.8 %all-to-all-start = ((f32[32,2,2,8,512]{4,3,2,1,0:T(8,128)}), f32[32,2,2,8,512]{4,3,2,1,0:T(8,128)}, u32[]{:S(2)}, u32[]{:S(2)}) async-start(f32[32,2,2,8,512]{4,3,2,1,0:T(8,128)} %bitcast.16), calls=%async_computation | async-start | bytes 4194304 | tf_op jit(solution)/shard_map/all_to_all | solution.py:323
  15.2 0.0 copy-done.7
  15.2 0.0 copy-done.8
  15.3 0.3 dynamic-slice_select_fusion
  15.6 2.6 %reshape.33 = s32[256,4,8,4]{3,2,1,0:T(8,128)} reshape(s32[1024,32]{1,0:T(8,128)S(1)} %dynamic-slice_select_fusion) | data formatting | bytes 262144 | tf_op jit(solution)/shard_map/reshape | solution.py:302
  18.1 4.2 %copy.15 = s32[256,4,8,4]{0,2,1,3:T(8,128)} copy(s32[256,4,8,4]{3,2,1,0:T(8,128)} %reshape.33) | data formatting | bytes 262144 | tf_op jit(solution)/shard_map/reshape | solution.py:302
  22.4 0.0 copy-start
  22.4 0.0 copy-start.2
  22.4 5.1 %first_transform.5 = f32[8,4,2,1,8,512]{5,4,3,2,1,0:T(8,128)} custom-call(f32[2,4,128,1024]{3,2,1,0:T(8,128)} %movie_ref.5, bf16[4,256,512]{2,1,0:T(8,128)(2,1)} %constant.31.clone.high_ref, bf16[4,256,512]{2,1,0:T(8,128)(2,1)} %constant.32.clone.low_ref, s32[4,4,8,256]{3,2,1,0:T(8,128)} %bitcast.19), custom_call_target="tpu_custom_call" | custom-call | flops 1024 | bytes 1024 | tf_op jit(solution)/shard_map/first_transform/pallas_call | solution.py:84
  27.5 14.7 %all-to-all-done = f32[32,2,2,8,512]{4,3,2,1,0:T(8,128)} async-done(((f32[32,2,2,8,512]{4,3,2,1,0:T(8,128)}), f32[32,2,2,8,512]{4,3,2,1,0:T(8,128)}, u32[]{:S(2)}, u32[]{:S(2)}) %all-to-all-start) | async-done | bytes 2097184 | tf_op jit(solution)/shard_map/all_to_all | solution.py:323
  42.2 5.9 %all-to-all-start.2 = ((f32[32,2,1,8,512]{4,3,1,2,0:T(8,128)}), f32[32,2,1,8,512]{4,3,1,2,0:T(8,128)S(1)}, u32[]{:S(2)}, u32[]{:S(2)}) async-start(f32[32,2,1,8,512]{4,3,1,2,0:T(8,128)} %bitcast.18), calls=%async_computation.2 | async-start | bytes 2097152 | tf_op jit(solution)/shard_map/all_to_all | solution.py:323
  48.1 0.0 copy-done
  48.2 0.0 copy-done.2
  48.2 4.4 %second_transform.3 = (f32[2,2,2,32,1024]{4,3,2,1,0:T(8,128)}, f32[2,2,2,32,1024]{4,3,2,1,0:T(8,128)}, f32[8,128]{1,0:T(8,128)S(1)}) custom-call(f32[8,4,2,2,8,512]{5,4,3,2,1,0:T(8,128)} %bitcast.3.piece_ref, bf16[4,256,512]{2,1,0:T(8,128)(2,1)S(1)} %copy-done, bf16[4,256,512]{2,1,0:T(8,128)(2,1)S(1)} %copy-done.2), custom_call_target="tpu_custom_call" | custom-call | flops 1024 | bytes 1024 | tf_op jit(solution)/shard_map/second_transform/pallas_call | solution.py:137
  52.5 0.0 copy-start.4
  52.5 0.6 copy-done.4
  53.1 5.6 %collective-permute-start = (f32[2,2,2,32,1024]{4,3,2,1,0:T(8,128)}, f32[2,2,2,32,1024]{4,3,2,1,0:T(8,128)}, u32[]{:S(2)}, u32[]{:S(2)}) collective-permute-start(f32[2,2,2,32,1024]{4,3,2,1,0:T(8,128)} %get-tuple-element.19.early_ref), channel_id=1, source_target_pairs={{0,56},{8,0},{16,8},{24,16},{32,24},{40,32},{48,40},{56,48},{1,57}... | collective-permute-start | bytes 3145736 | tf_op jit(solution)/shard_map/ppermute | solution.py:310
  58.7 0.0 collective-permute-start.1
  58.7 0.0 copy-start.6
  58.7 0.0 copy-start.1
  58.7 0.0 copy-start.3
  58.7 5.1 %first_transform.4 = f32[8,4,2,1,8,512]{5,4,3,2,1,0:T(8,128)} custom-call(f32[2,4,128,1024]{3,2,1,0:T(8,128)} %movie_ref.5, bf16[4,256,512]{2,1,0:T(8,128)(2,1)} %constant.31.clone.high_ref, bf16[4,256,512]{2,1,0:T(8,128)(2,1)} %constant.32.clone.low_ref, f32[8,128]{1,0:T(8,128)} %copy-done.4), custom_call_target="tpu_custom_call" | custom-call | flops 1024 | bytes 1024 | tf_op jit(solution)/shard_map/first_transform/pallas_call | solution.py:84
  63.8 0.6 all-to-all-done.2
  64.5 7.1 %all-to-all-start.1 = ((f32[32,2,1,8,512]{4,3,1,2,0:T(8,128)}), f32[32,2,1,8,512]{4,3,1,2,0:T(8,128)}, u32[]{:S(2)}, u32[]{:S(2)}) async-start(f32[32,2,1,8,512]{4,3,1,2,0:T(8,128)} %bitcast.17), calls=%async_computation.1 | async-start | bytes 2097152 | tf_op jit(solution)/shard_map/all_to_all | solution.py:323
  71.6 0.0 copy-done.6
  71.6 0.1 add_convert_fusion.ends_ref
  71.7 0.0 copy-done.1
  71.7 0.0 copy-done.3
  71.7 2.0 %second_transform.4 = (f32[2,2,1,32,1024]{4,3,2,1,0:T(8,128)}, f32[2,2,1,32,1024]{4,3,2,1,0:T(8,128)}, f32[8,128]{1,0:T(8,128)S(1)}) custom-call(f32[8,4,2,1,8,512]{5,4,3,2,1,0:T(8,128)S(1)} %bitcast.15, bf16[4,256,512]{2,1,0:T(8,128)(2,1)S(1)} %copy-done.1, bf16[4,256,512]{2,1,0:T(8,128)(2,1)S(1)} %copy-done.3), custom_call_target="tpu_custom_call" | custom-call | flops 1024 | bytes 1024 | tf_op jit(solution)/shard_map/second_transform/pallas_call | solution.py:137
  73.7 3.8 %collective-permute-start.4 = (f32[2,2,1,32,1024]{4,3,2,1,0:T(8,128)}, f32[2,2,1,32,1024]{4,3,2,1,0:T(8,128)S(1)}, u32[]{:S(2)}, u32[]{:S(2)}) collective-permute-start(f32[2,2,1,32,1024]{4,3,2,1,0:T(8,128)} %get-tuple-element.25.early_ref), channel_id=1, source_target_pairs={{0,56},{8,0},{16,8},{24,16},{32,24},{40,32},{48,40},{56,48},{1,57}... | collective-permute-start | bytes 1572872 | tf_op jit(solution)/shard_map/ppermute | solution.py:310
  77.5 0.0 collective-permute-start.5
  77.5 3.8 %collective-permute-done.right_ref = f32[2,2,2,32,1024]{4,3,2,1,0:T(8,128)} collective-permute-done((f32[2,2,2,32,1024]{4,3,2,1,0:T(8,128)}, f32[2,2,2,32,1024]{4,3,2,1,0:T(8,128)}, u32[]{:S(2)}, u32[]{:S(2)}) %collective-permute-start) | collective-permute-done | bytes 1048608 | tf_op jit(solution)/shard_map/ppermute | solution.py:310
  81.3 3.1 %collective-permute-done.1.left_ref = f32[2,2,2,32,1024]{4,3,2,1,0:T(8,128)} collective-permute-done((f32[2,2,2,32,1024]{4,3,2,1,0:T(8,128)}, f32[2,2,2,32,1024]{4,3,2,1,0:T(8,128)}, u32[]{:S(2)}, u32[]{:S(2)}) %collective-permute-start.1) | collective-permute-done | bytes 1048608 | tf_op jit(solution)/shard_map/ppermute | solution.py:310
  84.4 5.1 %partial_lags.3 = (f32[32,2,8,128]{3,2,1,0:T(8,128)}, f32[8,128]{1,0:T(8,128)S(1)}) custom-call(s32[2]{0:T(128)S(1)} %add_convert_fusion.ends_ref, f32[2,2,2,32,1024]{4,3,2,1,0:T(8,128)} %get-tuple-element.19.early_ref, f32[2,2,2,32,1024]{4,3,2,1,0:T(8,128)} %get-tuple-element.20.late_ref, f32[2,2,2,32,1024]{4,3,2,1,0:T(8,128)} %collective-permute-done.right_ref, ...), custom_call_target="tpu_custom_call" | custom-call | flops 1024 | bytes 1024 | tf_op jit(solution)/shard_map/partial_lags/pallas_call | solution.py:241
  89.5 0.0 all-to-all-done.1
  89.6 3.3 %second_transform.5 = (f32[2,2,1,32,1024]{4,3,2,1,0:T(8,128)}, f32[2,2,1,32,1024]{4,3,2,1,0:T(8,128)}, f32[8,128]{1,0:T(8,128)S(1)}) custom-call(f32[8,4,2,1,8,512]{5,4,3,2,1,0:T(8,128)} %bitcast.6.piece_ref, bf16[4,256,512]{2,1,0:T(8,128)(2,1)S(1)} %copy-done.1, bf16[4,256,512]{2,1,0:T(8,128)(2,1)S(1)} %copy-done.3, ...), custom_call_target="tpu_custom_call" | custom-call | flops 1024 | bytes 1024 | tf_op jit(solution)/shard_map/second_transform/pallas_call | solution.py:137
  92.8 2.2 %collective-permute-start.2 = (f32[2,2,1,32,1024]{4,3,2,1,0:T(8,128)}, f32[2,2,1,32,1024]{4,3,2,1,0:T(8,128)S(1)}, u32[]{:S(2)}, u32[]{:S(2)}) collective-permute-start(f32[2,2,1,32,1024]{4,3,2,1,0:T(8,128)} %get-tuple-element.23.early_ref), channel_id=1, source_target_pairs={{0,56},{8,0},{16,8},{24,16},{32,24},{40,32},{48,40},{56,48},{1,57}... | collective-permute-start | bytes 1572872 | tf_op jit(solution)/shard_map/ppermute | solution.py:310
  95.1 0.0 collective-permute-start.3
  95.1 5.6 %all-to-all-start.3 = ((f32[32,2,8,128]{3,2,1,0:T(8,128)}), f32[32,2,8,128]{3,2,1,0:T(8,128)}, u32[]{:S(2)}, u32[]{:S(2)}) async-start(f32[32,2,8,128]{3,2,1,0:T(8,128)} %get-tuple-element.31), calls=%async_computation.3 | async-start | bytes 524288 | tf_op jit(solution)/shard_map/all_to_all | solution.py:339
  100.7 0.0 collective-permute-done.4.right_ref
  100.7 0.0 collective-permute-done.5.left_ref
  100.7 2.5 %partial_lags.4 = (f32[32,1,8,128]{3,2,1,0:T(8,128)S(1)}, f32[8,128]{1,0:T(8,128)S(1)}) custom-call(s32[2]{0:T(128)S(1)} %add_convert_fusion.ends_ref, f32[2,2,1,32,1024]{4,3,2,1,0:T(8,128)} %get-tuple-element.25.early_ref, f32[2,2,1,32,1024]{4,3,2,1,0:T(8,128)} %get-tuple-element.26.late_ref, f32[2,2,1,32,1024]{4,3,2,1,0:T(8,128)S(1)} %collective-permute-done.4.right_ref, ...), custom_call_target="tpu_custom_call" | custom-call | flops 1024 | bytes 1024 | tf_op jit(solution)/shard_map/partial_lags/pallas_call | solution.py:241
  103.2 3.8 %collective-permute-done.2.right_ref = f32[2,2,1,32,1024]{4,3,2,1,0:T(8,128)S(1)} collective-permute-done((f32[2,2,1,32,1024]{4,3,2,1,0:T(8,128)}, f32[2,2,1,32,1024]{4,3,2,1,0:T(8,128)S(1)}, u32[]{:S(2)}, u32[]{:S(2)}) %collective-permute-start.2) | collective-permute-done | bytes 524320 | tf_op jit(solution)/shard_map/ppermute | solution.py:310
  107.0 2.2 %collective-permute-done.3.left_ref = f32[2,2,1,32,1024]{4,3,2,1,0:T(8,128)S(1)} collective-permute-done((f32[2,2,1,32,1024]{4,3,2,1,0:T(8,128)}, f32[2,2,1,32,1024]{4,3,2,1,0:T(8,128)S(1)}, u32[]{:S(2)}, u32[]{:S(2)}) %collective-permute-start.3) | collective-permute-done | bytes 524320 | tf_op jit(solution)/shard_map/ppermute | solution.py:310
  109.2 3.1 %partial_lags.5 = (f32[32,3,8,128]{3,2,1,0:T(8,128)S(1)}, f32[8,128]{1,0:T(8,128)}) custom-call(s32[2]{0:T(128)S(1)} %add_convert_fusion.ends_ref, f32[2,2,1,32,1024]{4,3,2,1,0:T(8,128)} %get-tuple-element.23.early_ref, f32[2,2,1,32,1024]{4,3,2,1,0:T(8,128)} %get-tuple-element.24.late_ref, f32[2,2,1,32,1024]{4,3,2,1,0:T(8,128)S(1)} %collective-permute-done.2.right_ref, ...), custom_call_target="tpu_custom_call" | custom-call | flops 1024 | bytes 1024 | tf_op jit(solution)/shard_map/partial_lags/pallas_call | solution.py:241
  112.3 0.5 all-to-all-done.3.refs_0_
  112.7 16.6 %all_to_all.30.refs_1_ = f32[32,3,8,128]{3,2,1,0:T(8,128)S(1)} all-to-all(f32[32,3,8,128]{3,2,1,0:T(8,128)S(1)} %get-tuple-element.32), channel_id=1, replica_groups=mesh['tm_0'=4,'tm_1'=8,'row_0'=4,'row_1'=2] {'tm_0','tm_1'}, dimensions={0} | all-to-all | bytes 786432 | tf_op jit(solution)/shard_map/all_to_all | solution.py:343
  129.4 0.0 copy-start.5
  129.4 0.7 broadcast_in_dim.16
  130.1 9.1 %all-to-all-start.5 = ((f32[8,8,128]{2,1,0:T(8,128)}), f32[8,8,128]{2,1,0:T(8,128)S(1)}, u32[]{:S(2)}, u32[]{:S(2)}) async-start(f32[8,8,128]{2,1,0:T(8,128)} %broadcast_in_dim.16), calls=%async_computation.5 | async-start | bytes 65536 | tf_op jit(solution)/shard_map/all_to_all | solution.py:346
  139.2 0.0 copy-done.5
  139.2 2.1 %settle.1 = f32[4,32,128]{2,1,0:T(8,128)} custom-call(f32[32,2,8,128]{3,2,1,0:T(8,128)} %all-to-all-done.3.refs_0_, f32[32,3,8,128]{3,2,1,0:T(8,128)} %copy-done.5), custom_call_target="tpu_custom_call" | custom-call | tf_op jit(solution)/shard_map/settle/pallas_call | solution.py:287
  141.3 2.6 %all-to-all-done.5 = f32[8,8,128]{2,1,0:T(8,128)S(1)} async-done(((f32[8,8,128]{2,1,0:T(8,128)}), f32[8,8,128]{2,1,0:T(8,128)S(1)}, u32[]{:S(2)}, u32[]{:S(2)}) %all-to-all-start.5) | async-done | bytes 32800 | tf_op jit(solution)/shard_map/all_to_all | solution.py:346
  144.0 0.6 slice_divide_fusion
  (6 shorter events, 0.1 us)
Async XLA Ops:
  6.4 8.8 %copy-start.7 = (s32[1024,128]{1,0:T(8,128)S(1)}, s32[1024,128]{1,0:T(8,128)}, u32[]{:S(2)}) copy-start(s32[1024,128]{1,0:T(8,128)} %param.6) | copy-start | bytes 1572868
  6.4 8.8 %copy-start.8 = (s32[1024,128]{1,0:T(8,128)S(1)}, s32[1024,128]{1,0:T(8,128)}, u32[]{:S(2)}) copy-start(s32[1024,128]{1,0:T(8,128)} %param.7) | copy-start | bytes 1572868
  6.4 35.8 %all-to-all-start = ((f32[32,2,2,8,512]{4,3,2,1,0:T(8,128)}), f32[32,2,2,8,512]{4,3,2,1,0:T(8,128)}, u32[]{:S(2)}, u32[]{:S(2)}) async-start(f32[32,2,2,8,512]{4,3,2,1,0:T(8,128)} %bitcast.16), calls=%async_computation | async-start | bytes 4194304 | tf_op jit(solution)/shard_map/all_to_all | solution.py:323
  22.4 25.8 %copy-start = (bf16[4,256,512]{2,1,0:T(8,128)(2,1)S(1)}, bf16[4,256,512]{2,1,0:T(8,128)(2,1)}, u32[]{:S(2)}) copy-start(bf16[4,256,512]{2,1,0:T(8,128)(2,1)} %constant.31.clone.high_ref) | copy-start | bytes 3145732
  22.4 25.8 %copy-start.2 = (bf16[4,256,512]{2,1,0:T(8,128)(2,1)S(1)}, bf16[4,256,512]{2,1,0:T(8,128)(2,1)}, u32[]{:S(2)}) copy-start(bf16[4,256,512]{2,1,0:T(8,128)(2,1)} %constant.32.clone.low_ref) | copy-start | bytes 3145732
  42.2 22.2 %all-to-all-start.2 = ((f32[32,2,1,8,512]{4,3,1,2,0:T(8,128)}), f32[32,2,1,8,512]{4,3,1,2,0:T(8,128)S(1)}, u32[]{:S(2)}, u32[]{:S(2)}) async-start(f32[32,2,1,8,512]{4,3,1,2,0:T(8,128)} %bitcast.18), calls=%async_computation.2 | async-start | bytes 2097152 | tf_op jit(solution)/shard_map/all_to_all | solution.py:323
  52.5 0.6 copy-start.4
  53.1 28.2 %collective-permute-start = (f32[2,2,2,32,1024]{4,3,2,1,0:T(8,128)}, f32[2,2,2,32,1024]{4,3,2,1,0:T(8,128)}, u32[]{:S(2)}, u32[]{:S(2)}) collective-permute-start(f32[2,2,2,32,1024]{4,3,2,1,0:T(8,128)} %get-tuple-element.19.early_ref), channel_id=1, source_target_pairs={{0,56},{8,0},{16,8},{24,16},{32,24},{40,32},{48,40},{56,48},{1,57}... | collective-permute-start | bytes 3145736 | tf_op jit(solution)/shard_map/ppermute | solution.py:310
  58.7 25.7 %collective-permute-start.1 = (f32[2,2,2,32,1024]{4,3,2,1,0:T(8,128)}, f32[2,2,2,32,1024]{4,3,2,1,0:T(8,128)}, u32[]{:S(2)}, u32[]{:S(2)}) collective-permute-start(f32[2,2,2,32,1024]{4,3,2,1,0:T(8,128)} %get-tuple-element.20.late_ref), channel_id=1, source_target_pairs={{0,8},{8,16},{16,24},{24,32},{32,40},{40,48},{48,56},{56,0},{1,9},... | collective-permute-start | bytes 3145736 | tf_op jit(solution)/shard_map/ppermute | solution.py:310
  58.7 12.9 %copy-start.6 = (s32[256,4,8,4]{0,2,1,3:T(8,128)S(1)}, s32[256,4,8,4]{0,2,1,3:T(8,128)}, u32[]{:S(2)}) copy-start(s32[256,4,8,4]{0,2,1,3:T(8,128)} %copy.15) | copy-start | bytes 393220
  58.7 13.0 %copy-start.1 = (bf16[4,256,512]{2,1,0:T(8,128)(2,1)S(1)}, bf16[4,256,512]{2,1,0:T(8,128)(2,1)}, u32[]{:S(2)}) copy-start(bf16[4,256,512]{2,1,0:T(8,128)(2,1)} %constant.31.clone.high_ref) | copy-start | bytes 3145732
  58.7 13.0 %copy-start.3 = (bf16[4,256,512]{2,1,0:T(8,128)(2,1)S(1)}, bf16[4,256,512]{2,1,0:T(8,128)(2,1)}, u32[]{:S(2)}) copy-start(bf16[4,256,512]{2,1,0:T(8,128)(2,1)} %constant.32.clone.low_ref) | copy-start | bytes 3145732
  64.5 25.1 %all-to-all-start.1 = ((f32[32,2,1,8,512]{4,3,1,2,0:T(8,128)}), f32[32,2,1,8,512]{4,3,1,2,0:T(8,128)}, u32[]{:S(2)}, u32[]{:S(2)}) async-start(f32[32,2,1,8,512]{4,3,1,2,0:T(8,128)} %bitcast.17), calls=%async_computation.1 | async-start | bytes 2097152 | tf_op jit(solution)/shard_map/all_to_all | solution.py:323
  73.7 26.9 %collective-permute-start.4 = (f32[2,2,1,32,1024]{4,3,2,1,0:T(8,128)}, f32[2,2,1,32,1024]{4,3,2,1,0:T(8,128)S(1)}, u32[]{:S(2)}, u32[]{:S(2)}) collective-permute-start(f32[2,2,1,32,1024]{4,3,2,1,0:T(8,128)} %get-tuple-element.25.early_ref), channel_id=1, source_target_pairs={{0,56},{8,0},{16,8},{24,16},{32,24},{40,32},{48,40},{56,48},{1,57}... | collective-permute-start | bytes 1572872 | tf_op jit(solution)/shard_map/ppermute | solution.py:310
  77.5 23.2 %collective-permute-start.5 = (f32[2,2,1,32,1024]{4,3,2,1,0:T(8,128)}, f32[2,2,1,32,1024]{4,3,2,1,0:T(8,128)S(1)}, u32[]{:S(2)}, u32[]{:S(2)}) collective-permute-start(f32[2,2,1,32,1024]{4,3,2,1,0:T(8,128)} %get-tuple-element.26.late_ref), channel_id=1, source_target_pairs={{0,8},{8,16},{16,24},{24,32},{32,40},{40,48},{48,56},{56,0},{1,9},... | collective-permute-start | bytes 1572872 | tf_op jit(solution)/shard_map/ppermute | solution.py:310
  92.8 14.2 %collective-permute-start.2 = (f32[2,2,1,32,1024]{4,3,2,1,0:T(8,128)}, f32[2,2,1,32,1024]{4,3,2,1,0:T(8,128)S(1)}, u32[]{:S(2)}, u32[]{:S(2)}) collective-permute-start(f32[2,2,1,32,1024]{4,3,2,1,0:T(8,128)} %get-tuple-element.23.early_ref), channel_id=1, source_target_pairs={{0,56},{8,0},{16,8},{24,16},{32,24},{40,32},{48,40},{56,48},{1,57}... | collective-permute-start | bytes 1572872 | tf_op jit(solution)/shard_map/ppermute | solution.py:310
  95.1 14.1 %collective-permute-start.3 = (f32[2,2,1,32,1024]{4,3,2,1,0:T(8,128)}, f32[2,2,1,32,1024]{4,3,2,1,0:T(8,128)S(1)}, u32[]{:S(2)}, u32[]{:S(2)}) collective-permute-start(f32[2,2,1,32,1024]{4,3,2,1,0:T(8,128)} %get-tuple-element.24.late_ref), channel_id=1, source_target_pairs={{0,8},{8,16},{16,24},{24,32},{32,40},{40,48},{48,56},{56,0},{1,9},... | collective-permute-start | bytes 1572872 | tf_op jit(solution)/shard_map/ppermute | solution.py:310
  95.1 17.6 %all-to-all-start.3 = ((f32[32,2,8,128]{3,2,1,0:T(8,128)}), f32[32,2,8,128]{3,2,1,0:T(8,128)}, u32[]{:S(2)}, u32[]{:S(2)}) async-start(f32[32,2,8,128]{3,2,1,0:T(8,128)} %get-tuple-element.31), calls=%async_computation.3 | async-start | bytes 524288 | tf_op jit(solution)/shard_map/all_to_all | solution.py:339
  129.4 9.9 %copy-start.5 = (f32[32,3,8,128]{3,2,1,0:T(8,128)}, f32[32,3,8,128]{3,2,1,0:T(8,128)S(1)}, u32[]{:S(2)}) copy-start(f32[32,3,8,128]{3,2,1,0:T(8,128)S(1)} %all_to_all.30.refs_1_) | copy-start | bytes 1179652
  130.1 13.9 %all-to-all-start.5 = ((f32[8,8,128]{2,1,0:T(8,128)}), f32[8,8,128]{2,1,0:T(8,128)S(1)}, u32[]{:S(2)}, u32[]{:S(2)}) async-start(f32[8,8,128]{2,1,0:T(8,128)} %broadcast_in_dim.16), calls=%async_computation.5 | async-start | bytes 65536 | tf_op jit(solution)/shard_map/all_to_all | solution.py:346

commit v5 on v2

--- a/solution.py
+++ b/solution.py
@@ -18,11 +18,11 @@
 RADIX = 4
 SUB = N // RADIX
 OWN = 4
-REST_VMEM, SECOND_VMEM, LAG_VMEM = 56, 24, 24
+REST_VMEM, SECOND_VMEM, LAG_VMEM = 56, 16, 16
 CHUNKS = ((0, 1), (2,), (3,))
 ROW = ("row_0", "row_1")
 TM = ("tm_0", "tm_1")
-YROW = ("tm_0", "row_0", "row_1")
+ROWY = ("row_0", "row_1", "tm_0")
 
 f32 = jnp.float32
 bf16 = jnp.bfloat16
@@ -73,9 +73,7 @@
         th, tl = high_ref[j], low_ref[j]
         got = nt(th, zh) + nt(tl, zh) + nt(th, zl)
         for c in range(2):
-            piece = got[:, c * 128:(c + 1) * 128].reshape(8, 4, 8, 128)
-            for y in range(4):
-                out_ref[y, :, c, j] = piece[:, y]
+            out_ref[:, :, c, j] = got[:, c * 128:(c + 1) * 128].reshape(8, 4, 8, 128)
 
 
 def first_transform(movie, high, low, residues, after):
@@ -87,8 +85,8 @@
         functools.partial(first_kernel, residues),
         grid=(OWN,),
         in_specs=[pl.BlockSpec((2, 1, 128, N), lambda f: (0, f, 0, 0)), table, table] + order,
-        out_specs=pl.BlockSpec((4, 8, 2, count, 8, 128), lambda f: (0, 0, 0, 0, 0, f)),
-        out_shape=jax.ShapeDtypeStruct((4, 8, 2, count, 8, OWN * 128), f32),
+        out_specs=pl.BlockSpec((8, 4, 2, count, 8, 128), lambda f: (0, 0, 0, 0, 0, f)),
+        out_shape=jax.ShapeDtypeStruct((8, 4, 2, count, 8, OWN * 128), f32),
         compiler_params=pltpu.CompilerParams(vmem_limit_bytes=(56 if residues[0] == 0 else REST_VMEM) << 20),
         cost_estimate=pl.CostEstimate(
             flops=1024, bytes_accessed=1024, transcendentals=0
@@ -107,7 +105,7 @@
                 [
                     jnp.concatenate(
                         [
-                            piece_ref[y, 2 * q + h, c, j, :, f * 128:(f + 1) * 128]
+                            piece_ref[2 * q + h, y, c, j, :, f * 128:(f + 1) * 128]
                             for f in range(OWN)
                             for y in range(4)
                         ],
@@ -162,56 +160,70 @@
     ones = jnp.ones((16, SUB), bf16)
     cycle_sums = jnp.zeros((32, CYCLES), f32)
     cycle_counts = jnp.zeros((16, CYCLES), f32)
+    def lag_block(step, _):
+        j, b = step // 8, step % 8
+        p, h = b // 2, b % 2
+        lanes = pl.ds(pl.multiple_of(b * 128, 128), 128)
+        sums = [0.0] * LAGS
+        for y in range(4):
+            own_rows = slice(y * 8, (y + 1) * 8)
+            right_rows = pl.ds(pl.multiple_of(8 * jnp.minimum(y + at_end, 3), 8), 8)
+            left_rows = pl.ds(pl.multiple_of(8 * jnp.maximum(y - at_start, 0), 8), 8)
+            frames = {}
+            for f in range(2):
+                frames[f] = [early_ref[f, c, j, own_rows, lanes] for c in range(2)]
+                frames[2 + f] = [late_ref[f, c, j, own_rows, lanes] for c in range(2)]
+                frames[4 + f] = [right_ref[f, c, j, right_rows, lanes] for c in range(2)]
+                frames[f - 2] = [left_ref[f, c, j, left_rows, lanes] for c in range(2)]
+
+            def total(pairs):
+                terms = []
+                for s, t in pairs:
+                    dr = frames[t][0] - frames[s][0]
+                    di = frames[t][1] - frames[s][1]
+                    terms.append(dr * dr + di * di)
+                return functools.reduce(lambda x, z: x + z, terms)
+
+            for lag in range(1, LAGS + 1):
+                own = [(s, s + lag) for s in range(OWN) if s + lag < OWN]
+                right = [(s, s + lag) for s in range(OWN) if 4 <= s + lag < 6]
+                left = [(s, s + lag) for s in (-2, -1) if s + lag in (2, 3)]
+                terms = [sums[lag - 1]]
+                if own:
+                    terms.append(total(own))
+                terms.append(total(right) * has_right if y == 3 else total(right))
+                if left:
+                    terms.append(total(left) * has_left if y == 0 else total(left))
+                sums[lag - 1] = functools.reduce(lambda x, z: x + z, terms)
+        place = pl.multiple_of(j * 128 + p * 32, 32)
+        stacked_lags = jnp.concatenate(
+            [sums[lag - 1] * (1.0 / float(FRAMES - lag)) for lag in range(1, LAGS + 1)], axis=0
+        )
+        lags_ref[h, pl.ds(place, 32), :] = stacked_lags
+        return 0
+
+    lax.fori_loop(0, 8 * count, lag_block, 0)
     for j in range(count):
-        for b in range(8):
-            lanes = slice(b * 128, (b + 1) * 128)
-            sums = [0.0] * LAGS
-            for y in range(4):
-                own_rows = slice(y * 8, (y + 1) * 8)
-                right_rows = pl.ds(pl.multiple_of(8 * jnp.minimum(y + at_end, 3), 8), 8)
-                left_rows = pl.ds(pl.multiple_of(8 * jnp.maximum(y - at_start, 0), 8), 8)
-                frames = {}
-                for f in range(2):
-                    frames[f] = [early_ref[f, c, j, own_rows, lanes] for c in range(2)]
-                    frames[2 + f] = [late_ref[f, c, j, own_rows, lanes] for c in range(2)]
-                    frames[4 + f] = [right_ref[f, c, j, right_rows, lanes] for c in range(2)]
-                    frames[f - 2] = [left_ref[f, c, j, left_rows, lanes] for c in range(2)]
-
-                def total(pairs):
-                    terms = []
-                    for s, t in pairs:
-                        dr = frames[t][0] - frames[s][0]
-                        di = frames[t][1] - frames[s][1]
-                        terms.append(dr * dr + di * di)
-                    return functools.reduce(lambda x, z: x + z, terms)
-
-                for lag in range(1, LAGS + 1):
-                    own = [(s, s + lag) for s in range(OWN) if s + lag < OWN]
-                    right = [(s, s + lag) for s in range(OWN) if 4 <= s + lag < 6]
-                    left = [(s, s + lag) for s in (-2, -1) if s + lag in (2, 3)]
-                    terms = [sums[lag - 1]]
-                    if own:
-                        terms.append(total(own))
-                    terms.append(total(right) * has_right if y == 3 else total(right))
-                    if left:
-                        terms.append(total(left) * has_left if y == 0 else total(left))
-                    sums[lag - 1] = functools.reduce(lambda x, z: x + z, terms)
-            p, h = b // 2, b % 2
-            for lag in range(1, LAGS + 1):
-                lags_ref[p * 32 + (lag - 1) * 8:p * 32 + lag * 8, h * 128:(h + 1) * 128] = sums[
-                    lag - 1
-                ] * (1.0 / float(FRAMES - lag))
         for h in range(2):
-            block = lags_ref[:, h * 128:(h + 1) * 128].T
+            block = lags_ref[h, j * 128:(j + 1) * 128, :].T
             out_ref[16 * h:16 * h + 16, j] = block.reshape(16, 8, 128)
-        for p in range(RADIX):
-            dh, dl = split(lags_ref[p * 32:(p + 1) * 32, :])
-            rows = jnp.concatenate([dh, dl, ones], axis=0)
-            for k in range(8):
-                chosen = jnp.where(cycle_row == label_ref[j, p, k:k + 1, :], 1.0, 0.0).astype(bf16)
-                got = nt(rows, chosen)
-                cycle_sums += jnp.where(sub_row == k, got[:32] + got[32:64], 0.0)
-                cycle_counts += got[64:]
+
+    def cycle_block(step, carried_sums):
+        cycle_sums, cycle_counts = carried_sums
+        place = pl.ds(pl.multiple_of(step * 32, 32), 32)
+        dh, dl = split(jnp.concatenate([lags_ref[h, place, :] for h in range(2)], axis=1))
+        rows = jnp.concatenate([dh, dl, ones], axis=0)
+        for k in range(8):
+            label_row = label_ref[step // RADIX, step % RADIX, k:k + 1, :]
+            chosen = jnp.where(cycle_row == label_row, 1.0, 0.0).astype(bf16)
+            got = nt(rows, chosen)
+            cycle_sums += jnp.where(sub_row == k, got[:32] + got[32:64], 0.0)
+            cycle_counts += got[64:]
+        return cycle_sums, cycle_counts
+
+    cycle_sums, cycle_counts = lax.fori_loop(
+        0, RADIX * count, cycle_block, (cycle_sums, cycle_counts)
+    )
     tile = jnp.concatenate(
         [
             jnp.sum(cycle_sums.reshape(LAGS, 8, CYCLES), axis=1),
@@ -240,7 +252,7 @@
             jax.ShapeDtypeStruct((32, count + carried + int(final), 8, 128), f32),
             jax.ShapeDtypeStruct((8, CYCLES), f32),
         ),
-        scratch_shapes=[pltpu.VMEM((128, SUB), f32)],
+        scratch_shapes=[pltpu.VMEM((2, 128 * count, 128), f32)],
         compiler_params=pltpu.CompilerParams(vmem_limit_bytes=LAG_VMEM << 20),
         cost_estimate=pl.CostEstimate(
             flops=1024, bytes_accessed=1024, transcendentals=0
@@ -312,8 +324,8 @@
         return first_transform(movie, high, low, CHUNKS[index], after)
 
     def exchange(piece):
-        piece = lax.all_to_all(piece.reshape((32,) + piece.shape[2:]), YROW, 0, 0, tiled=True)
-        return piece.reshape((4, 8) + piece.shape[1:])
+        piece = lax.all_to_all(piece.reshape((32,) + piece.shape[2:]), ROWY, 0, 0, tiled=True)
+        return piece.reshape((8, 4) + piece.shape[1:])
 
     def transform_columns(piece, index, after):
         spectra.append(second_transform(piece, high, low, len(CHUNKS[index]), after))

time: 148 us -> 147 us (level)
  waiting for transfers between devices: 33.3 us -> 28.6 us
  starting transfers between devices: 47.2 us -> 50.1 us
  Pallas kernels: 39 us -> 41.7 us
  blocking collectives: 18.2 us -> 15.5 us
    ppermute x3, waiting for transfers between devices: 9.48 us -> 5.6 us  [halo(): lax.ppermute(early, 'tm_1', to_left)]
    all_to_all x1, starting transfers between devices: 8.2 us -> 11.7 us  [body(): cycles = jnp.sum(lax.all_to_all(copies, ROW, 0, 0, tiled=True), axis=0)]
    ppermute x3, starting transfers between devices: 12.2 us -> 9.36 us  [halo(): lax.ppermute(early, 'tm_1', to_left)]
    pallas_call x3, Pallas kernels: 10.7 us -> 13.5 us  [partial_lags(): pl.pallas_call(functools.partial(lag_kernel, count, carried, final), in_s...]
    all_to_all x1, blocking collectives: 18.2 us -> 15.5 us  [body(): sums_1 = lax.all_to_all(part_2, TM, 0, 0, tiled=True)]
    all_to_all x3, waiting for transfers between devices: 16.8 us -> 14.9 us  [exchange(): lax.all_to_all(piece.reshape((32,) + piece.shape[2:]), ROWY, 0, 0, tiled=...]
  transfers between devices with their start and end apart: 11 -> 11, of which waited for: 7 -> 8; matrix products, arithmetic and copies ran while one was open for 5% -> 5% of each run, Pallas kernels for 22% -> 25%
where the time goes in v5:
time: 147 us; the launch traced here: 146 us
  starting transfers between devices  50.1 us (34%)
  Pallas kernels  41.7 us (28%)
  waiting for transfers between devices  28.6 us (19%)
  blocking collectives  15.5 us (11%)
  local copies, waits for them, and re-layouts  8.09 us (6%)
    all_to_all x3, starting transfers between devices, exchange(): lax.all_to_all(piece.reshape((32,) + piece.shape[2:]), ROWY, 0, 0, tiled=...  22.2 us
    pallas_call x3, Pallas kernels, first_transform(): pl.pallas_call(functools.partial(first_kernel, residues), grid=(OWN,), in...  16.1 us
    all_to_all x1, blocking collectives, body(): sums_1 = lax.all_to_all(part_2, TM, 0, 0, tiled=True)  15.5 us
    all_to_all x3, waiting for transfers between devices, exchange(): lax.all_to_all(piece.reshape((32,) + piece.shape[2:]), ROWY, 0, 0, tiled=...  14.9 us
    pallas_call x3, Pallas kernels, partial_lags(): pl.pallas_call(functools.partial(lag_kernel, count, carried, final), in_s...  13.5 us
    all_to_all x1, starting transfers between devices, body(): cycles = jnp.sum(lax.all_to_all(copies, ROW, 0, 0, tiled=True), axis=0)  11.7 us
    pallas_call x3, Pallas kernels, second_transform(): pl.pallas_call(functools.partial(second_kernel, count), in_specs=[vmem] *...  10.1 us
    ppermute x3, starting transfers between devices, halo(): lax.ppermute(early, 'tm_1', to_left)  9.36 us
  transfers between devices with their start and end apart: 11, of which 8 were waited for; matrix products, arithmetic and copies ran while one was open for 5% of the time, Pallas kernels for 25%

profile of v5, /device:TPU:1, one launch (start us, length us, event | category | flops | bytes accessed | tf_op | source)
XLA Modules:
  0.0 145.9 jit_solution(9574776273695866520)
XLA Ops:
  0.6 5.8 %first_transform.3 = f32[8,4,2,2,8,512]{5,4,3,2,1,0:T(8,128)} custom-call(f32[2,4,128,1024]{3,2,1,0:T(8,128)} %movie_ref.5, bf16[4,256,512]{2,1,0:T(8,128)(2,1)} %constant.31.clone.high_ref, bf16[4,256,512]{2,1,0:T(8,128)(2,1)} %constant.32.clone.low_ref), custom_call_target="tpu_custom_call" | custom-call | flops 1024 | bytes 1024 | tf_op jit(solution)/shard_map/first_transform/pallas_call | solution.py:84
  6.4 0.0 copy-start.7
  6.4 0.0 copy-start.8
  6.4 8.8 %all-to-all-start = ((f32[32,2,2,8,512]{4,3,2,1,0:T(8,128)}), f32[32,2,2,8,512]{4,3,2,1,0:T(8,128)}, u32[]{:S(2)}, u32[]{:S(2)}) async-start(f32[32,2,2,8,512]{4,3,2,1,0:T(8,128)} %bitcast.16), calls=%async_computation | async-start | bytes 4194304 | tf_op jit(solution)/shard_map/all_to_all | solution.py:327
  15.2 0.0 copy-done.7
  15.2 0.0 copy-done.8
  15.3 0.3 dynamic-slice_select_fusion
  15.6 2.6 %reshape.33 = s32[256,4,8,4]{3,2,1,0:T(8,128)} reshape(s32[1024,32]{1,0:T(8,128)S(1)} %dynamic-slice_select_fusion) | data formatting | bytes 262144 | tf_op jit(solution)/shard_map/reshape | solution.py:306
  18.1 4.2 %copy.15 = s32[256,4,8,4]{0,2,1,3:T(8,128)} copy(s32[256,4,8,4]{3,2,1,0:T(8,128)} %reshape.33) | data formatting | bytes 262144 | tf_op jit(solution)/shard_map/reshape | solution.py:306
  22.4 0.0 copy-start
  22.4 0.0 copy-start.2
  22.4 5.1 %first_transform.5 = f32[8,4,2,1,8,512]{5,4,3,2,1,0:T(8,128)} custom-call(f32[2,4,128,1024]{3,2,1,0:T(8,128)} %movie_ref.5, bf16[4,256,512]{2,1,0:T(8,128)(2,1)} %constant.31.clone.high_ref, bf16[4,256,512]{2,1,0:T(8,128)(2,1)} %constant.32.clone.low_ref, s32[4,4,8,256]{3,2,1,0:T(8,128)} %bitcast.19), custom_call_target="tpu_custom_call" | custom-call | flops 1024 | bytes 1024 | tf_op jit(solution)/shard_map/first_transform/pallas_call | solution.py:84
  27.5 14.7 %all-to-all-done = f32[32,2,2,8,512]{4,3,2,1,0:T(8,128)} async-done(((f32[32,2,2,8,512]{4,3,2,1,0:T(8,128)}), f32[32,2,2,8,512]{4,3,2,1,0:T(8,128)}, u32[]{:S(2)}, u32[]{:S(2)}) %all-to-all-start) | async-done | bytes 2097184 | tf_op jit(solution)/shard_map/all_to_all | solution.py:327
  42.2 5.9 %all-to-all-start.2 = ((f32[32,2,1,8,512]{4,3,1,2,0:T(8,128)}), f32[32,2,1,8,512]{4,3,1,2,0:T(8,128)S(1)}, u32[]{:S(2)}, u32[]{:S(2)}) async-start(f32[32,2,1,8,512]{4,3,1,2,0:T(8,128)} %bitcast.18), calls=%async_computation.2 | async-start | bytes 2097152 | tf_op jit(solution)/shard_map/all_to_all | solution.py:327
  48.1 0.0 copy-done
  48.2 0.0 copy-done.2
  48.2 4.8 %second_transform.3 = (f32[2,2,2,32,1024]{4,3,2,1,0:T(8,128)}, f32[2,2,2,32,1024]{4,3,2,1,0:T(8,128)}, f32[8,128]{1,0:T(8,128)S(1)}) custom-call(f32[8,4,2,2,8,512]{5,4,3,2,1,0:T(8,128)} %bitcast.3.piece_ref, bf16[4,256,512]{2,1,0:T(8,128)(2,1)S(1)} %copy-done, bf16[4,256,512]{2,1,0:T(8,128)(2,1)S(1)} %copy-done.2), custom_call_target="tpu_custom_call" | custom-call | flops 1024 | bytes 1024 | tf_op jit(solution)/shard_map/second_transform/pallas_call | solution.py:136
  53.0 0.0 copy-start.4
  53.0 0.6 copy-done.4
  53.6 5.6 %collective-permute-start = (f32[2,2,2,32,1024]{4,3,2,1,0:T(8,128)}, f32[2,2,2,32,1024]{4,3,2,1,0:T(8,128)}, u32[]{:S(2)}, u32[]{:S(2)}) collective-permute-start(f32[2,2,2,32,1024]{4,3,2,1,0:T(8,128)} %get-tuple-element.19.early_ref), channel_id=1, source_target_pairs={{0,56},{8,0},{16,8},{24,16},{32,24},{40,32},{48,40},{56,48},{1,57}... | collective-permute-start | bytes 3145736 | tf_op jit(solution)/shard_map/ppermute | solution.py:314
  59.1 0.0 collective-permute-start.1
  59.1 0.0 copy-start.6
  59.2 0.0 copy-start.1
  59.2 0.0 copy-start.3
  59.2 5.1 %first_transform.4 = f32[8,4,2,1,8,512]{5,4,3,2,1,0:T(8,128)} custom-call(f32[2,4,128,1024]{3,2,1,0:T(8,128)} %movie_ref.5, bf16[4,256,512]{2,1,0:T(8,128)(2,1)} %constant.31.clone.high_ref, bf16[4,256,512]{2,1,0:T(8,128)(2,1)} %constant.32.clone.low_ref, f32[8,128]{1,0:T(8,128)} %copy-done.4), custom_call_target="tpu_custom_call" | custom-call | flops 1024 | bytes 1024 | tf_op jit(solution)/shard_map/first_transform/pallas_call | solution.py:84
  64.3 0.2 all-to-all-done.2
  64.5 7.5 %all-to-all-start.1 = ((f32[32,2,1,8,512]{4,3,1,2,0:T(8,128)}), f32[32,2,1,8,512]{4,3,1,2,0:T(8,128)}, u32[]{:S(2)}, u32[]{:S(2)}) async-start(f32[32,2,1,8,512]{4,3,1,2,0:T(8,128)} %bitcast.17), calls=%async_computation.1 | async-start | bytes 2097152 | tf_op jit(solution)/shard_map/all_to_all | solution.py:327
  72.0 0.0 copy-done.6
  72.0 0.1 add_convert_fusion.ends_ref
  72.1 0.0 copy-done.1
  72.1 0.0 copy-done.3
  72.1 2.0 %second_transform.4 = (f32[2,2,1,32,1024]{4,3,2,1,0:T(8,128)}, f32[2,2,1,32,1024]{4,3,2,1,0:T(8,128)}, f32[8,128]{1,0:T(8,128)S(1)}) custom-call(f32[8,4,2,1,8,512]{5,4,3,2,1,0:T(8,128)S(1)} %bitcast.15, bf16[4,256,512]{2,1,0:T(8,128)(2,1)S(1)} %copy-done.1, bf16[4,256,512]{2,1,0:T(8,128)(2,1)S(1)} %copy-done.3), custom_call_target="tpu_custom_call" | custom-call | flops 1024 | bytes 1024 | tf_op jit(solution)/shard_map/second_transform/pallas_call | solution.py:136
  74.2 3.3 %collective-permute-start.4 = (f32[2,2,1,32,1024]{4,3,2,1,0:T(8,128)}, f32[2,2,1,32,1024]{4,3,2,1,0:T(8,128)S(1)}, u32[]{:S(2)}, u32[]{:S(2)}) collective-permute-start(f32[2,2,1,32,1024]{4,3,2,1,0:T(8,128)} %get-tuple-element.25.early_ref), channel_id=1, source_target_pairs={{0,56},{8,0},{16,8},{24,16},{32,24},{40,32},{48,40},{56,48},{1,57}... | collective-permute-start | bytes 1572872 | tf_op jit(solution)/shard_map/ppermute | solution.py:314
  77.5 0.0 collective-permute-start.5
  77.5 4.3 %collective-permute-done.right_ref = f32[2,2,2,32,1024]{4,3,2,1,0:T(8,128)} collective-permute-done((f32[2,2,2,32,1024]{4,3,2,1,0:T(8,128)}, f32[2,2,2,32,1024]{4,3,2,1,0:T(8,128)}, u32[]{:S(2)}, u32[]{:S(2)}) %collective-permute-start) | collective-permute-done | bytes 1048608 | tf_op jit(solution)/shard_map/ppermute | solution.py:314
  81.8 3.1 %collective-permute-done.1.left_ref = f32[2,2,2,32,1024]{4,3,2,1,0:T(8,128)} collective-permute-done((f32[2,2,2,32,1024]{4,3,2,1,0:T(8,128)}, f32[2,2,2,32,1024]{4,3,2,1,0:T(8,128)}, u32[]{:S(2)}, u32[]{:S(2)}) %collective-permute-start.1) | collective-permute-done | bytes 1048608 | tf_op jit(solution)/shard_map/ppermute | solution.py:314
  84.9 6.5 %partial_lags.3 = (f32[32,2,8,128]{3,2,1,0:T(8,128)}, f32[8,128]{1,0:T(8,128)S(1)}) custom-call(s32[2]{0:T(128)S(1)} %add_convert_fusion.ends_ref, f32[2,2,2,32,1024]{4,3,2,1,0:T(8,128)} %get-tuple-element.19.early_ref, f32[2,2,2,32,1024]{4,3,2,1,0:T(8,128)} %get-tuple-element.20.late_ref, f32[2,2,2,32,1024]{4,3,2,1,0:T(8,128)} %collective-permute-done.right_ref, ...), custom_call_target="tpu_custom_call" | custom-call | flops 1024 | bytes 1024 | tf_op jit(solution)/shard_map/partial_lags/pallas_call | solution.py:245
  91.3 0.0 all-to-all-done.1
  91.4 3.3 %second_transform.5 = (f32[2,2,1,32,1024]{4,3,2,1,0:T(8,128)}, f32[2,2,1,32,1024]{4,3,2,1,0:T(8,128)}, f32[8,128]{1,0:T(8,128)S(1)}) custom-call(f32[8,4,2,1,8,512]{5,4,3,2,1,0:T(8,128)} %bitcast.6.piece_ref, bf16[4,256,512]{2,1,0:T(8,128)(2,1)S(1)} %copy-done.1, bf16[4,256,512]{2,1,0:T(8,128)(2,1)S(1)} %copy-done.3, ...), custom_call_target="tpu_custom_call" | custom-call | flops 1024 | bytes 1024 | tf_op jit(solution)/shard_map/second_transform/pallas_call | solution.py:136
  94.6 0.4 collective-permute-start.2
  95.1 1.0 collective-permute-start.3
  96.1 5.8 %all-to-all-start.3 = ((f32[32,2,8,128]{3,2,1,0:T(8,128)}), f32[32,2,8,128]{3,2,1,0:T(8,128)}, u32[]{:S(2)}, u32[]{:S(2)}) async-start(f32[32,2,8,128]{3,2,1,0:T(8,128)} %get-tuple-element.31), calls=%async_computation.3 | async-start | bytes 524288 | tf_op jit(solution)/shard_map/all_to_all | solution.py:343
  101.9 0.0 collective-permute-done.4.right_ref
  101.9 0.0 collective-permute-done.5.left_ref
  101.9 3.2 %partial_lags.4 = (f32[32,1,8,128]{3,2,1,0:T(8,128)S(1)}, f32[8,128]{1,0:T(8,128)S(1)}) custom-call(s32[2]{0:T(128)S(1)} %add_convert_fusion.ends_ref, f32[2,2,1,32,1024]{4,3,2,1,0:T(8,128)} %get-tuple-element.25.early_ref, f32[2,2,1,32,1024]{4,3,2,1,0:T(8,128)} %get-tuple-element.26.late_ref, f32[2,2,1,32,1024]{4,3,2,1,0:T(8,128)S(1)} %collective-permute-done.4.right_ref, ...), custom_call_target="tpu_custom_call" | custom-call | flops 1024 | bytes 1024 | tf_op jit(solution)/shard_map/partial_lags/pallas_call | solution.py:245
  105.1 1.3 collective-permute-done.2.right_ref
  106.5 2.0 %collective-permute-done.3.left_ref = f32[2,2,1,32,1024]{4,3,2,1,0:T(8,128)S(1)} collective-permute-done((f32[2,2,1,32,1024]{4,3,2,1,0:T(8,128)}, f32[2,2,1,32,1024]{4,3,2,1,0:T(8,128)S(1)}, u32[]{:S(2)}, u32[]{:S(2)}) %collective-permute-start.3) | collective-permute-done | bytes 524320 | tf_op jit(solution)/shard_map/ppermute | solution.py:314
  108.5 3.8 %partial_lags.5 = (f32[32,3,8,128]{3,2,1,0:T(8,128)S(1)}, f32[8,128]{1,0:T(8,128)}) custom-call(s32[2]{0:T(128)S(1)} %add_convert_fusion.ends_ref, f32[2,2,1,32,1024]{4,3,2,1,0:T(8,128)} %get-tuple-element.23.early_ref, f32[2,2,1,32,1024]{4,3,2,1,0:T(8,128)} %get-tuple-element.24.late_ref, f32[2,2,1,32,1024]{4,3,2,1,0:T(8,128)S(1)} %collective-permute-done.2.right_ref, ...), custom_call_target="tpu_custom_call" | custom-call | flops 1024 | bytes 1024 | tf_op jit(solution)/shard_map/partial_lags/pallas_call | solution.py:245
  112.3 0.4 all-to-all-done.3.refs_0_
  112.6 15.5 %all_to_all.30.refs_1_ = f32[32,3,8,128]{3,2,1,0:T(8,128)S(1)} all-to-all(f32[32,3,8,128]{3,2,1,0:T(8,128)S(1)} %get-tuple-element.32), channel_id=1, replica_groups=mesh['tm_0'=4,'tm_1'=8,'row_0'=4,'row_1'=2] {'tm_0','tm_1'}, dimensions={0} | all-to-all | bytes 786432 | tf_op jit(solution)/shard_map/all_to_all | solution.py:347
  128.1 0.0 copy-start.5
  128.2 0.7 broadcast_in_dim.16
  128.9 11.7 %all-to-all-start.5 = ((f32[8,8,128]{2,1,0:T(8,128)}), f32[8,8,128]{2,1,0:T(8,128)S(1)}, u32[]{:S(2)}, u32[]{:S(2)}) async-start(f32[8,8,128]{2,1,0:T(8,128)} %broadcast_in_dim.16), calls=%async_computation.5 | async-start | bytes 65536 | tf_op jit(solution)/shard_map/all_to_all | solution.py:350
  140.5 0.0 copy-done.5
  140.5 2.1 %settle.1 = f32[4,32,128]{2,1,0:T(8,128)} custom-call(f32[32,2,8,128]{3,2,1,0:T(8,128)} %all-to-all-done.3.refs_0_, f32[32,3,8,128]{3,2,1,0:T(8,128)} %copy-done.5), custom_call_target="tpu_custom_call" | custom-call | tf_op jit(solution)/shard_map/settle/pallas_call | solution.py:291
  142.6 2.6 %all-to-all-done.5 = f32[8,8,128]{2,1,0:T(8,128)S(1)} async-done(((f32[8,8,128]{2,1,0:T(8,128)}), f32[8,8,128]{2,1,0:T(8,128)S(1)}, u32[]{:S(2)}, u32[]{:S(2)}) %all-to-all-start.5) | async-done | bytes 32800 | tf_op jit(solution)/shard_map/all_to_all | solution.py:350
  145.3 0.6 slice_divide_fusion
  (6 shorter events, 0.1 us)
Async XLA Ops:
  6.4 8.8 %copy-start.7 = (s32[1024,128]{1,0:T(8,128)S(1)}, s32[1024,128]{1,0:T(8,128)}, u32[]{:S(2)}) copy-start(s32[1024,128]{1,0:T(8,128)} %param.6) | copy-start | bytes 1572868
  6.4 8.8 %copy-start.8 = (s32[1024,128]{1,0:T(8,128)S(1)}, s32[1024,128]{1,0:T(8,128)}, u32[]{:S(2)}) copy-start(s32[1024,128]{1,0:T(8,128)} %param.7) | copy-start | bytes 1572868
  6.4 35.8 %all-to-all-start = ((f32[32,2,2,8,512]{4,3,2,1,0:T(8,128)}), f32[32,2,2,8,512]{4,3,2,1,0:T(8,128)}, u32[]{:S(2)}, u32[]{:S(2)}) async-start(f32[32,2,2,8,512]{4,3,2,1,0:T(8,128)} %bitcast.16), calls=%async_computation | async-start | bytes 4194304 | tf_op jit(solution)/shard_map/all_to_all | solution.py:327
  22.4 25.8 %copy-start = (bf16[4,256,512]{2,1,0:T(8,128)(2,1)S(1)}, bf16[4,256,512]{2,1,0:T(8,128)(2,1)}, u32[]{:S(2)}) copy-start(bf16[4,256,512]{2,1,0:T(8,128)(2,1)} %constant.31.clone.high_ref) | copy-start | bytes 3145732
  22.4 25.8 %copy-start.2 = (bf16[4,256,512]{2,1,0:T(8,128)(2,1)S(1)}, bf16[4,256,512]{2,1,0:T(8,128)(2,1)}, u32[]{:S(2)}) copy-start(bf16[4,256,512]{2,1,0:T(8,128)(2,1)} %constant.32.clone.low_ref) | copy-start | bytes 3145732
  42.2 22.2 %all-to-all-start.2 = ((f32[32,2,1,8,512]{4,3,1,2,0:T(8,128)}), f32[32,2,1,8,512]{4,3,1,2,0:T(8,128)S(1)}, u32[]{:S(2)}, u32[]{:S(2)}) async-start(f32[32,2,1,8,512]{4,3,1,2,0:T(8,128)} %bitcast.18), calls=%async_computation.2 | async-start | bytes 2097152 | tf_op jit(solution)/shard_map/all_to_all | solution.py:327
  53.0 0.6 copy-start.4
  53.6 28.2 %collective-permute-start = (f32[2,2,2,32,1024]{4,3,2,1,0:T(8,128)}, f32[2,2,2,32,1024]{4,3,2,1,0:T(8,128)}, u32[]{:S(2)}, u32[]{:S(2)}) collective-permute-start(f32[2,2,2,32,1024]{4,3,2,1,0:T(8,128)} %get-tuple-element.19.early_ref), channel_id=1, source_target_pairs={{0,56},{8,0},{16,8},{24,16},{32,24},{40,32},{48,40},{56,48},{1,57}... | collective-permute-start | bytes 3145736 | tf_op jit(solution)/shard_map/ppermute | solution.py:314
  59.1 25.7 %collective-permute-start.1 = (f32[2,2,2,32,1024]{4,3,2,1,0:T(8,128)}, f32[2,2,2,32,1024]{4,3,2,1,0:T(8,128)}, u32[]{:S(2)}, u32[]{:S(2)}) collective-permute-start(f32[2,2,2,32,1024]{4,3,2,1,0:T(8,128)} %get-tuple-element.20.late_ref), channel_id=1, source_target_pairs={{0,8},{8,16},{16,24},{24,32},{32,40},{40,48},{48,56},{56,0},{1,9},... | collective-permute-start | bytes 3145736 | tf_op jit(solution)/shard_map/ppermute | solution.py:314
  59.1 12.9 %copy-start.6 = (s32[256,4,8,4]{0,2,1,3:T(8,128)S(1)}, s32[256,4,8,4]{0,2,1,3:T(8,128)}, u32[]{:S(2)}) copy-start(s32[256,4,8,4]{0,2,1,3:T(8,128)} %copy.15) | copy-start | bytes 393220
  59.2 13.0 %copy-start.1 = (bf16[4,256,512]{2,1,0:T(8,128)(2,1)S(1)}, bf16[4,256,512]{2,1,0:T(8,128)(2,1)}, u32[]{:S(2)}) copy-start(bf16[4,256,512]{2,1,0:T(8,128)(2,1)} %constant.31.clone.high_ref) | copy-start | bytes 3145732
  59.2 13.0 %copy-start.3 = (bf16[4,256,512]{2,1,0:T(8,128)(2,1)S(1)}, bf16[4,256,512]{2,1,0:T(8,128)(2,1)}, u32[]{:S(2)}) copy-start(bf16[4,256,512]{2,1,0:T(8,128)(2,1)} %constant.32.clone.low_ref) | copy-start | bytes 3145732
  64.5 26.9 %all-to-all-start.1 = ((f32[32,2,1,8,512]{4,3,1,2,0:T(8,128)}), f32[32,2,1,8,512]{4,3,1,2,0:T(8,128)}, u32[]{:S(2)}, u32[]{:S(2)}) async-start(f32[32,2,1,8,512]{4,3,1,2,0:T(8,128)} %bitcast.17), calls=%async_computation.1 | async-start | bytes 2097152 | tf_op jit(solution)/shard_map/all_to_all | solution.py:327
  74.2 27.7 %collective-permute-start.4 = (f32[2,2,1,32,1024]{4,3,2,1,0:T(8,128)}, f32[2,2,1,32,1024]{4,3,2,1,0:T(8,128)S(1)}, u32[]{:S(2)}, u32[]{:S(2)}) collective-permute-start(f32[2,2,1,32,1024]{4,3,2,1,0:T(8,128)} %get-tuple-element.25.early_ref), channel_id=1, source_target_pairs={{0,56},{8,0},{16,8},{24,16},{32,24},{40,32},{48,40},{56,48},{1,57}... | collective-permute-start | bytes 1572872 | tf_op jit(solution)/shard_map/ppermute | solution.py:314
  77.5 24.4 %collective-permute-start.5 = (f32[2,2,1,32,1024]{4,3,2,1,0:T(8,128)}, f32[2,2,1,32,1024]{4,3,2,1,0:T(8,128)S(1)}, u32[]{:S(2)}, u32[]{:S(2)}) collective-permute-start(f32[2,2,1,32,1024]{4,3,2,1,0:T(8,128)} %get-tuple-element.26.late_ref), channel_id=1, source_target_pairs={{0,8},{8,16},{16,24},{24,32},{32,40},{40,48},{48,56},{56,0},{1,9},... | collective-permute-start | bytes 1572872 | tf_op jit(solution)/shard_map/ppermute | solution.py:314
  94.6 11.8 %collective-permute-start.2 = (f32[2,2,1,32,1024]{4,3,2,1,0:T(8,128)}, f32[2,2,1,32,1024]{4,3,2,1,0:T(8,128)S(1)}, u32[]{:S(2)}, u32[]{:S(2)}) collective-permute-start(f32[2,2,1,32,1024]{4,3,2,1,0:T(8,128)} %get-tuple-element.23.early_ref), channel_id=1, source_target_pairs={{0,56},{8,0},{16,8},{24,16},{32,24},{40,32},{48,40},{56,48},{1,57}... | collective-permute-start | bytes 1572872 | tf_op jit(solution)/shard_map/ppermute | solution.py:314
  95.1 13.4 %collective-permute-start.3 = (f32[2,2,1,32,1024]{4,3,2,1,0:T(8,128)}, f32[2,2,1,32,1024]{4,3,2,1,0:T(8,128)S(1)}, u32[]{:S(2)}, u32[]{:S(2)}) collective-permute-start(f32[2,2,1,32,1024]{4,3,2,1,0:T(8,128)} %get-tuple-element.24.late_ref), channel_id=1, source_target_pairs={{0,8},{8,16},{16,24},{24,32},{32,40},{40,48},{48,56},{56,0},{1,9},... | collective-permute-start | bytes 1572872 | tf_op jit(solution)/shard_map/ppermute | solution.py:314
  96.1 16.6 %all-to-all-start.3 = ((f32[32,2,8,128]{3,2,1,0:T(8,128)}), f32[32,2,8,128]{3,2,1,0:T(8,128)}, u32[]{:S(2)}, u32[]{:S(2)}) async-start(f32[32,2,8,128]{3,2,1,0:T(8,128)} %get-tuple-element.31), calls=%async_computation.3 | async-start | bytes 524288 | tf_op jit(solution)/shard_map/all_to_all | solution.py:343
  128.1 12.4 %copy-start.5 = (f32[32,3,8,128]{3,2,1,0:T(8,128)}, f32[32,3,8,128]{3,2,1,0:T(8,128)S(1)}, u32[]{:S(2)}) copy-start(f32[32,3,8,128]{3,2,1,0:T(8,128)S(1)} %all_to_all.30.refs_1_) | copy-start | bytes 1179652
  128.9 16.4 %all-to-all-start.5 = ((f32[8,8,128]{2,1,0:T(8,128)}), f32[8,8,128]{2,1,0:T(8,128)S(1)}, u32[]{:S(2)}, u32[]{:S(2)}) async-start(f32[8,8,128]{2,1,0:T(8,128)} %broadcast_in_dim.16), calls=%async_computation.5 | async-start | bytes 65536 | tf_op jit(solution)/shard_map/all_to_all | solution.py:350
